TPU v7x, 128 devices: a whole 4x4x4 slice. The times are simulated.
128 devices in a mesh: pipe: 2 (over x_hi), tensor: 4 (over z), dp: 16 (over x_lo, y, core).
Axes of the slice: x: 4 (x_hi: 2, x_lo: 2; x = x_hi * 2 + x_lo), y: 4, z: 4, core: 2. Of those that a mesh axis runs over, the one named last changes fastest.
Arguments:
- tokens: bfloat16 [8192, 1024], P('dp', 'tensor'), may hold values from -6 to 6
- lengths: int32 [64, 4], P('dp'), may hold values from 1 to 85, 128 in all within a row
- ln_gain: bfloat16 [2, 2, 1024], P('pipe'), may hold values from 0.099609375 to 1.8984375
- ln_bias: bfloat16 [2, 2, 1024], P('pipe'), may hold values from -3 to 3
- joined_weight: bfloat16 [2, 1024, 3, 1024], P('pipe', None, None, 'tensor'), may hold values from -0.1875 to 0.1875
- joined_bias: bfloat16 [2, 3, 1024], P('pipe', None, 'tensor'), may hold values from -3 to 3
- dense_weight: bfloat16 [2, 1024, 1024], P('pipe', 'tensor'), may hold values from -0.5 to 0.5
- up_weight: bfloat16 [2, 1024, 4096], P('pipe', None, 'tensor'), may hold values from -0.1875 to 0.1875
- up_bias: bfloat16 [2, 4096], P('pipe', 'tensor'), may hold values from -3 to 3
- down_weight: bfloat16 [2, 4096, 1024], P('pipe', 'tensor'), may hold values from -0.09375 to 0.09375
- output_bias: bfloat16 [2, 2, 1024], P('pipe'), may hold values from -3 to 3
- cotangent: bfloat16 [8192, 1024], P('dp', 'tensor'), may hold values from -6 to 6
Outputs:
- section_out: bfloat16 [2, 8192, 1024], P('pipe', 'dp', 'tensor')
- input_grad: bfloat16 [2, 8192, 1024], P('pipe', 'dp', 'tensor')
- grad_ln_gain: float32 [2, 2, 1024], P('pipe')
- grad_ln_bias: float32 [2, 2, 1024], P('pipe')
- grad_joined: float32 [2, 1024, 3, 1024], P('pipe', None, None, 'tensor')
- grad_joined_bias: float32 [2, 3, 1024], P('pipe', None, 'tensor')
- grad_dense: float32 [2, 1024, 1024], P('pipe', 'tensor')
- grad_up: float32 [2, 1024, 4096], P('pipe', None, 'tensor')
- grad_up_bias: float32 [2, 4096], P('pipe', 'tensor')
- grad_down: float32 [2, 4096, 1024], P('pipe', 'tensor')
- grad_output_bias: float32 [2, 2, 1024], P('pipe')
Inputs may be any that keep to these rules, and one draw needn't show every extreme that they name: Row b gives, in order, the lengths of the 4 sequences that fill block b (tokens b * 128 to (b + 1) * 128 - 1); every row sums to 128.
All inputs are finite; a program needn't handle non-finite values.
Results may differ from a plain program's by a relative error of at most 0.035.
Values may be sent and summed in bfloat16 or wider, within the bound.
No kernel may reach another device: no remote copies, remote signals or barrier semaphores. Data moves between devices by JAX's collectives and lax.ppermute only.
A program may use at most 192 MiB of HBM per device.

v0:
```python
import jax
import jax.numpy as jnp
from jax import lax
from jax.sharding import PartitionSpec as P

HD = 64
ROT = 16
MB = 128
NMB = 4


EPSILON = 1e-05
MASKED = -1e30


def passed_along(x, axis, by):
    peers = lax.axis_size(axis)
    pairs = [(i, i + by) for i in range(peers) if 0 <= i + by < peers]
    return lax.ppermute(x, axis, pairs)


def tensor_pieces(x):
    peers = lax.axis_size("tensor")
    me = lax.axis_index("tensor")
    parts = [x]
    for shift in range(1, peers):
        pairs = [(i, (i + shift) % peers) for i in range(peers)]
        parts.append(lax.ppermute(x, "tensor", pairs))
    ordered = []
    for owner in range(peers):
        slot = (me - owner) % peers
        chosen = parts[peers - 1]
        for k in range(peers - 2, -1, -1):
            chosen = jnp.where(slot == k, parts[k], chosen)
        ordered.append(chosen)
    return ordered


def tensor_sum(x):
    pieces = tensor_pieces(x)
    total = pieces[0].astype(jnp.float32)
    for piece in pieces[1:]:
        total = total + piece.astype(jnp.float32)
    return total

def as_sent(x):
    return jax.tree.map(lambda a: a.astype(jnp.bfloat16) if a.dtype == jnp.float32 else a, x)


def positions(lengths, block_rows):
    seq_count = lengths.shape[1]
    counter = jnp.arange(seq_count, dtype=jnp.int32)
    lower_tri = (counter[:, None] >= counter[None, :]).astype(jnp.int32)
    seg_ends = jnp.sum(lengths[:, None, :] * lower_tri[None, :, :], axis=2)
    starts = seg_ends - lengths
    row_index = jnp.arange(block_rows, dtype=jnp.int32)
    segment = jnp.sum((row_index[None, :, None] >= seg_ends[:, None, :]).astype(jnp.int32), axis=2)
    member = (segment[:, :, None] == counter[None, None, :]).astype(jnp.int32)
    place = row_index[None, :] - jnp.sum(member * starts[:, None, :], axis=2)
    return (segment, place)


def rotary(place):
    half_rot = ROT // 2
    inv_freq = jnp.power(10000.0, -2.0 * jnp.arange(half_rot, dtype=jnp.float32) / ROT)
    angles = place.astype(jnp.float32)[..., None] * inv_freq
    return (jnp.cos(angles), jnp.sin(angles))


def rotate(heads_in, cosv, sinv):
    half_rot = ROT // 2
    first_half = heads_in[..., :half_rot]
    second_half = heads_in[..., half_rot:ROT]
    cos_rows = cosv[:, None, :]
    sin_rows = sinv[:, None, :]
    return jnp.concatenate(
        [
            first_half * cos_rows - second_half * sin_rows,
            second_half * cos_rows + first_half * sin_rows,
            heads_in[..., ROT:],
        ],
        axis=-1,
    )


def rotate_back(heads_in, cosv, sinv):
    half_rot = ROT // 2
    first_half = heads_in[..., :half_rot]
    second_half = heads_in[..., half_rot:ROT]
    cos_rows = cosv[:, None, :]
    sin_rows = sinv[:, None, :]
    return jnp.concatenate(
        [
            first_half * cos_rows + second_half * sin_rows,
            second_half * cos_rows - first_half * sin_rows,
            heads_in[..., ROT:],
        ],
        axis=-1,
    )


def exact_gelu(values):
    return jax.nn.gelu(values, approximate=False)


def allowed_keys(segment):
    row_index = jnp.arange(segment.shape[0], dtype=jnp.int32)
    return (segment[:, None] == segment[None, :]) & (row_index[None, :] <= row_index[:, None])


def contract_rows(left, right):
    return lax.dot_general(
        left, right, (((0,), (0,)), ((), ())), preferred_element_type=jnp.float32
    )


def contract_cols(left, right):
    return lax.dot_general(
        left, right, (((1,), (1,)), ((), ())), preferred_element_type=jnp.float32
    )


def per_device(
    tokens,
    lengths,
    ln_gain,
    ln_bias,
    joined_weight,
    joined_bias,
    dense_weight,
    up_weight,
    up_bias,
    down_weight,
    output_bias,
    cotangent,
):
    leading = lax.axis_index("pipe") == 0
    model_width = joined_weight.shape[1]
    local_width = joined_weight.shape[3]
    local_heads = local_width // HD
    hidden_local = up_weight.shape[2]
    quarter = tokens.shape[1]
    score_scale = HD ** (-0.5)
    ln_gains = ln_gain[0].astype(jnp.float32)
    ln_shifts = ln_bias[0].astype(jnp.float32)
    joined_mat = joined_weight[0].reshape(model_width, 3 * local_width)
    joined_add = joined_bias[0].astype(jnp.float32).reshape(3 * local_width)
    dense_mat = dense_weight[0]
    up_mat = up_weight[0]
    up_add = up_bias[0].astype(jnp.float32)
    down_mat = down_weight[0]
    bias_sum = output_bias[0, 0].astype(jnp.float32) + output_bias[0, 1].astype(jnp.float32)
    gathered_pieces = tensor_pieces(jnp.concatenate([tokens, cotangent], axis=0))
    gathered_rows = jnp.concatenate(gathered_pieces, axis=1)
    input_rows = gathered_rows[: tokens.shape[0]]
    output_grads = gathered_rows[tokens.shape[0] :]
    segment_all, place_all = positions(lengths, MB)
    cos_all, sin_all = rotary(place_all)

    def pick(early_val, late_val):
        return jax.tree.map(
            lambda upper_val, lower_val: jnp.where(leading, upper_val, lower_val),
            early_val,
            late_val,
        )

    received = jnp.zeros((MB, model_width), jnp.bfloat16)
    tick_outputs = []
    tick_stored = []
    for section_tick in range(NMB + 1):
        early_block = min(section_tick, NMB - 1)
        late_block = max(section_tick - 1, 0)
        block_rows = jnp.where(
            leading, input_rows[early_block * MB : (early_block + 1) * MB], received
        )
        segment, cosv, sinv = pick(
            (segment_all[early_block], cos_all[early_block], sin_all[early_block]),
            (segment_all[late_block], cos_all[late_block], sin_all[late_block]),
        )
        inputs = block_rows.astype(jnp.float32)
        row_mean = jnp.mean(inputs, axis=1, keepdims=True)
        centred = inputs - row_mean
        forward_inv_scale = lax.rsqrt(jnp.mean(centred * centred, axis=1, keepdims=True) + EPSILON)
        forward_normed = centred * forward_inv_scale
        forward_h_attn = (forward_normed * ln_gains[0] + ln_shifts[0]).astype(jnp.bfloat16)
        forward_h_mlp = (forward_normed * ln_gains[1] + ln_shifts[1]).astype(jnp.bfloat16)
        joined_proj = (
            jnp.dot(forward_h_attn, joined_mat, preferred_element_type=jnp.float32) + joined_add
        )
        forward_block_len = block_rows.shape[0]
        forward_queries = rotate(
            joined_proj[:, :local_width].reshape(forward_block_len, local_heads, HD), cosv, sinv
        ).astype(jnp.bfloat16)
        forward_keys_rot = rotate(
            joined_proj[:, local_width : 2 * local_width].reshape(
                forward_block_len, local_heads, HD
            ),
            cosv,
            sinv,
        ).astype(jnp.bfloat16)
        forward_values = (
            joined_proj[:, 2 * local_width :]
            .reshape(forward_block_len, local_heads, HD)
            .astype(jnp.bfloat16)
        )
        forward_scores = (
            jnp.einsum(
                "qhd,khd->hqk",
                forward_queries,
                forward_keys_rot,
                preferred_element_type=jnp.float32,
            )
            * score_scale
        )
        forward_scores = jnp.where(allowed_keys(segment)[None], forward_scores, MASKED)
        row_top = jnp.max(forward_scores, axis=2, keepdims=True)
        exponent = jnp.exp(forward_scores - row_top)
        row_total = jnp.sum(exponent, axis=2, keepdims=True)
        forward_log_total = row_top + jnp.log(row_total)
        weights_low = (exponent / row_total).astype(jnp.bfloat16)
        forward_context = jnp.einsum(
            "hqk,khd->qhd", weights_low, forward_values, preferred_element_type=jnp.float32
        )
        forward_context = forward_context.reshape(forward_block_len, local_width).astype(
            jnp.bfloat16
        )
        forward_up_proj = (
            jnp.dot(forward_h_mlp, up_mat, preferred_element_type=jnp.float32) + up_add
        )
        forward_activated = exact_gelu(forward_up_proj).astype(jnp.bfloat16)
        partial_value = jnp.dot(forward_context, dense_mat, preferred_element_type=jnp.float32)
        partial_value = partial_value + jnp.dot(
            forward_activated, down_mat, preferred_element_type=jnp.float32
        )
        branches = tensor_sum(partial_value.astype(jnp.bfloat16))
        result = inputs + branches + bias_sum
        forward_stored = (
            forward_normed,
            forward_inv_scale,
            forward_h_attn,
            forward_h_mlp,
            forward_queries,
            forward_keys_rot,
            forward_values,
            forward_log_total,
            forward_context,
            forward_up_proj,
            forward_activated,
        )
        result, stored = (result, forward_stored)
        result_low = result.astype(jnp.bfloat16)
        tick_outputs.append(result_low)
        tick_stored.append((stored, segment, cosv, sinv))
        if section_tick < NMB:
            received = passed_along(result_low, "pipe", 1)
    column_start = lax.axis_index("tensor") * quarter
    section_rows = jnp.concatenate(
        [jnp.where(leading, tick_outputs[block], tick_outputs[block + 1]) for block in range(NMB)],
        axis=0,
    )
    section_out = lax.dynamic_slice_in_dim(section_rows, column_start, quarter, 1)[None]
    returned = jnp.zeros((MB, model_width), jnp.bfloat16)
    tick_grads = []
    totals = None
    for section_tick in range(NMB + 1):
        own_block = min(section_tick, NMB - 1)
        late_tick = max(section_tick - 1, 0)
        upper_tick = min(section_tick + 1, NMB)
        from_output = output_grads[own_block * MB : (own_block + 1) * MB]
        if section_tick == NMB:
            from_output = jnp.zeros_like(from_output)
        grad_rows = jnp.where(leading, returned, from_output)
        stored, segment, cosv, sinv = pick(tick_stored[late_tick], tick_stored[upper_tick])
        (
            normed,
            inv_scale,
            h_attn,
            h_mlp,
            queries,
            keys_rot,
            values,
            log_total,
            context,
            up_proj,
            activated,
        ) = stored
        block_len = grad_rows.shape[0]
        grad_wide = grad_rows.astype(jnp.float32)
        column_sum = jnp.sum(grad_wide, axis=0)
        backward_grad_dense = contract_rows(context, grad_rows)
        backward_grad_down = contract_rows(activated, grad_rows)
        d_context = contract_cols(grad_rows, dense_mat).astype(jnp.bfloat16)
        d_act = contract_cols(grad_rows, down_mat)
        unused, slope_back = jax.vjp(exact_gelu, up_proj)
        d_up = slope_back(d_act)[0].astype(jnp.bfloat16)
        grad_up_add = jnp.sum(d_up.astype(jnp.float32), axis=0)
        backward_grad_up = contract_rows(h_mlp, d_up)
        d_hmlp = contract_cols(d_up, up_mat)
        scores = (
            jnp.einsum("qhd,khd->hqk", queries, keys_rot, preferred_element_type=jnp.float32)
            * score_scale
        )
        scores = jnp.where(allowed_keys(segment)[None], scores, MASKED)
        weights_soft = jnp.exp(scores - log_total)
        d_context3 = d_context.reshape(block_len, local_heads, HD)
        d_values = jnp.einsum(
            "hqk,qhd->khd",
            weights_soft.astype(jnp.bfloat16),
            d_context3,
            preferred_element_type=jnp.float32,
        ).astype(jnp.bfloat16)
        d_weights = jnp.einsum(
            "qhd,khd->hqk", d_context3, values, preferred_element_type=jnp.float32
        )
        row_delta = jnp.sum(weights_soft * d_weights, axis=2, keepdims=True)
        d_scores = (weights_soft * (d_weights - row_delta)).astype(jnp.bfloat16)
        d_queries = (
            jnp.einsum("hqk,khd->qhd", d_scores, keys_rot, preferred_element_type=jnp.float32)
            * score_scale
        )
        d_keys = (
            jnp.einsum("hqk,qhd->khd", d_scores, queries, preferred_element_type=jnp.float32)
            * score_scale
        )
        d_queries = (
            rotate_back(d_queries, cosv, sinv).reshape(block_len, local_width).astype(jnp.bfloat16)
        )
        d_keys = (
            rotate_back(d_keys, cosv, sinv).reshape(block_len, local_width).astype(jnp.bfloat16)
        )
        d_joined = jnp.concatenate(
            [d_queries, d_keys, d_values.reshape(block_len, local_width)], axis=1
        )
        grad_joined_add = jnp.sum(d_joined.astype(jnp.float32), axis=0)
        backward_grad_joined = contract_rows(d_joined, h_attn)
        d_hattn = contract_cols(d_joined, joined_mat)
        d_both = tensor_sum(
            jnp.concatenate([d_hattn, d_hmlp], axis=1).astype(jnp.bfloat16)
        )
        d_hattn, d_hmlp = d_both[:, :model_width], d_both[:, model_width:]
        grad_gains = jnp.concatenate(
            [jnp.sum(d_hattn * normed, axis=0), jnp.sum(d_hmlp * normed, axis=0)]
        )
        grad_shifts = jnp.concatenate([jnp.sum(d_hattn, axis=0), jnp.sum(d_hmlp, axis=0)])
        d_norm = d_hattn * ln_gains[0] + d_hmlp * ln_gains[1]
        grad_input = grad_wide + inv_scale * (
            d_norm
            - jnp.mean(d_norm, axis=1, keepdims=True)
            - normed * jnp.mean(d_norm * normed, axis=1, keepdims=True)
        )
        small_terms = jnp.concatenate(
            [grad_gains, grad_shifts, column_sum, column_sum, grad_joined_add, grad_up_add]
        )
        terms = (
            backward_grad_joined[None],
            backward_grad_dense[None],
            backward_grad_up[None],
            backward_grad_down[None],
            small_terms[None],
        )
        grad_input, terms = (grad_input, terms)
        grad_low = grad_input.astype(jnp.bfloat16)
        tick_grads.append(grad_low)
        if totals is None:
            totals = terms
        else:
            totals = jax.tree.map(lambda older, newer: older + newer, totals, terms)
        if section_tick < NMB:
            returned = passed_along(grad_low, "pipe", -1)
    small_rows = totals[4][0]
    small_pad = (-small_rows.shape[0]) % model_width
    small_rows = jnp.pad(small_rows, (0, small_pad)).reshape(-1, model_width)
    pieces = (totals[0][0], totals[1][0], totals[2][0], totals[3][0], small_rows)
    slab = jnp.concatenate([piece.astype(jnp.bfloat16) for piece in pieces], axis=0)
    slab = lax.psum(slab, "dp").astype(jnp.float32)
    summed = []
    offset = 0
    for piece in pieces:
        summed.append(slab[offset : offset + piece.shape[0]])
        offset = offset + piece.shape[0]
    grad_rows_all = jnp.concatenate(
        [jnp.where(leading, tick_grads[block + 1], tick_grads[block]) for block in range(NMB)],
        axis=0,
    )
    input_grad = lax.dynamic_slice_in_dim(grad_rows_all, column_start, quarter, 1)[None]
    grad_joined = summed[0].T.reshape(1, model_width, 3, local_width)
    grad_dense = summed[1][None]
    grad_up = summed[2][None]
    grad_down = summed[3][None]
    small_sum = summed[4].reshape(-1)
    offset = 0
    grad_ln_gain = small_sum[offset : offset + 2 * model_width].reshape(1, 2, model_width)
    offset = offset + 2 * model_width
    grad_ln_bias = small_sum[offset : offset + 2 * model_width].reshape(1, 2, model_width)
    offset = offset + 2 * model_width
    grad_output_bias = small_sum[offset : offset + 2 * model_width].reshape(1, 2, model_width)
    offset = offset + 2 * model_width
    grad_joined_bias = small_sum[offset : offset + 3 * local_width].reshape(1, 3, local_width)
    offset = offset + 3 * local_width
    grad_up_bias = small_sum[offset : offset + hidden_local].reshape(1, hidden_local)
    return (
        section_out,
        input_grad,
        grad_ln_gain,
        grad_ln_bias,
        grad_joined,
        grad_joined_bias,
        grad_dense,
        grad_up,
        grad_up_bias,
        grad_down,
        grad_output_bias,
    )


def solution(mesh):
    placed = (
        P("dp", "tensor"),
        P("dp", None),
        P("pipe", None, None),
        P("pipe", None, None),
        P("pipe", None, None, "tensor"),
        P("pipe", None, "tensor"),
        P("pipe", "tensor", None),
        P("pipe", None, "tensor"),
        P("pipe", "tensor"),
        P("pipe", "tensor", None),
        P("pipe", None, None),
        P("dp", "tensor"),
    )
    return jax.shard_map(
        per_device,
        mesh=mesh,
        in_specs=placed,
        out_specs=(
            P("pipe", "dp", "tensor"),
            P("pipe", "dp", "tensor"),
            P("pipe", None, None),
            P("pipe", None, None),
            P("pipe", None, None, "tensor"),
            P("pipe", None, "tensor"),
            P("pipe", "tensor", None),
            P("pipe", None, "tensor"),
            P("pipe", "tensor"),
            P("pipe", "tensor", None),
            P("pipe", None, None),
        ),
        check_vma=False,
    )
```

profile of v0, /device:TPU:0, one launch (start us, length us, event | category | flops | bytes accessed | tf_op | source)
XLA Modules:
  0.0 557.1 jit_solution(13667004256023735411)
XLA Ops:
  11.4 3.6 collective-permute-start.1
  29.6 8.4 %collective-permute-done.1 = bf16[1024,256]{1,0:T(8,128)(2,1)} collective-permute-done((bf16[1024,256]{1,0:T(8,128)(2,1)S(1)}, bf16[1024,256]{1,0:T(8,128)(2,1)}, u32[]{:S(2)}, u32[]{:S(2)}) %collective-permute-start.1) | collective-permute-done | bytes 524320 | tf_op jit(solution)/shard_map/ppermute | solution.py:28
  53.1 3.0 collective-permute-done.3
  56.1 6.8 %collective-permute-done.4 = bf16[128,1024]{1,0:T(8,128)(2,1)S(1)} collective-permute-done((bf16[128,1024]{1,0:T(8,128)(2,1)S(1)}, bf16[128,1024]{1,0:T(8,128)(2,1)S(1)}, u32[]{:S(2)}, u32[]{:S(2)}) %collective-permute-start.4) | collective-permute-done | bytes 262176 | tf_op jit(solution)/shard_map/ppermute | solution.py:28
  64.1 5.7 %collective-permute-start.6 = (bf16[128,1024]{1,0:T(8,128)(2,1)S(1)}, bf16[128,1024]{1,0:T(8,128)(2,1)}, u32[]{:S(2)}, u32[]{:S(2)}) collective-permute-start(bf16[128,1024]{1,0:T(8,128)(2,1)S(1)} %fusion.193), channel_id=1, source_target_pairs={{0,64},{1,65},{2,66},{3,67},{4,68},{5,69},{6,70},{7,71},{8,72},{9,... | collective-permute-start | bytes 786440 | tf_op jit(solution)/shard_map/ppermute | solution.py:19
  104.4 4.4 fusion.357
  118.0 6.2 %collective-permute-start.10 = (bf16[128,1024]{1,0:T(8,128)(2,1)S(1)}, bf16[128,1024]{1,0:T(8,128)(2,1)S(1)}, u32[]{:S(2)}, u32[]{:S(2)}) collective-permute-start(bf16[128,1024]{1,0:T(8,128)(2,1)S(1)} %get-tuple-element.134), channel_id=1, source_target_pairs={{0,64},{1,65},{2,66},{3,67},{4,68},{5,69},{6,70},{7,71},{8,72},{9,... | collective-permute-start | bytes 786440 | tf_op jit(solution)/shard_map/ppermute | solution.py:19
  124.3 4.4 collective-permute-done.23
  131.9 8.6 %collective-permute-done.25 = bf16[128,1024]{1,0:T(8,128)(2,1)S(1)} collective-permute-done((bf16[128,1024]{1,0:T(8,128)(2,1)S(1)}, bf16[128,1024]{1,0:T(8,128)(2,1)S(1)}, u32[]{:S(2)}, u32[]{:S(2)}) %collective-permute-start.25) | collective-permute-done | bytes 262176 | tf_op jit(solution)/shard_map/ppermute | solution.py:19
  165.1 3.2 convert_reduce_fusion.13
  180.1 4.4 fusion.355
  184.7 3.0 fusion.364
  196.2 5.7 %collective-permute-done.26 = bf16[128,2048]{1,0:T(8,128)(2,1)S(1)} collective-permute-done((bf16[128,2048]{1,0:T(8,128)(2,1)S(1)}, bf16[128,2048]{1,0:T(8,128)(2,1)S(1)}, u32[]{:S(2)}, u32[]{:S(2)}) %collective-permute-start.26) | collective-permute-done | bytes 524320 | tf_op jit(solution)/shard_map/ppermute | solution.py:28
  210.0 4.6 collective-permute-done.29
  241.1 3.2 convert_reduce_fusion.12
  256.1 4.4 fusion.353
  260.7 2.9 fusion.362
  271.8 4.8 collective-permute-done.30
  281.1 8.3 %collective-permute-done.33 = bf16[128,1024]{1,0:T(8,128)(2,1)S(1)} collective-permute-done((bf16[128,1024]{1,0:T(8,128)(2,1)S(1)}, bf16[128,1024]{1,0:T(8,128)(2,1)S(1)}, u32[]{:S(2)}, u32[]{:S(2)}) %collective-permute-start.33) | collective-permute-done | bytes 262176 | tf_op jit(solution)/shard_map/ppermute | solution.py:19
  319.9 3.0 collective-permute-start.35
  325.7 4.4 fusion.351
  337.0 5.5 collective-permute-done.35
  381.9 7.4 %fusion = bf16[3080,1024]{1,0:T(8,128)(2,1)} fusion(bf16[3080,1024]{1,0:T(8,128)(2,1)} %fusion.41, f32[1024,1024]{1,0:T(8,128)} %fusion.351, f32[1024,1024]{1,0:T(8,128)} %fusion.353, f32[1024,1024]{1,0:T(8,128)S(1)} %copy-done.277, f32[1024,1024]{1,0:T(8,128)} %fusion.355, pred[]{:T(512)S(6)} %eq.179, bf16[128,1024]{1,0:T(8,128)(2,1)S(1)} %copy-done.35, ...), kind=kOutput, calls=%fused_computation.5 | convolution fusion | flops 290979840 | bytes 20186112 | tf_op jit(solution)/shard_map/dot_general | solution.py:112
  389.5 4.2 collective-permute-done.39
  398.1 3.2 fusion.92
  405.9 4.5 collective-permute-done.19
  410.4 6.8 %collective-permute-done.20 = bf16[128,1024]{1,0:T(8,128)(2,1)} collective-permute-done((bf16[128,1024]{1,0:T(8,128)(2,1)}, bf16[128,1024]{1,0:T(8,128)(2,1)}, u32[]{:S(2)}, u32[]{:S(2)}) %collective-permute-start.20) | collective-permute-done | bytes 262176 | tf_op jit(solution)/shard_map/ppermute | solution.py:28
  421.7 109.6 %all-reduce.3.cloned.1.call-done = bf16[3080,1024]{1,0:T(8,128)(2,1)} async-done(((bf16[3080,1024]{1,0:T(8,128)(2,1)}), bf16[3080,1024]{1,0:T(8,128)(2,1)}) %all-reduce.3.cloned.1.call-update) | async-done | bytes 6307856 | tf_op jit(solution)/shard_map/psum | solution.py:375
  531.3 4.3 convert_element_type.749
  537.3 4.2 slice_bitcast_fusion
  542.2 3.4 slice.681
  545.6 3.5 copy.182
  (940 shorter events, 278.5 us)
Async XLA Ops:
  7.2 524.1 %all-reduce.3.cloned.1.call-start = ((), (), s32[]{:S(2)}) async-start(), calls=%async_computation | async-start | bytes 12615680 | tf_op jit(solution)/shard_map/psum | solution.py:375
  9.4 20.2 %collective-permute-start = (bf16[1024,256]{1,0:T(8,128)(2,1)S(1)}, bf16[1024,256]{1,0:T(8,128)(2,1)S(1)}, u32[]{:S(2)}, u32[]{:S(2)}) collective-permute-start(bf16[1024,256]{1,0:T(8,128)(2,1)S(1)} %constant_dynamic-update-slice_fusion), channel_id=1, source_target_pairs={{0,16},{16,32},{32,48},{48,0},{1,17},{17,33},{33,49},{49,1},{2,18}... | collective-permute-start | bytes 1572872 | tf_op jit(solution)/shard_map/ppermute | solution.py:28
  11.4 26.6 %collective-permute-start.1 = (bf16[1024,256]{1,0:T(8,128)(2,1)S(1)}, bf16[1024,256]{1,0:T(8,128)(2,1)}, u32[]{:S(2)}, u32[]{:S(2)}) collective-permute-start(bf16[1024,256]{1,0:T(8,128)(2,1)S(1)} %constant_dynamic-update-slice_fusion), channel_id=1, source_target_pairs={{0,32},{16,48},{32,0},{48,16},{1,33},{17,49},{33,1},{49,17},{2,34}... | collective-permute-start | bytes 1572872 | tf_op jit(solution)/shard_map/ppermute | solution.py:28
  15.0 23.0 %collective-permute-start.2 = (bf16[1024,256]{1,0:T(8,128)(2,1)S(1)}, bf16[1024,256]{1,0:T(8,128)(2,1)}, u32[]{:S(2)}, u32[]{:S(2)}) collective-permute-start(bf16[1024,256]{1,0:T(8,128)(2,1)S(1)} %constant_dynamic-update-slice_fusion), channel_id=1, source_target_pairs={{0,48},{16,0},{32,16},{48,32},{1,49},{17,1},{33,17},{49,33},{2,50}... | collective-permute-start | bytes 1572872 | tf_op jit(solution)/shard_map/ppermute | solution.py:28
  48.7 14.2 %collective-permute-start.4 = (bf16[128,1024]{1,0:T(8,128)(2,1)S(1)}, bf16[128,1024]{1,0:T(8,128)(2,1)S(1)}, u32[]{:S(2)}, u32[]{:S(2)}) collective-permute-start(bf16[128,1024]{1,0:T(8,128)(2,1)S(1)} %fusion.104), channel_id=1, source_target_pairs={{0,32},{16,48},{32,0},{48,16},{1,33},{17,49},{33,1},{49,17},{2,34}... | collective-permute-start | bytes 786440 | tf_op jit(solution)/shard_map/ppermute | solution.py:28
  90.7 21.8 %collective-permute-start.7 = (bf16[128,1024]{1,0:T(8,128)(2,1)S(1)}, bf16[128,1024]{1,0:T(8,128)(2,1)S(1)}, u32[]{:S(2)}, u32[]{:S(2)}) collective-permute-start(bf16[128,1024]{1,0:T(8,128)(2,1)S(1)} %fusion.101), channel_id=1, source_target_pairs={{0,16},{16,32},{32,48},{48,0},{1,17},{17,33},{33,49},{49,1},{2,18}... | collective-permute-start | bytes 786440 | tf_op jit(solution)/shard_map/ppermute | solution.py:28
  92.5 24.6 %collective-permute-start.8 = (bf16[128,1024]{1,0:T(8,128)(2,1)S(1)}, bf16[128,1024]{1,0:T(8,128)(2,1)S(1)}, u32[]{:S(2)}, u32[]{:S(2)}) collective-permute-start(bf16[128,1024]{1,0:T(8,128)(2,1)S(1)} %fusion.101), channel_id=1, source_target_pairs={{0,32},{16,48},{32,0},{48,16},{1,33},{17,49},{33,1},{49,17},{2,34}... | collective-permute-start | bytes 786440 | tf_op jit(solution)/shard_map/ppermute | solution.py:28
  95.3 21.8 %collective-permute-start.9 = (bf16[128,1024]{1,0:T(8,128)(2,1)S(1)}, bf16[128,1024]{1,0:T(8,128)(2,1)S(1)}, u32[]{:S(2)}, u32[]{:S(2)}) collective-permute-start(bf16[128,1024]{1,0:T(8,128)(2,1)S(1)} %fusion.101), channel_id=1, source_target_pairs={{0,48},{16,0},{32,16},{48,32},{1,49},{17,1},{33,17},{49,33},{2,50}... | collective-permute-start | bytes 786440 | tf_op jit(solution)/shard_map/ppermute | solution.py:28
  101.7 22.6 %collective-permute-start.22 = (bf16[128,2048]{1,0:T(8,128)(2,1)S(1)}, bf16[128,2048]{1,0:T(8,128)(2,1)S(1)}, u32[]{:S(2)}, u32[]{:S(2)}) collective-permute-start(bf16[128,2048]{1,0:T(8,128)(2,1)S(1)} %pad_maximum_fusion.1), channel_id=1, source_target_pairs={{0,16},{16,32},{32,48},{48,0},{1,17},{17,33},{33,49},{49,1},{2,18}... | collective-permute-start | bytes 1572872 | tf_op jit(solution)/shard_map/ppermute | solution.py:28
  103.7 25.0 %collective-permute-start.23 = (bf16[128,2048]{1,0:T(8,128)(2,1)S(1)}, bf16[128,2048]{1,0:T(8,128)(2,1)S(1)}, u32[]{:S(2)}, u32[]{:S(2)}) collective-permute-start(bf16[128,2048]{1,0:T(8,128)(2,1)S(1)} %pad_maximum_fusion.1), channel_id=1, source_target_pairs={{0,32},{16,48},{32,0},{48,16},{1,33},{17,49},{33,1},{49,17},{2,34}... | collective-permute-start | bytes 1572872 | tf_op jit(solution)/shard_map/ppermute | solution.py:28
  112.5 16.2 %collective-permute-start.24 = (bf16[128,2048]{1,0:T(8,128)(2,1)S(1)}, bf16[128,2048]{1,0:T(8,128)(2,1)S(1)}, u32[]{:S(2)}, u32[]{:S(2)}) collective-permute-start(bf16[128,2048]{1,0:T(8,128)(2,1)S(1)} %pad_maximum_fusion.1), channel_id=1, source_target_pairs={{0,48},{16,0},{32,16},{48,32},{1,49},{17,1},{33,17},{49,33},{2,50}... | collective-permute-start | bytes 1572872 | tf_op jit(solution)/shard_map/ppermute | solution.py:28
  118.0 13.9 %collective-permute-start.10 = (bf16[128,1024]{1,0:T(8,128)(2,1)S(1)}, bf16[128,1024]{1,0:T(8,128)(2,1)S(1)}, u32[]{:S(2)}, u32[]{:S(2)}) collective-permute-start(bf16[128,1024]{1,0:T(8,128)(2,1)S(1)} %get-tuple-element.134), channel_id=1, source_target_pairs={{0,64},{1,65},{2,66},{3,67},{4,68},{5,69},{6,70},{7,71},{8,72},{9,... | collective-permute-start | bytes 786440 | tf_op jit(solution)/shard_map/ppermute | solution.py:19
  160.3 27.4 %collective-permute-start.11 = (bf16[128,1024]{1,0:T(8,128)(2,1)}, bf16[128,1024]{1,0:T(8,128)(2,1)}, u32[]{:S(2)}, u32[]{:S(2)}) collective-permute-start(bf16[128,1024]{1,0:T(8,128)(2,1)} %fusion.98), channel_id=1, source_target_pairs={{0,16},{16,32},{32,48},{48,0},{1,17},{17,33},{33,49},{49,1},{2,18}... | collective-permute-start | bytes 786440 | tf_op jit(solution)/shard_map/ppermute | solution.py:28
  162.4 30.0 %collective-permute-start.12 = (bf16[128,1024]{1,0:T(8,128)(2,1)}, bf16[128,1024]{1,0:T(8,128)(2,1)}, u32[]{:S(2)}, u32[]{:S(2)}) collective-permute-start(bf16[128,1024]{1,0:T(8,128)(2,1)} %fusion.98), channel_id=1, source_target_pairs={{0,32},{16,48},{32,0},{48,16},{1,33},{17,49},{33,1},{49,17},{2,34}... | collective-permute-start | bytes 786440 | tf_op jit(solution)/shard_map/ppermute | solution.py:28
  165.1 27.3 %collective-permute-start.13 = (bf16[128,1024]{1,0:T(8,128)(2,1)}, bf16[128,1024]{1,0:T(8,128)(2,1)}, u32[]{:S(2)}, u32[]{:S(2)}) collective-permute-start(bf16[128,1024]{1,0:T(8,128)(2,1)} %fusion.98), channel_id=1, source_target_pairs={{0,48},{16,0},{32,16},{48,32},{1,49},{17,1},{33,17},{49,33},{2,50}... | collective-permute-start | bytes 786440 | tf_op jit(solution)/shard_map/ppermute | solution.py:28
  177.1 24.7 %collective-permute-start.26 = (bf16[128,2048]{1,0:T(8,128)(2,1)S(1)}, bf16[128,2048]{1,0:T(8,128)(2,1)S(1)}, u32[]{:S(2)}, u32[]{:S(2)}) collective-permute-start(bf16[128,2048]{1,0:T(8,128)(2,1)S(1)} %pad_maximum_fusion.2), channel_id=1, source_target_pairs={{0,16},{16,32},{32,48},{48,0},{1,17},{17,33},{33,49},{49,1},{2,18}... | collective-permute-start | bytes 1572872 | tf_op jit(solution)/shard_map/ppermute | solution.py:28
  179.2 22.7 %collective-permute-start.27 = (bf16[128,2048]{1,0:T(8,128)(2,1)S(1)}, bf16[128,2048]{1,0:T(8,128)(2,1)S(1)}, u32[]{:S(2)}, u32[]{:S(2)}) collective-permute-start(bf16[128,2048]{1,0:T(8,128)(2,1)S(1)} %pad_maximum_fusion.2), channel_id=1, source_target_pairs={{0,32},{16,48},{32,0},{48,16},{1,33},{17,49},{33,1},{49,17},{2,34}... | collective-permute-start | bytes 1572872 | tf_op jit(solution)/shard_map/ppermute | solution.py:28
  187.7 14.8 %collective-permute-start.28 = (bf16[128,2048]{1,0:T(8,128)(2,1)S(1)}, bf16[128,2048]{1,0:T(8,128)(2,1)S(1)}, u32[]{:S(2)}, u32[]{:S(2)}) collective-permute-start(bf16[128,2048]{1,0:T(8,128)(2,1)S(1)} %pad_maximum_fusion.2), channel_id=1, source_target_pairs={{0,48},{16,0},{32,16},{48,32},{1,49},{17,1},{33,17},{49,33},{2,50}... | collective-permute-start | bytes 1572872 | tf_op jit(solution)/shard_map/ppermute | solution.py:28
  194.6 15.4 %collective-permute-start.14 = (bf16[128,1024]{1,0:T(8,128)(2,1)S(1)}, bf16[128,1024]{1,0:T(8,128)(2,1)S(1)}, u32[]{:S(2)}, u32[]{:S(2)}) collective-permute-start(bf16[128,1024]{1,0:T(8,128)(2,1)S(1)} %get-tuple-element.130), channel_id=1, source_target_pairs={{0,64},{1,65},{2,66},{3,67},{4,68},{5,69},{6,70},{7,71},{8,72},{9,... | collective-permute-start | bytes 786440 | tf_op jit(solution)/shard_map/ppermute | solution.py:19
  236.5 27.1 %collective-permute-start.15 = (bf16[128,1024]{1,0:T(8,128)(2,1)}, bf16[128,1024]{1,0:T(8,128)(2,1)}, u32[]{:S(2)}, u32[]{:S(2)}) collective-permute-start(bf16[128,1024]{1,0:T(8,128)(2,1)} %fusion.95), channel_id=1, source_target_pairs={{0,16},{16,32},{32,48},{48,0},{1,17},{17,33},{33,49},{49,1},{2,18}... | collective-permute-start | bytes 786440 | tf_op jit(solution)/shard_map/ppermute | solution.py:28
  238.3 29.6 %collective-permute-start.16 = (bf16[128,1024]{1,0:T(8,128)(2,1)}, bf16[128,1024]{1,0:T(8,128)(2,1)}, u32[]{:S(2)}, u32[]{:S(2)}) collective-permute-start(bf16[128,1024]{1,0:T(8,128)(2,1)} %fusion.95), channel_id=1, source_target_pairs={{0,32},{16,48},{32,0},{48,16},{1,33},{17,49},{33,1},{49,17},{2,34}... | collective-permute-start | bytes 786440 | tf_op jit(solution)/shard_map/ppermute | solution.py:28
  241.0 26.9 %collective-permute-start.17 = (bf16[128,1024]{1,0:T(8,128)(2,1)}, bf16[128,1024]{1,0:T(8,128)(2,1)}, u32[]{:S(2)}, u32[]{:S(2)}) collective-permute-start(bf16[128,1024]{1,0:T(8,128)(2,1)} %fusion.95), channel_id=1, source_target_pairs={{0,48},{16,0},{32,16},{48,32},{1,49},{17,1},{33,17},{49,33},{2,50}... | collective-permute-start | bytes 786440 | tf_op jit(solution)/shard_map/ppermute | solution.py:28
  253.0 23.5 %collective-permute-start.30 = (bf16[128,2048]{1,0:T(8,128)(2,1)S(1)}, bf16[128,2048]{1,0:T(8,128)(2,1)S(1)}, u32[]{:S(2)}, u32[]{:S(2)}) collective-permute-start(bf16[128,2048]{1,0:T(8,128)(2,1)S(1)} %pad_maximum_fusion.3), channel_id=1, source_target_pairs={{0,16},{16,32},{32,48},{48,0},{1,17},{17,33},{33,49},{49,1},{2,18}... | collective-permute-start | bytes 1572872 | tf_op jit(solution)/shard_map/ppermute | solution.py:28
  255.1 21.4 %collective-permute-start.31 = (bf16[128,2048]{1,0:T(8,128)(2,1)S(1)}, bf16[128,2048]{1,0:T(8,128)(2,1)S(1)}, u32[]{:S(2)}, u32[]{:S(2)}) collective-permute-start(bf16[128,2048]{1,0:T(8,128)(2,1)S(1)} %pad_maximum_fusion.3), channel_id=1, source_target_pairs={{0,32},{16,48},{32,0},{48,16},{1,33},{17,49},{33,1},{49,17},{2,34}... | collective-permute-start | bytes 1572872 | tf_op jit(solution)/shard_map/ppermute | solution.py:28
  263.6 13.7 %collective-permute-start.32 = (bf16[128,2048]{1,0:T(8,128)(2,1)S(1)}, bf16[128,2048]{1,0:T(8,128)(2,1)S(1)}, u32[]{:S(2)}, u32[]{:S(2)}) collective-permute-start(bf16[128,2048]{1,0:T(8,128)(2,1)S(1)} %pad_maximum_fusion.3), channel_id=1, source_target_pairs={{0,48},{16,0},{32,16},{48,32},{1,49},{17,1},{33,17},{49,33},{2,50}... | collective-permute-start | bytes 1572872 | tf_op jit(solution)/shard_map/ppermute | solution.py:28
  318.5 18.6 %collective-permute-start.34 = (bf16[128,2048]{1,0:T(8,128)(2,1)S(1)}, bf16[128,2048]{1,0:T(8,128)(2,1)S(1)}, u32[]{:S(2)}, u32[]{:S(2)}) collective-permute-start(bf16[128,2048]{1,0:T(8,128)(2,1)S(1)} %pad_maximum_fusion.4), channel_id=1, source_target_pairs={{0,16},{16,32},{32,48},{48,0},{1,17},{17,33},{33,49},{49,1},{2,18}... | collective-permute-start | bytes 1572872 | tf_op jit(solution)/shard_map/ppermute | solution.py:28
  319.9 22.6 %collective-permute-start.35 = (bf16[128,2048]{1,0:T(8,128)(2,1)S(1)}, bf16[128,2048]{1,0:T(8,128)(2,1)S(1)}, u32[]{:S(2)}, u32[]{:S(2)}) collective-permute-start(bf16[128,2048]{1,0:T(8,128)(2,1)S(1)} %pad_maximum_fusion.4), channel_id=1, source_target_pairs={{0,32},{16,48},{32,0},{48,16},{1,33},{17,49},{33,1},{49,17},{2,34}... | collective-permute-start | bytes 1572872 | tf_op jit(solution)/shard_map/ppermute | solution.py:28
  322.9 19.6 %collective-permute-start.36 = (bf16[128,2048]{1,0:T(8,128)(2,1)S(1)}, bf16[128,2048]{1,0:T(8,128)(2,1)S(1)}, u32[]{:S(2)}, u32[]{:S(2)}) collective-permute-start(bf16[128,2048]{1,0:T(8,128)(2,1)S(1)} %pad_maximum_fusion.4), channel_id=1, source_target_pairs={{0,48},{16,0},{32,16},{48,32},{1,49},{17,1},{33,17},{49,33},{2,50}... | collective-permute-start | bytes 1572872 | tf_op jit(solution)/shard_map/ppermute | solution.py:28
  366.2 23.2 %collective-permute-start.38 = (bf16[128,2048]{1,0:T(8,128)(2,1)S(1)}, bf16[128,2048]{1,0:T(8,128)(2,1)S(1)}, u32[]{:S(2)}, u32[]{:S(2)}) collective-permute-start(bf16[128,2048]{1,0:T(8,128)(2,1)S(1)} %pad_maximum_fusion.5), channel_id=1, source_target_pairs={{0,16},{16,32},{32,48},{48,0},{1,17},{17,33},{33,49},{49,1},{2,18}... | collective-permute-start | bytes 1572872 | tf_op jit(solution)/shard_map/ppermute | solution.py:28
  368.8 24.9 %collective-permute-start.39 = (bf16[128,2048]{1,0:T(8,128)(2,1)S(1)}, bf16[128,2048]{1,0:T(8,128)(2,1)S(1)}, u32[]{:S(2)}, u32[]{:S(2)}) collective-permute-start(bf16[128,2048]{1,0:T(8,128)(2,1)S(1)} %pad_maximum_fusion.5), channel_id=1, source_target_pairs={{0,32},{16,48},{32,0},{48,16},{1,33},{17,49},{33,1},{49,17},{2,34}... | collective-permute-start | bytes 1572872 | tf_op jit(solution)/shard_map/ppermute | solution.py:28
  371.5 22.2 %collective-permute-start.40 = (bf16[128,2048]{1,0:T(8,128)(2,1)S(1)}, bf16[128,2048]{1,0:T(8,128)(2,1)S(1)}, u32[]{:S(2)}, u32[]{:S(2)}) collective-permute-start(bf16[128,2048]{1,0:T(8,128)(2,1)S(1)} %pad_maximum_fusion.5), channel_id=1, source_target_pairs={{0,48},{16,0},{32,16},{48,32},{1,49},{17,1},{33,17},{49,33},{2,50}... | collective-permute-start | bytes 1572872 | tf_op jit(solution)/shard_map/ppermute | solution.py:28
  402.4 14.8 %collective-permute-start.20 = (bf16[128,1024]{1,0:T(8,128)(2,1)}, bf16[128,1024]{1,0:T(8,128)(2,1)}, u32[]{:S(2)}, u32[]{:S(2)}) collective-permute-start(bf16[128,1024]{1,0:T(8,128)(2,1)} %fusion.92), channel_id=1, source_target_pairs={{0,32},{16,48},{32,0},{48,16},{1,33},{17,49},{33,1},{49,17},{2,34}... | collective-permute-start | bytes 786440 | tf_op jit(solution)/shard_map/ppermute | solution.py:28
  (288 other events, 2163.4 us)
Sparse Core Ops, SparseCore 0:
  397.1 134.1 all-reduce.2
where the time goes:
time: 568 us; the launch traced here: 557 us
  waiting for transfers between devices  191 us (34%)
  matrix products  134 us (24%)
  local copies, waits for them, and re-layouts  80.3 us (14%)
  starting transfers between devices  76.1 us (13%)
  other arithmetic  57.4 us (10%)
  between operations  19 us (3%)
    psum x1, waiting for transfers between devices, per_device(): slab = lax.psum(slab, 'dp').astype(jnp.float32)  110 us
    dot_general x20, matrix products, contract_rows(): lax.dot_general(left, right, (((0,), (0,)), ((), ())), preferred_element_...  56.5 us
    ppermute x33, starting transfers between devices, tensor_pieces(): parts.append(lax.ppermute(x, 'tensor', pairs))  55.7 us
    ppermute x33, waiting for transfers between devices, tensor_pieces(): parts.append(lax.ppermute(x, 'tensor', pairs))  55.3 us
    ppermute x8, waiting for transfers between devices, passed_along(): return lax.ppermute(x, axis, pairs)  25.7 us
    unnamed x596, local copies, waits for them, and re-layouts  25.1 us
    dot_general x20, matrix products, contract_cols(): lax.dot_general(left, right, (((1,), (1,)), ((), ())), preferred_element_...  23.8 us
    ppermute x8, starting transfers between devices, passed_along(): return lax.ppermute(x, axis, pairs)  20.4 us
  transfers between devices with their start and end apart: 42, of which 18 were waited for; matrix products, arithmetic and copies ran while one was open for 24% of the time, Pallas kernels for 0%

commit v1 on v0

--- a/solution.py
+++ b/solution.py
@@ -2,6 +2,8 @@
 import jax.numpy as jnp
 from jax import lax
 from jax.sharding import PartitionSpec as P
+from jax.experimental import pallas as pl
+from jax.experimental.pallas import tpu as pltpu
 
 HD = 64
 ROT = 16
@@ -118,6 +120,109 @@
     return lax.dot_general(
         left, right, (((1,), (1,)), ((), ())), preferred_element_type=jnp.float32
     )
+
+
+def _allowed_in_kernel(seg_col_ref, seg_row_ref, rows):
+    row_id = lax.broadcasted_iota(jnp.int32, (rows, rows), 0)
+    col_id = lax.broadcasted_iota(jnp.int32, (rows, rows), 1)
+    return (seg_col_ref[...] == seg_row_ref[...]) & (col_id <= row_id)
+
+
+def _masked_scores(q, k, allowed):
+    scores = lax.dot_general(
+        q, k, (((1,), (1,)), ((), ())), preferred_element_type=jnp.float32
+    ) * (HD ** (-0.5))
+    return jnp.where(allowed, scores, MASKED)
+
+
+def _attention_forward_kernel(seg_col_ref, seg_row_ref, q_ref, k_ref, v_ref, ctx_ref, lt_ref):
+    rows = q_ref.shape[0]
+    allowed = _allowed_in_kernel(seg_col_ref, seg_row_ref, rows)
+    for head in range(q_ref.shape[1] // HD):
+        cols = slice(head * HD, (head + 1) * HD)
+        scores = _masked_scores(q_ref[:, cols], k_ref[:, cols], allowed)
+        row_top = jnp.max(scores, axis=1, keepdims=True)
+        exponent = jnp.exp(scores - row_top)
+        row_total = jnp.sum(exponent, axis=1, keepdims=True)
+        lt_ref[:, head : head + 1] = row_top + jnp.log(row_total)
+        weights = (exponent / row_total).astype(jnp.bfloat16)
+        ctx_ref[:, cols] = jnp.dot(
+            weights, v_ref[:, cols], preferred_element_type=jnp.float32
+        ).astype(ctx_ref.dtype)
+
+
+def _attention_backward_kernel(
+    seg_col_ref, seg_row_ref, q_ref, k_ref, v_ref, dctx_ref, lt_ref, dq_ref, dk_ref, dv_ref
+):
+    rows = q_ref.shape[0]
+    allowed = _allowed_in_kernel(seg_col_ref, seg_row_ref, rows)
+    scale = HD ** (-0.5)
+    for head in range(q_ref.shape[1] // HD):
+        cols = slice(head * HD, (head + 1) * HD)
+        q = q_ref[:, cols]
+        k = k_ref[:, cols]
+        dctx = dctx_ref[:, cols]
+        scores = _masked_scores(q, k, allowed)
+        weights = jnp.exp(scores - lt_ref[:, head : head + 1])
+        dv_ref[:, cols] = lax.dot_general(
+            weights.astype(jnp.bfloat16),
+            dctx,
+            (((0,), (0,)), ((), ())),
+            preferred_element_type=jnp.float32,
+        ).astype(dv_ref.dtype)
+        d_weights = lax.dot_general(
+            dctx, v_ref[:, cols], (((1,), (1,)), ((), ())), preferred_element_type=jnp.float32
+        )
+        row_delta = jnp.sum(weights * d_weights, axis=1, keepdims=True)
+        d_scores = (weights * (d_weights - row_delta)).astype(jnp.bfloat16)
+        dq_ref[:, cols] = jnp.dot(d_scores, k, preferred_element_type=jnp.float32) * scale
+        dk_ref[:, cols] = (
+            lax.dot_general(
+                d_scores, q, (((0,), (0,)), ((), ())), preferred_element_type=jnp.float32
+            )
+            * scale
+        )
+
+
+def _vmem_specs(count):
+    return [pl.BlockSpec(memory_space=pltpu.VMEM)] * count
+
+
+def attention_forward(q, k, v, segment):
+    rows, width = q.shape
+    heads = width // HD
+    return pl.pallas_call(
+        _attention_forward_kernel,
+        out_shape=(
+            jax.ShapeDtypeStruct((rows, width), jnp.bfloat16),
+            jax.ShapeDtypeStruct((rows, heads), jnp.float32),
+        ),
+        in_specs=_vmem_specs(5),
+        out_specs=tuple(_vmem_specs(2)),
+        cost_estimate=pl.CostEstimate(
+            flops=4 * rows * rows * width, transcendentals=rows * rows * heads,
+            bytes_accessed=4 * rows * width * 2,
+        ),
+    )(segment[:, None], segment[None, :], q, k, v)
+
+
+def attention_backward(q, k, v, d_context, log_total, segment):
+    rows, width = q.shape
+    heads = width // HD
+    return pl.pallas_call(
+        _attention_backward_kernel,
+        out_shape=(
+            jax.ShapeDtypeStruct((rows, width), jnp.float32),
+            jax.ShapeDtypeStruct((rows, width), jnp.float32),
+            jax.ShapeDtypeStruct((rows, width), jnp.bfloat16),
+        ),
+        in_specs=_vmem_specs(7),
+        out_specs=tuple(_vmem_specs(3)),
+        cost_estimate=pl.CostEstimate(
+            flops=10 * rows * rows * width, transcendentals=rows * rows * heads,
+            bytes_accessed=4 * rows * width * 2 + 2 * rows * width * 4,
+        ),
+    )(segment[:, None], segment[None, :], q, k, v, d_context, log_total)
 
 
 def per_device(
@@ -203,26 +308,12 @@
             .reshape(forward_block_len, local_heads, HD)
             .astype(jnp.bfloat16)
         )
-        forward_scores = (
-            jnp.einsum(
-                "qhd,khd->hqk",
-                forward_queries,
-                forward_keys_rot,
-                preferred_element_type=jnp.float32,
-            )
-            * score_scale
-        )
-        forward_scores = jnp.where(allowed_keys(segment)[None], forward_scores, MASKED)
-        row_top = jnp.max(forward_scores, axis=2, keepdims=True)
-        exponent = jnp.exp(forward_scores - row_top)
-        row_total = jnp.sum(exponent, axis=2, keepdims=True)
-        forward_log_total = row_top + jnp.log(row_total)
-        weights_low = (exponent / row_total).astype(jnp.bfloat16)
-        forward_context = jnp.einsum(
-            "hqk,khd->qhd", weights_low, forward_values, preferred_element_type=jnp.float32
-        )
-        forward_context = forward_context.reshape(forward_block_len, local_width).astype(
-            jnp.bfloat16
+        local_rows = (forward_block_len, local_width)
+        forward_context, forward_log_total = attention_forward(
+            forward_queries.reshape(local_rows),
+            forward_keys_rot.reshape(local_rows),
+            forward_values.reshape(local_rows),
+            segment,
         )
         forward_up_proj = (
             jnp.dot(forward_h_mlp, up_mat, preferred_element_type=jnp.float32) + up_add
@@ -296,41 +387,23 @@
         grad_up_add = jnp.sum(d_up.astype(jnp.float32), axis=0)
         backward_grad_up = contract_rows(h_mlp, d_up)
         d_hmlp = contract_cols(d_up, up_mat)
-        scores = (
-            jnp.einsum("qhd,khd->hqk", queries, keys_rot, preferred_element_type=jnp.float32)
-            * score_scale
-        )
-        scores = jnp.where(allowed_keys(segment)[None], scores, MASKED)
-        weights_soft = jnp.exp(scores - log_total)
-        d_context3 = d_context.reshape(block_len, local_heads, HD)
-        d_values = jnp.einsum(
-            "hqk,qhd->khd",
-            weights_soft.astype(jnp.bfloat16),
-            d_context3,
-            preferred_element_type=jnp.float32,
-        ).astype(jnp.bfloat16)
-        d_weights = jnp.einsum(
-            "qhd,khd->hqk", d_context3, values, preferred_element_type=jnp.float32
-        )
-        row_delta = jnp.sum(weights_soft * d_weights, axis=2, keepdims=True)
-        d_scores = (weights_soft * (d_weights - row_delta)).astype(jnp.bfloat16)
+        flat = (block_len, local_width)
+        d_queries, d_keys, d_values = attention_backward(
+            queries.reshape(flat),
+            keys_rot.reshape(flat),
+            values.reshape(flat),
+            d_context,
+            log_total,
+            segment,
+        )
+        heads_shape = (block_len, local_heads, HD)
         d_queries = (
-            jnp.einsum("hqk,khd->qhd", d_scores, keys_rot, preferred_element_type=jnp.float32)
-            * score_scale
+            rotate_back(d_queries.reshape(heads_shape), cosv, sinv).reshape(flat).astype(jnp.bfloat16)
         )
         d_keys = (
-            jnp.einsum("hqk,qhd->khd", d_scores, queries, preferred_element_type=jnp.float32)
-            * score_scale
-        )
-        d_queries = (
-            rotate_back(d_queries, cosv, sinv).reshape(block_len, local_width).astype(jnp.bfloat16)
-        )
-        d_keys = (
-            rotate_back(d_keys, cosv, sinv).reshape(block_len, local_width).astype(jnp.bfloat16)
-        )
-        d_joined = jnp.concatenate(
-            [d_queries, d_keys, d_values.reshape(block_len, local_width)], axis=1
-        )
+            rotate_back(d_keys.reshape(heads_shape), cosv, sinv).reshape(flat).astype(jnp.bfloat16)
+        )
+        d_joined = jnp.concatenate([d_queries, d_keys, d_values], axis=1)
         grad_joined_add = jnp.sum(d_joined.astype(jnp.float32), axis=0)
         backward_grad_joined = contract_rows(d_joined, h_attn)
         d_hattn = contract_cols(d_joined, joined_mat)

time: 568 us -> 658 us (1.16)
  other arithmetic: 57.4 us -> 97.3 us
  Pallas kernels: 0 us -> 32.4 us
  local copies, waits for them, and re-layouts: 80.3 us -> 109 us
  waiting for transfers between devices: 191 us -> 179 us
    pallas_call x0 -> x10, Pallas kernels: none -> 32.4 us  [the longest x5 16.9 us: attention_backward(): pl.pallas_call(_attention_backward_kernel, out_shape=(jax.ShapeDtypeStruc...]
    dot_general x35 -> x0, matrix products: 25.2 us -> none  [the longest x5 5.29 us: per_device(): jnp.einsum('qhd,khd->hqk', queries, keys_rot, preferred_element_type=jnp....]
    ppermute x33, waiting for transfers between devices: 55.3 us -> 36.9 us  [tensor_pieces(): parts.append(lax.ppermute(x, 'tensor', pairs))]
    select_n x18 -> x33, other arithmetic: 9.95 us -> 25.9 us  [pick(): jnp.where(leading, upper_val, lower_val)]
    pallas_call x0 -> x10, local copies, waits for them, and re-layouts: none -> 15.2 us  [attention_backward(): pl.pallas_call(_attention_backward_kernel, out_shape=(jax.ShapeDtypeStruc...]
    convert_element_type x5 -> x20, local copies, waits for them, and re-layouts: 6.36 us -> 20.9 us  [the longest x5 6.57 us: per_device(): rotate_back(d_queries.reshape(heads_shape), cosv, sinv).reshape(flat)]
    dot_general x20, matrix products: 23.8 us -> 37.9 us  [contract_cols(): lax.dot_general(left, right, (((1,), (1,)), ((), ())), preferred_element_...]
    slice x10, local copies, waits for them, and re-layouts: 0.1 us -> 12.1 us  [rotate_back(): heads_in[..., ROT:]]
  transfers between devices with their start and end apart: 42 -> 42, of which waited for: 18 -> 18; matrix products, arithmetic and copies ran while one was open for 24% -> 26% of each run, Pallas kernels for 0% -> 2%
where the time goes in v1:
time: 658 us; the launch traced here: 645 us
  waiting for transfers between devices  179 us (27%)
  matrix products  134 us (20%)
  local copies, waits for them, and re-layouts  109 us (17%)
  other arithmetic  97.3 us (15%)
  starting transfers between devices  76.4 us (12%)
  Pallas kernels  32.4 us (5%)
  between operations  17.4 us (3%)
    psum x1, waiting for transfers between devices, per_device(): slab = lax.psum(slab, 'dp').astype(jnp.float32)  111 us
    dot_general x20, matrix products, contract_rows(): lax.dot_general(left, right, (((0,), (0,)), ((), ())), preferred_element_...  61.2 us
    ppermute x33, starting transfers between devices, tensor_pieces(): parts.append(lax.ppermute(x, 'tensor', pairs))  55.9 us
    dot_general x20, matrix products, contract_cols(): lax.dot_general(left, right, (((1,), (1,)), ((), ())), preferred_element_...  37.9 us
    ppermute x33, waiting for transfers between devices, tensor_pieces(): parts.append(lax.ppermute(x, 'tensor', pairs))  36.9 us
    ppermute x8, waiting for transfers between devices, passed_along(): return lax.ppermute(x, axis, pairs)  31.2 us
    select_n x33, other arithmetic, pick(): jnp.where(leading, upper_val, lower_val)  25.9 us
    ppermute x8, starting transfers between devices, passed_along(): return lax.ppermute(x, axis, pairs)  20.4 us
  transfers between devices with their start and end apart: 42, of which 18 were waited for; matrix products, arithmetic and copies ran while one was open for 26% of the time, Pallas kernels for 2%

profile of v1, /device:TPU:0, one launch (start us, length us, event | category | flops | bytes accessed | tf_op | source)
XLA Modules:
  0.0 645.4 jit_solution(18440377154277070602)
XLA Ops:
  11.4 3.6 collective-permute-start.1
  32.3 5.7 collective-permute-done.1
  62.0 6.8 %collective-permute-done.4 = bf16[128,1024]{1,0:T(8,128)(2,1)S(1)} collective-permute-done((bf16[128,1024]{1,0:T(8,128)(2,1)S(1)}, bf16[128,1024]{1,0:T(8,128)(2,1)S(1)}, u32[]{:S(2)}, u32[]{:S(2)}) %collective-permute-start.4) | collective-permute-done | bytes 262176 | tf_op jit(solution)/shard_map/ppermute | solution.py:30
  70.1 4.9 collective-permute-start.6
  105.6 3.4 convert_reduce_fusion.14
  111.8 3.4 shard_map.208
  134.7 4.5 fusion.327
  147.7 6.0 collective-permute-start.10
  157.8 8.2 %collective-permute-done.25 = bf16[128,1024]{1,0:T(8,128)(2,1)S(1)} collective-permute-done((bf16[128,1024]{1,0:T(8,128)(2,1)S(1)}, bf16[128,1024]{1,0:T(8,128)(2,1)S(1)}, u32[]{:S(2)}, u32[]{:S(2)}) %collective-permute-start.25) | collective-permute-done | bytes 262176 | tf_op jit(solution)/shard_map/ppermute | solution.py:21
  188.7 3.3 fusion.98
  203.8 3.4 shard_map.209
  229.6 4.4 fusion.325
  254.9 4.0 collective-permute-done.29
  285.2 3.3 fusion.95
  300.5 3.4 shard_map.210
  320.1 4.4 fusion.323
  343.5 8.2 %collective-permute-done.33 = bf16[128,1024]{1,0:T(8,128)(2,1)S(1)} collective-permute-done((bf16[128,1024]{1,0:T(8,128)(2,1)S(1)}, bf16[128,1024]{1,0:T(8,128)(2,1)S(1)}, u32[]{:S(2)}, u32[]{:S(2)}) %collective-permute-start.33) | collective-permute-done | bytes 262176 | tf_op jit(solution)/shard_map/ppermute | solution.py:21
  381.2 3.7 convert_reduce_fusion.11
  387.1 3.4 shard_map.211
  410.1 4.4 fusion.321
  418.8 6.0 collective-permute-done.35
  428.6 8.3 %collective-permute-done.37 = bf16[128,1024]{1,0:T(8,128)(2,1)S(1)} collective-permute-done((bf16[128,1024]{1,0:T(8,128)(2,1)S(1)}, bf16[128,1024]{1,0:T(8,128)(2,1)S(1)}, u32[]{:S(2)}, u32[]{:S(2)}) %collective-permute-start.37) | collective-permute-done | bytes 262176 | tf_op jit(solution)/shard_map/ppermute | solution.py:21
  441.9 3.4 shard_map.212
  456.8 4.0 collective-permute-start.39
  461.2 6.9 %fusion.42 = bf16[3080,1024]{1,0:T(8,128)(2,1)} fusion(f32[768,1024]{1,0:T(8,128)} %fusion.339, f32[768,1024]{1,0:T(8,128)} %fusion.341, f32[768,1024]{1,0:T(8,128)} %fusion.345, f32[768,1024]{1,0:T(8,128)} %fusion.343, pred[]{:T(512)S(6)} %eq.77, bf16[128,256]{1,0:T(8,128)(2,1)S(1)} %copy-done.82, bf16[128,256]{1,0:T(8,128)(2,1)S(1)} %copy.182, ...), kind=kOutput, calls=%fused_computation.48 | convolution fusion | flops 207552512 | bytes 14886913 | tf_op jit(solution)/shard_map/dot_general | solution.py:114
  475.3 7.3 %fusion = bf16[3080,1024]{1,0:T(8,128)(2,1)} fusion(bf16[3080,1024]{1,0:T(8,128)(2,1)} %fusion.41, f32[1024,1024]{1,0:T(8,128)} %fusion.321, f32[1024,1024]{1,0:T(8,128)} %fusion.323, f32[1024,1024]{1,0:T(8,128)S(1)} %copy-done.229, f32[1024,1024]{1,0:T(8,128)} %fusion.325, pred[]{:T(512)S(6)} %eq.77, bf16[128,1024]{1,0:T(8,128)(2,1)S(1)} %collective-permute-done.37, ...), kind=kOutput, calls=%fused_computation.5 | convolution fusion | flops 290979840 | bytes 20186112 | tf_op jit(solution)/shard_map/dot_general | solution.py:114
  497.9 6.4 collective-permute-done.20
  508.8 110.9 %all-reduce.3.cloned.1.call-done = bf16[3080,1024]{1,0:T(8,128)(2,1)} async-done(((bf16[3080,1024]{1,0:T(8,128)(2,1)}), bf16[3080,1024]{1,0:T(8,128)(2,1)}) %all-reduce.3.cloned.1.call-update) | async-done | bytes 6307856 | tf_op jit(solution)/shard_map/psum | solution.py:448
  619.6 4.3 convert_element_type.644
  625.6 4.2 slice_bitcast_fusion
  630.5 3.4 slice.681
  633.9 3.5 copy.183
  (849 shorter events, 366.8 us)
Async XLA Ops:
  7.2 612.4 %all-reduce.3.cloned.1.call-start = ((), (), s32[]{:S(2)}) async-start(), calls=%async_computation | async-start | bytes 12615680 | tf_op jit(solution)/shard_map/psum | solution.py:448
  9.4 23.0 %collective-permute-start = (bf16[1024,256]{1,0:T(8,128)(2,1)S(1)}, bf16[1024,256]{1,0:T(8,128)(2,1)S(1)}, u32[]{:S(2)}, u32[]{:S(2)}) collective-permute-start(bf16[1024,256]{1,0:T(8,128)(2,1)S(1)} %constant_dynamic-update-slice_fusion), channel_id=1, source_target_pairs={{0,16},{16,32},{32,48},{48,0},{1,17},{17,33},{33,49},{49,1},{2,18}... | collective-permute-start | bytes 1572872 | tf_op jit(solution)/shard_map/ppermute | solution.py:30
  11.4 26.6 %collective-permute-start.1 = (bf16[1024,256]{1,0:T(8,128)(2,1)S(1)}, bf16[1024,256]{1,0:T(8,128)(2,1)}, u32[]{:S(2)}, u32[]{:S(2)}) collective-permute-start(bf16[1024,256]{1,0:T(8,128)(2,1)S(1)} %constant_dynamic-update-slice_fusion), channel_id=1, source_target_pairs={{0,32},{16,48},{32,0},{48,16},{1,33},{17,49},{33,1},{49,17},{2,34}... | collective-permute-start | bytes 1572872 | tf_op jit(solution)/shard_map/ppermute | solution.py:30
  15.0 23.0 %collective-permute-start.2 = (bf16[1024,256]{1,0:T(8,128)(2,1)S(1)}, bf16[1024,256]{1,0:T(8,128)(2,1)}, u32[]{:S(2)}, u32[]{:S(2)}) collective-permute-start(bf16[1024,256]{1,0:T(8,128)(2,1)S(1)} %constant_dynamic-update-slice_fusion), channel_id=1, source_target_pairs={{0,48},{16,0},{32,16},{48,32},{1,49},{17,1},{33,17},{49,33},{2,50}... | collective-permute-start | bytes 1572872 | tf_op jit(solution)/shard_map/ppermute | solution.py:30
  54.6 14.2 %collective-permute-start.4 = (bf16[128,1024]{1,0:T(8,128)(2,1)S(1)}, bf16[128,1024]{1,0:T(8,128)(2,1)S(1)}, u32[]{:S(2)}, u32[]{:S(2)}) collective-permute-start(bf16[128,1024]{1,0:T(8,128)(2,1)S(1)} %fusion.104), channel_id=1, source_target_pairs={{0,32},{16,48},{32,0},{48,16},{1,33},{17,49},{33,1},{49,17},{2,34}... | collective-permute-start | bytes 786440 | tf_op jit(solution)/shard_map/ppermute | solution.py:30
  57.0 11.8 %collective-permute-start.5 = (bf16[128,1024]{1,0:T(8,128)(2,1)S(1)}, bf16[128,1024]{1,0:T(8,128)(2,1)S(1)}, u32[]{:S(2)}, u32[]{:S(2)}) collective-permute-start(bf16[128,1024]{1,0:T(8,128)(2,1)S(1)} %fusion.104), channel_id=1, source_target_pairs={{0,48},{16,0},{32,16},{48,32},{1,49},{17,1},{33,17},{49,33},{2,50}... | collective-permute-start | bytes 786440 | tf_op jit(solution)/shard_map/ppermute | solution.py:30
  100.5 41.7 %collective-permute-start.7 = (bf16[128,1024]{1,0:T(8,128)(2,1)}, bf16[128,1024]{1,0:T(8,128)(2,1)}, u32[]{:S(2)}, u32[]{:S(2)}) collective-permute-start(bf16[128,1024]{1,0:T(8,128)(2,1)} %fusion.101), channel_id=1, source_target_pairs={{0,16},{16,32},{32,48},{48,0},{1,17},{17,33},{33,49},{49,1},{2,18}... | collective-permute-start | bytes 786440 | tf_op jit(solution)/shard_map/ppermute | solution.py:30
  102.8 42.8 %collective-permute-start.8 = (bf16[128,1024]{1,0:T(8,128)(2,1)}, bf16[128,1024]{1,0:T(8,128)(2,1)}, u32[]{:S(2)}, u32[]{:S(2)}) collective-permute-start(bf16[128,1024]{1,0:T(8,128)(2,1)} %fusion.101), channel_id=1, source_target_pairs={{0,32},{16,48},{32,0},{48,16},{1,33},{17,49},{33,1},{49,17},{2,34}... | collective-permute-start | bytes 786440 | tf_op jit(solution)/shard_map/ppermute | solution.py:30
  105.6 40.0 %collective-permute-start.9 = (bf16[128,1024]{1,0:T(8,128)(2,1)}, bf16[128,1024]{1,0:T(8,128)(2,1)}, u32[]{:S(2)}, u32[]{:S(2)}) collective-permute-start(bf16[128,1024]{1,0:T(8,128)(2,1)} %fusion.101), channel_id=1, source_target_pairs={{0,48},{16,0},{32,16},{48,32},{1,49},{17,1},{33,17},{49,33},{2,50}... | collective-permute-start | bytes 786440 | tf_op jit(solution)/shard_map/ppermute | solution.py:30
  128.9 25.0 %collective-permute-start.22 = (bf16[128,2048]{1,0:T(8,128)(2,1)S(1)}, bf16[128,2048]{1,0:T(8,128)(2,1)S(1)}, u32[]{:S(2)}, u32[]{:S(2)}) collective-permute-start(bf16[128,2048]{1,0:T(8,128)(2,1)S(1)} %pad_maximum_fusion.1), channel_id=1, source_target_pairs={{0,16},{16,32},{32,48},{48,0},{1,17},{17,33},{33,49},{49,1},{2,18}... | collective-permute-start | bytes 1572872 | tf_op jit(solution)/shard_map/ppermute | solution.py:30
  131.0 22.9 %collective-permute-start.23 = (bf16[128,2048]{1,0:T(8,128)(2,1)S(1)}, bf16[128,2048]{1,0:T(8,128)(2,1)S(1)}, u32[]{:S(2)}, u32[]{:S(2)}) collective-permute-start(bf16[128,2048]{1,0:T(8,128)(2,1)S(1)} %pad_maximum_fusion.1), channel_id=1, source_target_pairs={{0,32},{16,48},{32,0},{48,16},{1,33},{17,49},{33,1},{49,17},{2,34}... | collective-permute-start | bytes 1572872 | tf_op jit(solution)/shard_map/ppermute | solution.py:30
  142.2 12.3 %collective-permute-start.24 = (bf16[128,2048]{1,0:T(8,128)(2,1)S(1)}, bf16[128,2048]{1,0:T(8,128)(2,1)S(1)}, u32[]{:S(2)}, u32[]{:S(2)}) collective-permute-start(bf16[128,2048]{1,0:T(8,128)(2,1)S(1)} %pad_maximum_fusion.1), channel_id=1, source_target_pairs={{0,48},{16,0},{32,16},{48,32},{1,49},{17,1},{33,17},{49,33},{2,50}... | collective-permute-start | bytes 1572872 | tf_op jit(solution)/shard_map/ppermute | solution.py:30
  192.1 44.5 %collective-permute-start.11 = (bf16[128,1024]{1,0:T(8,128)(2,1)}, bf16[128,1024]{1,0:T(8,128)(2,1)}, u32[]{:S(2)}, u32[]{:S(2)}) collective-permute-start(bf16[128,1024]{1,0:T(8,128)(2,1)} %fusion.98), channel_id=1, source_target_pairs={{0,16},{16,32},{32,48},{48,0},{1,17},{17,33},{33,49},{49,1},{2,18}... | collective-permute-start | bytes 786440 | tf_op jit(solution)/shard_map/ppermute | solution.py:30
  193.6 46.6 %collective-permute-start.12 = (bf16[128,1024]{1,0:T(8,128)(2,1)}, bf16[128,1024]{1,0:T(8,128)(2,1)}, u32[]{:S(2)}, u32[]{:S(2)}) collective-permute-start(bf16[128,1024]{1,0:T(8,128)(2,1)} %fusion.98), channel_id=1, source_target_pairs={{0,32},{16,48},{32,0},{48,16},{1,33},{17,49},{33,1},{49,17},{2,34}... | collective-permute-start | bytes 786440 | tf_op jit(solution)/shard_map/ppermute | solution.py:30
  196.6 43.6 %collective-permute-start.13 = (bf16[128,1024]{1,0:T(8,128)(2,1)}, bf16[128,1024]{1,0:T(8,128)(2,1)}, u32[]{:S(2)}, u32[]{:S(2)}) collective-permute-start(bf16[128,1024]{1,0:T(8,128)(2,1)} %fusion.98), channel_id=1, source_target_pairs={{0,48},{16,0},{32,16},{48,32},{1,49},{17,1},{33,17},{49,33},{2,50}... | collective-permute-start | bytes 786440 | tf_op jit(solution)/shard_map/ppermute | solution.py:30
  224.0 21.9 %collective-permute-start.26 = (bf16[128,2048]{1,0:T(8,128)(2,1)S(1)}, bf16[128,2048]{1,0:T(8,128)(2,1)S(1)}, u32[]{:S(2)}, u32[]{:S(2)}) collective-permute-start(bf16[128,2048]{1,0:T(8,128)(2,1)S(1)} %pad_maximum_fusion.2), channel_id=1, source_target_pairs={{0,16},{16,32},{32,48},{48,0},{1,17},{17,33},{33,49},{49,1},{2,18}... | collective-permute-start | bytes 1572872 | tf_op jit(solution)/shard_map/ppermute | solution.py:30
  225.8 20.1 %collective-permute-start.27 = (bf16[128,2048]{1,0:T(8,128)(2,1)S(1)}, bf16[128,2048]{1,0:T(8,128)(2,1)S(1)}, u32[]{:S(2)}, u32[]{:S(2)}) collective-permute-start(bf16[128,2048]{1,0:T(8,128)(2,1)S(1)} %pad_maximum_fusion.2), channel_id=1, source_target_pairs={{0,32},{16,48},{32,0},{48,16},{1,33},{17,49},{33,1},{49,17},{2,34}... | collective-permute-start | bytes 1572872 | tf_op jit(solution)/shard_map/ppermute | solution.py:30
  242.5 11.9 %collective-permute-start.14 = (bf16[128,1024]{1,0:T(8,128)(2,1)S(1)}, bf16[128,1024]{1,0:T(8,128)(2,1)S(1)}, u32[]{:S(2)}, u32[]{:S(2)}) collective-permute-start(bf16[128,1024]{1,0:T(8,128)(2,1)S(1)} %get-tuple-element.194), channel_id=1, source_target_pairs={{0,64},{1,65},{2,66},{3,67},{4,68},{5,69},{6,70},{7,71},{8,72},{9,... | collective-permute-start | bytes 786440 | tf_op jit(solution)/shard_map/ppermute | solution.py:21
  288.5 39.0 %collective-permute-start.15 = (bf16[128,1024]{1,0:T(8,128)(2,1)}, bf16[128,1024]{1,0:T(8,128)(2,1)}, u32[]{:S(2)}, u32[]{:S(2)}) collective-permute-start(bf16[128,1024]{1,0:T(8,128)(2,1)} %fusion.95), channel_id=1, source_target_pairs={{0,16},{16,32},{32,48},{48,0},{1,17},{17,33},{33,49},{49,1},{2,18}... | collective-permute-start | bytes 786440 | tf_op jit(solution)/shard_map/ppermute | solution.py:30
  290.0 42.1 %collective-permute-start.16 = (bf16[128,1024]{1,0:T(8,128)(2,1)}, bf16[128,1024]{1,0:T(8,128)(2,1)}, u32[]{:S(2)}, u32[]{:S(2)}) collective-permute-start(bf16[128,1024]{1,0:T(8,128)(2,1)} %fusion.95), channel_id=1, source_target_pairs={{0,32},{16,48},{32,0},{48,16},{1,33},{17,49},{33,1},{49,17},{2,34}... | collective-permute-start | bytes 786440 | tf_op jit(solution)/shard_map/ppermute | solution.py:30
  293.0 39.1 %collective-permute-start.17 = (bf16[128,1024]{1,0:T(8,128)(2,1)}, bf16[128,1024]{1,0:T(8,128)(2,1)}, u32[]{:S(2)}, u32[]{:S(2)}) collective-permute-start(bf16[128,1024]{1,0:T(8,128)(2,1)} %fusion.95), channel_id=1, source_target_pairs={{0,48},{16,0},{32,16},{48,32},{1,49},{17,1},{33,17},{49,33},{2,50}... | collective-permute-start | bytes 786440 | tf_op jit(solution)/shard_map/ppermute | solution.py:30
  317.7 19.2 %collective-permute-start.30 = (bf16[128,2048]{1,0:T(8,128)(2,1)S(1)}, bf16[128,2048]{1,0:T(8,128)(2,1)S(1)}, u32[]{:S(2)}, u32[]{:S(2)}) collective-permute-start(bf16[128,2048]{1,0:T(8,128)(2,1)S(1)} %pad_maximum_fusion.3), channel_id=1, source_target_pairs={{0,16},{16,32},{32,48},{48,0},{1,17},{17,33},{33,49},{49,1},{2,18}... | collective-permute-start | bytes 1572872 | tf_op jit(solution)/shard_map/ppermute | solution.py:30
  319.5 17.4 %collective-permute-start.31 = (bf16[128,2048]{1,0:T(8,128)(2,1)S(1)}, bf16[128,2048]{1,0:T(8,128)(2,1)S(1)}, u32[]{:S(2)}, u32[]{:S(2)}) collective-permute-start(bf16[128,2048]{1,0:T(8,128)(2,1)S(1)} %pad_maximum_fusion.3), channel_id=1, source_target_pairs={{0,32},{16,48},{32,0},{48,16},{1,33},{17,49},{33,1},{49,17},{2,34}... | collective-permute-start | bytes 1572872 | tf_op jit(solution)/shard_map/ppermute | solution.py:30
  327.5 11.9 %collective-permute-start.32 = (bf16[128,2048]{1,0:T(8,128)(2,1)S(1)}, bf16[128,2048]{1,0:T(8,128)(2,1)S(1)}, u32[]{:S(2)}, u32[]{:S(2)}) collective-permute-start(bf16[128,2048]{1,0:T(8,128)(2,1)S(1)} %pad_maximum_fusion.3), channel_id=1, source_target_pairs={{0,48},{16,0},{32,16},{48,32},{1,49},{17,1},{33,17},{49,33},{2,50}... | collective-permute-start | bytes 1572872 | tf_op jit(solution)/shard_map/ppermute | solution.py:30
  402.0 16.8 %collective-permute-start.34 = (bf16[128,2048]{1,0:T(8,128)(2,1)S(1)}, bf16[128,2048]{1,0:T(8,128)(2,1)S(1)}, u32[]{:S(2)}, u32[]{:S(2)}) collective-permute-start(bf16[128,2048]{1,0:T(8,128)(2,1)S(1)} %pad_maximum_fusion.4), channel_id=1, source_target_pairs={{0,16},{16,32},{32,48},{48,0},{1,17},{17,33},{33,49},{49,1},{2,18}... | collective-permute-start | bytes 1572872 | tf_op jit(solution)/shard_map/ppermute | solution.py:30
  403.7 21.1 %collective-permute-start.35 = (bf16[128,2048]{1,0:T(8,128)(2,1)S(1)}, bf16[128,2048]{1,0:T(8,128)(2,1)S(1)}, u32[]{:S(2)}, u32[]{:S(2)}) collective-permute-start(bf16[128,2048]{1,0:T(8,128)(2,1)S(1)} %pad_maximum_fusion.4), channel_id=1, source_target_pairs={{0,32},{16,48},{32,0},{48,16},{1,33},{17,49},{33,1},{49,17},{2,34}... | collective-permute-start | bytes 1572872 | tf_op jit(solution)/shard_map/ppermute | solution.py:30
  407.1 17.8 %collective-permute-start.36 = (bf16[128,2048]{1,0:T(8,128)(2,1)S(1)}, bf16[128,2048]{1,0:T(8,128)(2,1)S(1)}, u32[]{:S(2)}, u32[]{:S(2)}) collective-permute-start(bf16[128,2048]{1,0:T(8,128)(2,1)S(1)} %pad_maximum_fusion.4), channel_id=1, source_target_pairs={{0,48},{16,0},{32,16},{48,32},{1,49},{17,1},{33,17},{49,33},{2,50}... | collective-permute-start | bytes 1572872 | tf_op jit(solution)/shard_map/ppermute | solution.py:30
  456.8 26.0 %collective-permute-start.38 = (bf16[128,2048]{1,0:T(8,128)(2,1)S(1)}, bf16[128,2048]{1,0:T(8,128)(2,1)S(1)}, u32[]{:S(2)}, u32[]{:S(2)}) collective-permute-start(bf16[128,2048]{1,0:T(8,128)(2,1)S(1)} %pad_maximum_fusion.5), channel_id=1, source_target_pairs={{0,16},{16,32},{32,48},{48,0},{1,17},{17,33},{33,49},{49,1},{2,18}... | collective-permute-start | bytes 1572872 | tf_op jit(solution)/shard_map/ppermute | solution.py:30
  456.8 25.9 %collective-permute-start.39 = (bf16[128,2048]{1,0:T(8,128)(2,1)S(1)}, bf16[128,2048]{1,0:T(8,128)(2,1)S(1)}, u32[]{:S(2)}, u32[]{:S(2)}) collective-permute-start(bf16[128,2048]{1,0:T(8,128)(2,1)S(1)} %pad_maximum_fusion.5), channel_id=1, source_target_pairs={{0,32},{16,48},{32,0},{48,16},{1,33},{17,49},{33,1},{49,17},{2,34}... | collective-permute-start | bytes 1572872 | tf_op jit(solution)/shard_map/ppermute | solution.py:30
  460.9 21.9 %collective-permute-start.40 = (bf16[128,2048]{1,0:T(8,128)(2,1)S(1)}, bf16[128,2048]{1,0:T(8,128)(2,1)S(1)}, u32[]{:S(2)}, u32[]{:S(2)}) collective-permute-start(bf16[128,2048]{1,0:T(8,128)(2,1)S(1)} %pad_maximum_fusion.5), channel_id=1, source_target_pairs={{0,48},{16,0},{32,16},{48,32},{1,49},{17,1},{33,17},{49,33},{2,50}... | collective-permute-start | bytes 1572872 | tf_op jit(solution)/shard_map/ppermute | solution.py:30
  491.8 12.5 %collective-permute-start.20 = (bf16[128,1024]{1,0:T(8,128)(2,1)}, bf16[128,1024]{1,0:T(8,128)(2,1)}, u32[]{:S(2)}, u32[]{:S(2)}) collective-permute-start(bf16[128,1024]{1,0:T(8,128)(2,1)} %fusion.92), channel_id=1, source_target_pairs={{0,32},{16,48},{32,0},{48,16},{1,33},{17,49},{33,1},{49,17},{2,34}... | collective-permute-start | bytes 786440 | tf_op jit(solution)/shard_map/ppermute | solution.py:30
  492.2 12.1 %collective-permute-start.21 = (bf16[128,1024]{1,0:T(8,128)(2,1)}, bf16[128,1024]{1,0:T(8,128)(2,1)}, u32[]{:S(2)}, u32[]{:S(2)}) collective-permute-start(bf16[128,1024]{1,0:T(8,128)(2,1)} %fusion.92), channel_id=1, source_target_pairs={{0,48},{16,0},{32,16},{48,32},{1,49},{17,1},{33,17},{49,33},{2,50}... | collective-permute-start | bytes 786440 | tf_op jit(solution)/shard_map/ppermute | solution.py:30
  (240 other events, 1847.5 us)
Sparse Core Ops, SparseCore 0:
  485.5 134.0 all-reduce.2

commit v2 on v0

--- a/solution.py
+++ b/solution.py
@@ -6,7 +6,7 @@
 HD = 64
 ROT = 16
 MB = 128
-NMB = 4
+NMB = 2
 
 
 EPSILON = 1e-05
@@ -104,8 +104,9 @@
 
 
 def allowed_keys(segment):
-    row_index = jnp.arange(segment.shape[0], dtype=jnp.int32)
-    return (segment[:, None] == segment[None, :]) & (row_index[None, :] <= row_index[:, None])
+    row_index = jnp.arange(segment.shape[-1], dtype=jnp.int32)
+    same = segment[..., :, None] == segment[..., None, :]
+    return same & (row_index[None, :] <= row_index[:, None])
 
 
 def contract_rows(left, right):
@@ -154,8 +155,13 @@
     gathered_rows = jnp.concatenate(gathered_pieces, axis=1)
     input_rows = gathered_rows[: tokens.shape[0]]
     output_grads = gathered_rows[tokens.shape[0] :]
+    tick_rows = tokens.shape[0] // NMB
+    sub_blocks = tick_rows // MB
     segment_all, place_all = positions(lengths, MB)
     cos_all, sin_all = rotary(place_all)
+    segment_all = segment_all.reshape(NMB, sub_blocks, MB)
+    cos_all = cos_all.reshape(NMB, tick_rows, cos_all.shape[-1])
+    sin_all = sin_all.reshape(NMB, tick_rows, sin_all.shape[-1])
 
     def pick(early_val, late_val):
         return jax.tree.map(
@@ -164,14 +170,14 @@
             late_val,
         )
 
-    received = jnp.zeros((MB, model_width), jnp.bfloat16)
+    received = jnp.zeros((tick_rows, model_width), jnp.bfloat16)
     tick_outputs = []
     tick_stored = []
     for section_tick in range(NMB + 1):
         early_block = min(section_tick, NMB - 1)
         late_block = max(section_tick - 1, 0)
         block_rows = jnp.where(
-            leading, input_rows[early_block * MB : (early_block + 1) * MB], received
+            leading, input_rows[early_block * tick_rows : (early_block + 1) * tick_rows], received
         )
         segment, cosv, sinv = pick(
             (segment_all[early_block], cos_all[early_block], sin_all[early_block]),
@@ -203,23 +209,27 @@
             .reshape(forward_block_len, local_heads, HD)
             .astype(jnp.bfloat16)
         )
+        blocked = (sub_blocks, MB, local_heads, HD)
         forward_scores = (
             jnp.einsum(
-                "qhd,khd->hqk",
-                forward_queries,
-                forward_keys_rot,
+                "bqhd,bkhd->bhqk",
+                forward_queries.reshape(blocked),
+                forward_keys_rot.reshape(blocked),
                 preferred_element_type=jnp.float32,
             )
             * score_scale
         )
-        forward_scores = jnp.where(allowed_keys(segment)[None], forward_scores, MASKED)
-        row_top = jnp.max(forward_scores, axis=2, keepdims=True)
+        forward_scores = jnp.where(allowed_keys(segment)[:, None], forward_scores, MASKED)
+        row_top = jnp.max(forward_scores, axis=3, keepdims=True)
         exponent = jnp.exp(forward_scores - row_top)
-        row_total = jnp.sum(exponent, axis=2, keepdims=True)
+        row_total = jnp.sum(exponent, axis=3, keepdims=True)
         forward_log_total = row_top + jnp.log(row_total)
         weights_low = (exponent / row_total).astype(jnp.bfloat16)
         forward_context = jnp.einsum(
-            "hqk,khd->qhd", weights_low, forward_values, preferred_element_type=jnp.float32
+            "bhqk,bkhd->bqhd",
+            weights_low,
+            forward_values.reshape(blocked),
+            preferred_element_type=jnp.float32,
         )
         forward_context = forward_context.reshape(forward_block_len, local_width).astype(
             jnp.bfloat16
@@ -259,14 +269,14 @@
         axis=0,
     )
     section_out = lax.dynamic_slice_in_dim(section_rows, column_start, quarter, 1)[None]
-    returned = jnp.zeros((MB, model_width), jnp.bfloat16)
+    returned = jnp.zeros((tick_rows, model_width), jnp.bfloat16)
     tick_grads = []
     totals = None
     for section_tick in range(NMB + 1):
         own_block = min(section_tick, NMB - 1)
         late_tick = max(section_tick - 1, 0)
         upper_tick = min(section_tick + 1, NMB)
-        from_output = output_grads[own_block * MB : (own_block + 1) * MB]
+        from_output = output_grads[own_block * tick_rows : (own_block + 1) * tick_rows]
         if section_tick == NMB:
             from_output = jnp.zeros_like(from_output)
         grad_rows = jnp.where(leading, returned, from_output)
@@ -296,32 +306,36 @@
         grad_up_add = jnp.sum(d_up.astype(jnp.float32), axis=0)
         backward_grad_up = contract_rows(h_mlp, d_up)
         d_hmlp = contract_cols(d_up, up_mat)
+        blocked = (sub_blocks, MB, local_heads, HD)
+        queries_b = queries.reshape(blocked)
+        keys_b = keys_rot.reshape(blocked)
         scores = (
-            jnp.einsum("qhd,khd->hqk", queries, keys_rot, preferred_element_type=jnp.float32)
+            jnp.einsum("bqhd,bkhd->bhqk", queries_b, keys_b, preferred_element_type=jnp.float32)
             * score_scale
         )
-        scores = jnp.where(allowed_keys(segment)[None], scores, MASKED)
+        scores = jnp.where(allowed_keys(segment)[:, None], scores, MASKED)
         weights_soft = jnp.exp(scores - log_total)
-        d_context3 = d_context.reshape(block_len, local_heads, HD)
+        d_context3 = d_context.reshape(blocked)
         d_values = jnp.einsum(
-            "hqk,qhd->khd",
+            "bhqk,bqhd->bkhd",
             weights_soft.astype(jnp.bfloat16),
             d_context3,
             preferred_element_type=jnp.float32,
         ).astype(jnp.bfloat16)
         d_weights = jnp.einsum(
-            "qhd,khd->hqk", d_context3, values, preferred_element_type=jnp.float32
-        )
-        row_delta = jnp.sum(weights_soft * d_weights, axis=2, keepdims=True)
+            "bqhd,bkhd->bhqk", d_context3, values.reshape(blocked), preferred_element_type=jnp.float32
+        )
+        row_delta = jnp.sum(weights_soft * d_weights, axis=3, keepdims=True)
         d_scores = (weights_soft * (d_weights - row_delta)).astype(jnp.bfloat16)
+        heads_shape = (block_len, local_heads, HD)
         d_queries = (
-            jnp.einsum("hqk,khd->qhd", d_scores, keys_rot, preferred_element_type=jnp.float32)
+            jnp.einsum("bhqk,bkhd->bqhd", d_scores, keys_b, preferred_element_type=jnp.float32)
             * score_scale
-        )
+        ).reshape(heads_shape)
         d_keys = (
-            jnp.einsum("hqk,qhd->khd", d_scores, queries, preferred_element_type=jnp.float32)
+            jnp.einsum("bhqk,bqhd->bkhd", d_scores, queries_b, preferred_element_type=jnp.float32)
             * score_scale
-        )
+        ).reshape(heads_shape)
         d_queries = (
             rotate_back(d_queries, cosv, sinv).reshape(block_len, local_width).astype(jnp.bfloat16)
         )

time: 568 us -> 549 us (0.967)
  waiting for transfers between devices: 191 us -> 287 us
  matrix products: 134 us -> 70.7 us
  starting transfers between devices: 76.1 us -> 51.5 us
  other arithmetic: 57.4 us -> 37.8 us
    ppermute x33 -> x21, waiting for transfers between devices: 55.3 us -> 162 us  [tensor_pieces(): parts.append(lax.ppermute(x, 'tensor', pairs))]
    dot_general x20 -> x12, matrix products: 56.5 us -> 21.8 us  [contract_rows(): lax.dot_general(left, right, (((0,), (0,)), ((), ())), preferred_element_...]
    ppermute x33 -> x21, starting transfers between devices: 55.7 us -> 36.4 us  [tensor_pieces(): parts.append(lax.ppermute(x, 'tensor', pairs))]
    dot_general x35 -> x21, matrix products: 25.2 us -> 10.3 us  [the longest x3 2.66 us: per_device(): jnp.einsum('bqhd,bkhd->bhqk', forward_queries.reshape(blocked), forward_k...]
    psum x1, waiting for transfers between devices: 110 us -> 98 us  [per_device(): slab = lax.psum(slab, 'dp').astype(jnp.float32)]
    slice x12 -> x2, local copies, waits for them, and re-layouts: 12.5 us -> 1.54 us  [the longest x1 0.77 us: per_device(): ln_gains[0]]
    reshape x0 -> x12, local copies, waits for them, and re-layouts: none -> 9.78 us  [the longest x6 9.66 us: per_device(): d_context3 = d_context.reshape(blocked)]
    select_n x18 -> x8, other arithmetic: 9.95 us -> 3 us  [pick(): jnp.where(leading, upper_val, lower_val)]
  transfers between devices with their start and end apart: 42 -> 26, of which waited for: 18 -> 16; matrix products, arithmetic and copies ran while one was open for 24% -> 11% of each run, Pallas kernels for 0% -> 0%
where the time goes in v2:
time: 549 us; the launch traced here: 540 us
  waiting for transfers between devices  287 us (52%)
  local copies, waits for them, and re-layouts  76.3 us (14%)
  matrix products  70.7 us (13%)
  starting transfers between devices  51.5 us (9%)
  other arithmetic  37.8 us (7%)
  between operations  16.7 us (3%)
    ppermute x21, waiting for transfers between devices, tensor_pieces(): parts.append(lax.ppermute(x, 'tensor', pairs))  162 us
    psum x1, waiting for transfers between devices, per_device(): slab = lax.psum(slab, 'dp').astype(jnp.float32)  98 us
    ppermute x21, starting transfers between devices, tensor_pieces(): parts.append(lax.ppermute(x, 'tensor', pairs))  36.4 us
    unnamed x336, local copies, waits for them, and re-layouts  29.6 us
    ppermute x4, waiting for transfers between devices, passed_along(): return lax.ppermute(x, axis, pairs)  26.9 us
    dot_general x12, matrix products, contract_rows(): lax.dot_general(left, right, (((0,), (0,)), ((), ())), preferred_element_...  21.8 us
    dot_general x12, matrix products, contract_cols(): lax.dot_general(left, right, (((1,), (1,)), ((), ())), preferred_element_...  18.4 us
    ppermute x4, starting transfers between devices, passed_along(): return lax.ppermute(x, axis, pairs)  15.1 us
  transfers between devices with their start and end apart: 26, of which 16 were waited for; matrix products, arithmetic and copies ran while one was open for 11% of the time, Pallas kernels for 0%

profile of v2, /device:TPU:0, one launch (start us, length us, event | category | flops | bytes accessed | tf_op | source)
XLA Modules:
  0.0 540.1 jit_solution(5994951020518459434)
XLA Ops:
  11.4 3.6 collective-permute-start.1
  25.5 12.5 %collective-permute-done.1 = bf16[1024,256]{1,0:T(8,128)(2,1)} collective-permute-done((bf16[1024,256]{1,0:T(8,128)(2,1)S(1)}, bf16[1024,256]{1,0:T(8,128)(2,1)}, u32[]{:S(2)}, u32[]{:S(2)}) %collective-permute-start.1) | collective-permute-done | bytes 524320 | tf_op jit(solution)/shard_map/ppermute | solution.py:28
  44.5 3.8 fusion.108
  54.9 9.4 %collective-permute-done.3 = bf16[256,1024]{1,0:T(8,128)(2,1)S(1)} collective-permute-done((bf16[256,1024]{1,0:T(8,128)(2,1)S(1)}, bf16[256,1024]{1,0:T(8,128)(2,1)S(1)}, u32[]{:S(2)}, u32[]{:S(2)}) %collective-permute-start.3) | collective-permute-done | bytes 524320 | tf_op jit(solution)/shard_map/ppermute | solution.py:28
  64.3 12.4 %collective-permute-done.4 = bf16[256,1024]{1,0:T(8,128)(2,1)S(1)} collective-permute-done((bf16[256,1024]{1,0:T(8,128)(2,1)S(1)}, bf16[256,1024]{1,0:T(8,128)(2,1)S(1)}, u32[]{:S(2)}, u32[]{:S(2)}) %collective-permute-start.4) | collective-permute-done | bytes 524320 | tf_op jit(solution)/shard_map/ppermute | solution.py:28
  77.3 6.2 %collective-permute-start.6 = (bf16[256,1024]{1,0:T(8,128)(2,1)S(1)}, bf16[256,1024]{1,0:T(8,128)(2,1)}, u32[]{:S(2)}, u32[]{:S(2)}) collective-permute-start(bf16[256,1024]{1,0:T(8,128)(2,1)S(1)} %fusion.105), channel_id=1, source_target_pairs={{0,64},{1,65},{2,66},{3,67},{4,68},{5,69},{6,70},{7,71},{8,72},{9,... | collective-permute-start | bytes 1572872 | tf_op jit(solution)/shard_map/ppermute | solution.py:19
  87.8 4.9 collective-permute-done.6
  94.9 3.8 fusion.113
  115.5 2.8 collective-permute-start.8
  121.3 4.4 convert_reduce_fusion.8
  136.3 3.1 fusion.198
  139.5 3.0 collective-permute-done.8
  143.9 6.2 %collective-permute-start.10 = (bf16[256,1024]{1,0:T(8,128)(2,1)S(1)}, bf16[256,1024]{1,0:T(8,128)(2,1)S(1)}, u32[]{:S(2)}, u32[]{:S(2)}) collective-permute-start(bf16[256,1024]{1,0:T(8,128)(2,1)S(1)} %get-tuple-element.81), channel_id=1, source_target_pairs={{0,64},{1,65},{2,66},{3,67},{4,68},{5,69},{6,70},{7,71},{8,72},{9,... | collective-permute-start | bytes 1572872 | tf_op jit(solution)/shard_map/ppermute | solution.py:19
  150.1 14.6 %collective-permute-done.14 = bf16[256,2048]{1,0:T(8,128)(2,1)S(1)} collective-permute-done((bf16[256,2048]{1,0:T(8,128)(2,1)S(1)}, bf16[256,2048]{1,0:T(8,128)(2,1)S(1)}, u32[]{:S(2)}, u32[]{:S(2)}) %collective-permute-start.14) | collective-permute-done | bytes 1048608 | tf_op jit(solution)/shard_map/ppermute | solution.py:28
  164.7 20.8 %collective-permute-done.15 = bf16[256,2048]{1,0:T(8,128)(2,1)S(1)} collective-permute-done((bf16[256,2048]{1,0:T(8,128)(2,1)S(1)}, bf16[256,2048]{1,0:T(8,128)(2,1)S(1)}, u32[]{:S(2)}, u32[]{:S(2)}) %collective-permute-start.15) | collective-permute-done | bytes 1048608 | tf_op jit(solution)/shard_map/ppermute | solution.py:28
  193.4 11.3 %collective-permute-done.17 = bf16[256,1024]{1,0:T(8,128)(2,1)S(1)} collective-permute-done((bf16[256,1024]{1,0:T(8,128)(2,1)S(1)}, bf16[256,1024]{1,0:T(8,128)(2,1)S(1)}, u32[]{:S(2)}, u32[]{:S(2)}) %collective-permute-start.17) | collective-permute-done | bytes 524320 | tf_op jit(solution)/shard_map/ppermute | solution.py:19
  207.3 3.9 fusion.118
  233.7 3.2 convert_reduce_fusion.7
  253.8 3.1 fusion.196
  256.9 9.8 %collective-permute-done.18 = bf16[256,2048]{1,0:T(8,128)(2,1)S(1)} collective-permute-done((bf16[256,2048]{1,0:T(8,128)(2,1)S(1)}, bf16[256,2048]{1,0:T(8,128)(2,1)S(1)}, u32[]{:S(2)}, u32[]{:S(2)}) %collective-permute-start.18) | collective-permute-done | bytes 1048608 | tf_op jit(solution)/shard_map/ppermute | solution.py:28
  266.7 23.3 %collective-permute-done.19 = bf16[256,2048]{1,0:T(8,128)(2,1)S(1)} collective-permute-done((bf16[256,2048]{1,0:T(8,128)(2,1)S(1)}, bf16[256,2048]{1,0:T(8,128)(2,1)S(1)}, u32[]{:S(2)}, u32[]{:S(2)}) %collective-permute-start.19) | collective-permute-done | bytes 1048608 | tf_op jit(solution)/shard_map/ppermute | solution.py:28
  299.4 10.6 %collective-permute-done.21 = bf16[256,1024]{1,0:T(8,128)(2,1)S(1)} collective-permute-done((bf16[256,1024]{1,0:T(8,128)(2,1)S(1)}, bf16[256,1024]{1,0:T(8,128)(2,1)S(1)}, u32[]{:S(2)}, u32[]{:S(2)}) %collective-permute-start.21) | collective-permute-done | bytes 524320 | tf_op jit(solution)/shard_map/ppermute | solution.py:19
  319.9 3.2 convert_reduce_fusion.6
  342.4 10.8 %collective-permute-done.22 = bf16[256,2048]{1,0:T(8,128)(2,1)S(1)} collective-permute-done((bf16[256,2048]{1,0:T(8,128)(2,1)S(1)}, bf16[256,2048]{1,0:T(8,128)(2,1)S(1)}, u32[]{:S(2)}, u32[]{:S(2)}) %collective-permute-start.22) | collective-permute-done | bytes 1048608 | tf_op jit(solution)/shard_map/ppermute | solution.py:28
  353.2 23.0 %collective-permute-done.23 = bf16[256,2048]{1,0:T(8,128)(2,1)S(1)} collective-permute-done((bf16[256,2048]{1,0:T(8,128)(2,1)S(1)}, bf16[256,2048]{1,0:T(8,128)(2,1)S(1)}, u32[]{:S(2)}, u32[]{:S(2)}) %collective-permute-start.23) | collective-permute-done | bytes 1048608 | tf_op jit(solution)/shard_map/ppermute | solution.py:28
  389.0 10.3 %collective-permute-done.11 = bf16[256,1024]{1,0:T(8,128)(2,1)} collective-permute-done((bf16[256,1024]{1,0:T(8,128)(2,1)}, bf16[256,1024]{1,0:T(8,128)(2,1)}, u32[]{:S(2)}, u32[]{:S(2)}) %collective-permute-start.11) | collective-permute-done | bytes 524320 | tf_op jit(solution)/shard_map/ppermute | solution.py:28
  399.2 12.4 %collective-permute-done.12 = bf16[256,1024]{1,0:T(8,128)(2,1)} collective-permute-done((bf16[256,1024]{1,0:T(8,128)(2,1)}, bf16[256,1024]{1,0:T(8,128)(2,1)}, u32[]{:S(2)}, u32[]{:S(2)}) %collective-permute-start.12) | collective-permute-done | bytes 524320 | tf_op jit(solution)/shard_map/ppermute | solution.py:28
  416.5 98.0 %all-reduce.3.cloned.1.call-done = bf16[3080,1024]{1,0:T(8,128)(2,1)} async-done(((bf16[3080,1024]{1,0:T(8,128)(2,1)}), bf16[3080,1024]{1,0:T(8,128)(2,1)}) %all-reduce.3.cloned.1.call-update) | async-done | bytes 6307856 | tf_op jit(solution)/shard_map/psum | solution.py:389
  514.5 4.3 convert_element_type.512
  520.5 4.2 slice_bitcast_fusion
  525.4 3.5 slice.437
  528.9 3.5 copy.198
  (562 shorter events, 173.3 us)
Async XLA Ops:
  7.2 37.1 %copy-start = (bf16[1,1024,1024]{2,1,0:T(8,128)(2,1)S(1)}, bf16[1,1024,1024]{2,1,0:T(8,128)(2,1)}, u32[]{:S(2)}) copy-start(bf16[1,1024,1024]{2,1,0:T(8,128)(2,1)} %param.19) | copy-start | bytes 6291460
  7.2 507.3 %all-reduce.3.cloned.1.call-start = ((), (), s32[]{:S(2)}) async-start(), calls=%async_computation | async-start | bytes 12615680 | tf_op jit(solution)/shard_map/psum | solution.py:389
  9.3 16.2 %collective-permute-start = (bf16[1024,256]{1,0:T(8,128)(2,1)S(1)}, bf16[1024,256]{1,0:T(8,128)(2,1)S(1)}, u32[]{:S(2)}, u32[]{:S(2)}) collective-permute-start(bf16[1024,256]{1,0:T(8,128)(2,1)S(1)} %constant_dynamic-update-slice_fusion), channel_id=1, source_target_pairs={{0,16},{16,32},{32,48},{48,0},{1,17},{17,33},{33,49},{49,1},{2,18}... | collective-permute-start | bytes 1572872 | tf_op jit(solution)/shard_map/ppermute | solution.py:28
  11.4 26.6 %collective-permute-start.1 = (bf16[1024,256]{1,0:T(8,128)(2,1)S(1)}, bf16[1024,256]{1,0:T(8,128)(2,1)}, u32[]{:S(2)}, u32[]{:S(2)}) collective-permute-start(bf16[1024,256]{1,0:T(8,128)(2,1)S(1)} %constant_dynamic-update-slice_fusion), channel_id=1, source_target_pairs={{0,32},{16,48},{32,0},{48,16},{1,33},{17,49},{33,1},{49,17},{2,34}... | collective-permute-start | bytes 1572872 | tf_op jit(solution)/shard_map/ppermute | solution.py:28
  15.0 23.0 %collective-permute-start.2 = (bf16[1024,256]{1,0:T(8,128)(2,1)S(1)}, bf16[1024,256]{1,0:T(8,128)(2,1)}, u32[]{:S(2)}, u32[]{:S(2)}) collective-permute-start(bf16[1024,256]{1,0:T(8,128)(2,1)S(1)} %constant_dynamic-update-slice_fusion), channel_id=1, source_target_pairs={{0,48},{16,0},{32,16},{48,32},{1,49},{17,1},{33,17},{49,33},{2,50}... | collective-permute-start | bytes 1572872 | tf_op jit(solution)/shard_map/ppermute | solution.py:28
  19.7 116.6 %copy-start.79 = (f32[1,1,1024]{2,1,0:T(1,128)}, f32[1,1,1024]{2,1,0:T(1,128)S(1)}, u32[]{:S(2)}) copy-start(f32[1,1,1024]{2,1,0:T(1,128)S(1)} %get-tuple-element.163) | copy-start | bytes 12292
  42.9 76.5 %copy-start.38 = (bf16[2,128,4,64]{1,3,2,0:T(8,128)(2,1)}, bf16[2,128,4,64]{1,3,2,0:T(8,128)(2,1)S(1)}, u32[]{:S(2)}) copy-start(bf16[2,128,4,64]{1,3,2,0:T(8,128)(2,1)S(1)} %bitcast_dynamic-update-slice_fusion.5) | copy-start | bytes 393220
  49.9 33.6 %copy-start.75 = (f32[4,128,8]{1,2,0:T(8,128)S(1)}, f32[4,128,8]{1,2,0:T(8,128)}, u32[]{:S(2)}) copy-start(f32[4,128,8]{1,2,0:T(8,128)} %copy-done.74) | copy-start | bytes 49156
  49.9 34.2 %copy-start.73 = (f32[4,128,8]{1,2,0:T(8,128)S(1)}, f32[4,128,8]{1,2,0:T(8,128)}, u32[]{:S(2)}) copy-start(f32[4,128,8]{1,2,0:T(8,128)} %copy-done.72) | copy-start | bytes 49156
  49.9 14.3 %collective-permute-start.3 = (bf16[256,1024]{1,0:T(8,128)(2,1)S(1)}, bf16[256,1024]{1,0:T(8,128)(2,1)S(1)}, u32[]{:S(2)}, u32[]{:S(2)}) collective-permute-start(bf16[256,1024]{1,0:T(8,128)(2,1)S(1)} %fusion.45), channel_id=1, source_target_pairs={{0,16},{16,32},{32,48},{48,0},{1,17},{17,33},{33,49},{49,1},{2,18}... | collective-permute-start | bytes 1572872 | tf_op jit(solution)/shard_map/ppermute | solution.py:28
  51.2 25.4 %collective-permute-start.4 = (bf16[256,1024]{1,0:T(8,128)(2,1)S(1)}, bf16[256,1024]{1,0:T(8,128)(2,1)S(1)}, u32[]{:S(2)}, u32[]{:S(2)}) collective-permute-start(bf16[256,1024]{1,0:T(8,128)(2,1)S(1)} %fusion.45), channel_id=1, source_target_pairs={{0,32},{16,48},{32,0},{48,16},{1,33},{17,49},{33,1},{49,17},{2,34}... | collective-permute-start | bytes 1572872 | tf_op jit(solution)/shard_map/ppermute | solution.py:28
  53.6 23.1 %collective-permute-start.5 = (bf16[256,1024]{1,0:T(8,128)(2,1)S(1)}, bf16[256,1024]{1,0:T(8,128)(2,1)S(1)}, u32[]{:S(2)}, u32[]{:S(2)}) collective-permute-start(bf16[256,1024]{1,0:T(8,128)(2,1)S(1)} %fusion.45), channel_id=1, source_target_pairs={{0,48},{16,0},{32,16},{48,32},{1,49},{17,1},{33,17},{49,33},{2,50}... | collective-permute-start | bytes 1572872 | tf_op jit(solution)/shard_map/ppermute | solution.py:28
  77.3 15.4 %collective-permute-start.6 = (bf16[256,1024]{1,0:T(8,128)(2,1)S(1)}, bf16[256,1024]{1,0:T(8,128)(2,1)}, u32[]{:S(2)}, u32[]{:S(2)}) collective-permute-start(bf16[256,1024]{1,0:T(8,128)(2,1)S(1)} %fusion.105), channel_id=1, source_target_pairs={{0,64},{1,65},{2,66},{3,67},{4,68},{5,69},{6,70},{7,71},{8,72},{9,... | collective-permute-start | bytes 1572872 | tf_op jit(solution)/shard_map/ppermute | solution.py:19
  113.8 17.6 %collective-permute-start.7 = (bf16[256,1024]{1,0:T(8,128)(2,1)S(1)}, bf16[256,1024]{1,0:T(8,128)(2,1)S(1)}, u32[]{:S(2)}, u32[]{:S(2)}) collective-permute-start(bf16[256,1024]{1,0:T(8,128)(2,1)S(1)} %fusion.46), channel_id=1, source_target_pairs={{0,16},{16,32},{32,48},{48,0},{1,17},{17,33},{33,49},{49,1},{2,18}... | collective-permute-start | bytes 1572872 | tf_op jit(solution)/shard_map/ppermute | solution.py:28
  115.5 26.9 %collective-permute-start.8 = (bf16[256,1024]{1,0:T(8,128)(2,1)S(1)}, bf16[256,1024]{1,0:T(8,128)(2,1)S(1)}, u32[]{:S(2)}, u32[]{:S(2)}) collective-permute-start(bf16[256,1024]{1,0:T(8,128)(2,1)S(1)} %fusion.46), channel_id=1, source_target_pairs={{0,32},{16,48},{32,0},{48,16},{1,33},{17,49},{33,1},{49,17},{2,34}... | collective-permute-start | bytes 1572872 | tf_op jit(solution)/shard_map/ppermute | solution.py:28
  118.3 24.1 %collective-permute-start.9 = (bf16[256,1024]{1,0:T(8,128)(2,1)S(1)}, bf16[256,1024]{1,0:T(8,128)(2,1)S(1)}, u32[]{:S(2)}, u32[]{:S(2)}) collective-permute-start(bf16[256,1024]{1,0:T(8,128)(2,1)S(1)} %fusion.46), channel_id=1, source_target_pairs={{0,48},{16,0},{32,16},{48,32},{1,49},{17,1},{33,17},{49,33},{2,50}... | collective-permute-start | bytes 1572872 | tf_op jit(solution)/shard_map/ppermute | solution.py:28
  128.5 36.1 %collective-permute-start.14 = (bf16[256,2048]{1,0:T(8,128)(2,1)S(1)}, bf16[256,2048]{1,0:T(8,128)(2,1)S(1)}, u32[]{:S(2)}, u32[]{:S(2)}) collective-permute-start(bf16[256,2048]{1,0:T(8,128)(2,1)S(1)} %pad_maximum_fusion.1), channel_id=1, source_target_pairs={{0,16},{16,32},{32,48},{48,0},{1,17},{17,33},{33,49},{49,1},{2,18}... | collective-permute-start | bytes 3145736 | tf_op jit(solution)/shard_map/ppermute | solution.py:28
  130.6 54.9 %collective-permute-start.15 = (bf16[256,2048]{1,0:T(8,128)(2,1)S(1)}, bf16[256,2048]{1,0:T(8,128)(2,1)S(1)}, u32[]{:S(2)}, u32[]{:S(2)}) collective-permute-start(bf16[256,2048]{1,0:T(8,128)(2,1)S(1)} %pad_maximum_fusion.1), channel_id=1, source_target_pairs={{0,32},{16,48},{32,0},{48,16},{1,33},{17,49},{33,1},{49,17},{2,34}... | collective-permute-start | bytes 3145736 | tf_op jit(solution)/shard_map/ppermute | solution.py:28
  131.4 54.2 %collective-permute-start.16 = (bf16[256,2048]{1,0:T(8,128)(2,1)S(1)}, bf16[256,2048]{1,0:T(8,128)(2,1)S(1)}, u32[]{:S(2)}, u32[]{:S(2)}) collective-permute-start(bf16[256,2048]{1,0:T(8,128)(2,1)S(1)} %pad_maximum_fusion.1), channel_id=1, source_target_pairs={{0,48},{16,0},{32,16},{48,32},{1,49},{17,1},{33,17},{49,33},{2,50}... | collective-permute-start | bytes 3145736 | tf_op jit(solution)/shard_map/ppermute | solution.py:28
  143.9 42.9 %copy-start.48 = (bf16[256,1024]{1,0:T(8,128)(2,1)}, bf16[256,1024]{1,0:T(8,128)(2,1)S(1)}, u32[]{:S(2)}) copy-start(bf16[256,1024]{1,0:T(8,128)(2,1)S(1)} %get-tuple-element.81) | copy-start | bytes 1572868
  143.9 49.5 %collective-permute-start.10 = (bf16[256,1024]{1,0:T(8,128)(2,1)S(1)}, bf16[256,1024]{1,0:T(8,128)(2,1)S(1)}, u32[]{:S(2)}, u32[]{:S(2)}) collective-permute-start(bf16[256,1024]{1,0:T(8,128)(2,1)S(1)} %get-tuple-element.81), channel_id=1, source_target_pairs={{0,64},{1,65},{2,66},{3,67},{4,68},{5,69},{6,70},{7,71},{8,72},{9,... | collective-permute-start | bytes 1572872 | tf_op jit(solution)/shard_map/ppermute | solution.py:19
  188.7 16.1 %collective-permute-start.17 = (bf16[256,1024]{1,0:T(8,128)(2,1)S(1)}, bf16[256,1024]{1,0:T(8,128)(2,1)S(1)}, u32[]{:S(2)}, u32[]{:S(2)}) collective-permute-start(bf16[256,1024]{1,0:T(8,128)(2,1)S(1)} %fusion.101), channel_id=1, source_target_pairs={{64,0},{65,1},{66,2},{67,3},{68,4},{69,5},{70,6},{71,7},{72,8},{73... | collective-permute-start | bytes 1572872 | tf_op jit(solution)/shard_map/ppermute | solution.py:19
  239.8 26.9 %collective-permute-start.18 = (bf16[256,2048]{1,0:T(8,128)(2,1)S(1)}, bf16[256,2048]{1,0:T(8,128)(2,1)S(1)}, u32[]{:S(2)}, u32[]{:S(2)}) collective-permute-start(bf16[256,2048]{1,0:T(8,128)(2,1)S(1)} %pad_maximum_fusion.2), channel_id=1, source_target_pairs={{0,16},{16,32},{32,48},{48,0},{1,17},{17,33},{33,49},{49,1},{2,18}... | collective-permute-start | bytes 3145736 | tf_op jit(solution)/shard_map/ppermute | solution.py:28
  242.2 47.8 %collective-permute-start.19 = (bf16[256,2048]{1,0:T(8,128)(2,1)S(1)}, bf16[256,2048]{1,0:T(8,128)(2,1)S(1)}, u32[]{:S(2)}, u32[]{:S(2)}) collective-permute-start(bf16[256,2048]{1,0:T(8,128)(2,1)S(1)} %pad_maximum_fusion.2), channel_id=1, source_target_pairs={{0,32},{16,48},{32,0},{48,16},{1,33},{17,49},{33,1},{49,17},{2,34}... | collective-permute-start | bytes 3145736 | tf_op jit(solution)/shard_map/ppermute | solution.py:28
  245.0 45.0 %collective-permute-start.20 = (bf16[256,2048]{1,0:T(8,128)(2,1)S(1)}, bf16[256,2048]{1,0:T(8,128)(2,1)S(1)}, u32[]{:S(2)}, u32[]{:S(2)}) collective-permute-start(bf16[256,2048]{1,0:T(8,128)(2,1)S(1)} %pad_maximum_fusion.2), channel_id=1, source_target_pairs={{0,48},{16,0},{32,16},{48,32},{1,49},{17,1},{33,17},{49,33},{2,50}... | collective-permute-start | bytes 3145736 | tf_op jit(solution)/shard_map/ppermute | solution.py:28
  294.1 15.9 %collective-permute-start.21 = (bf16[256,1024]{1,0:T(8,128)(2,1)S(1)}, bf16[256,1024]{1,0:T(8,128)(2,1)S(1)}, u32[]{:S(2)}, u32[]{:S(2)}) collective-permute-start(bf16[256,1024]{1,0:T(8,128)(2,1)S(1)} %get-tuple-element.75), channel_id=1, source_target_pairs={{64,0},{65,1},{66,2},{67,3},{68,4},{69,5},{70,6},{71,7},{72,8},{73... | collective-permute-start | bytes 1572872 | tf_op jit(solution)/shard_map/ppermute | solution.py:19
  326.2 27.1 %collective-permute-start.22 = (bf16[256,2048]{1,0:T(8,128)(2,1)S(1)}, bf16[256,2048]{1,0:T(8,128)(2,1)S(1)}, u32[]{:S(2)}, u32[]{:S(2)}) collective-permute-start(bf16[256,2048]{1,0:T(8,128)(2,1)S(1)} %pad_maximum_fusion.3), channel_id=1, source_target_pairs={{0,16},{16,32},{32,48},{48,0},{1,17},{17,33},{33,49},{49,1},{2,18}... | collective-permute-start | bytes 3145736 | tf_op jit(solution)/shard_map/ppermute | solution.py:28
  328.7 47.5 %collective-permute-start.23 = (bf16[256,2048]{1,0:T(8,128)(2,1)S(1)}, bf16[256,2048]{1,0:T(8,128)(2,1)S(1)}, u32[]{:S(2)}, u32[]{:S(2)}) collective-permute-start(bf16[256,2048]{1,0:T(8,128)(2,1)S(1)} %pad_maximum_fusion.3), channel_id=1, source_target_pairs={{0,32},{16,48},{32,0},{48,16},{1,33},{17,49},{33,1},{49,17},{2,34}... | collective-permute-start | bytes 3145736 | tf_op jit(solution)/shard_map/ppermute | solution.py:28
  331.5 44.7 %collective-permute-start.24 = (bf16[256,2048]{1,0:T(8,128)(2,1)S(1)}, bf16[256,2048]{1,0:T(8,128)(2,1)S(1)}, u32[]{:S(2)}, u32[]{:S(2)}) collective-permute-start(bf16[256,2048]{1,0:T(8,128)(2,1)S(1)} %pad_maximum_fusion.3), channel_id=1, source_target_pairs={{0,48},{16,0},{32,16},{48,32},{1,49},{17,1},{33,17},{49,33},{2,50}... | collective-permute-start | bytes 3145736 | tf_op jit(solution)/shard_map/ppermute | solution.py:28
  384.7 14.6 %collective-permute-start.11 = (bf16[256,1024]{1,0:T(8,128)(2,1)}, bf16[256,1024]{1,0:T(8,128)(2,1)}, u32[]{:S(2)}, u32[]{:S(2)}) collective-permute-start(bf16[256,1024]{1,0:T(8,128)(2,1)} %fusion.47), channel_id=1, source_target_pairs={{0,16},{16,32},{32,48},{48,0},{1,17},{17,33},{33,49},{49,1},{2,18}... | collective-permute-start | bytes 1572872 | tf_op jit(solution)/shard_map/ppermute | solution.py:28
  385.5 26.2 %collective-permute-start.12 = (bf16[256,1024]{1,0:T(8,128)(2,1)}, bf16[256,1024]{1,0:T(8,128)(2,1)}, u32[]{:S(2)}, u32[]{:S(2)}) collective-permute-start(bf16[256,1024]{1,0:T(8,128)(2,1)} %fusion.47), channel_id=1, source_target_pairs={{0,32},{16,48},{32,0},{48,16},{1,33},{17,49},{33,1},{49,17},{2,34}... | collective-permute-start | bytes 1572872 | tf_op jit(solution)/shard_map/ppermute | solution.py:28
  388.3 23.4 %collective-permute-start.13 = (bf16[256,1024]{1,0:T(8,128)(2,1)}, bf16[256,1024]{1,0:T(8,128)(2,1)}, u32[]{:S(2)}, u32[]{:S(2)}) collective-permute-start(bf16[256,1024]{1,0:T(8,128)(2,1)} %fusion.47), channel_id=1, source_target_pairs={{0,48},{16,0},{32,16},{48,32},{1,49},{17,1},{33,17},{49,33},{2,50}... | collective-permute-start | bytes 1572872 | tf_op jit(solution)/shard_map/ppermute | solution.py:28
  (142 other events, 876.6 us)
Sparse Core Ops, SparseCore 0:
  380.2 134.3 all-reduce.2

commit v3 on v2

--- a/solution.py
+++ b/solution.py
@@ -6,7 +6,7 @@
 HD = 64
 ROT = 16
 MB = 128
-NMB = 2
+NMB = 1
 
 
 EPSILON = 1e-05

time: 549 us -> 593 us (1.080)
  waiting for transfers between devices: 287 us -> 379 us
  local copies, waits for them, and re-layouts: 76.3 us -> 53.6 us
  starting transfers between devices: 51.5 us -> 34 us
  matrix products: 70.7 us -> 60.7 us
    ppermute x21 -> x15, waiting for transfers between devices: 162 us -> 272 us  [tensor_pieces(): parts.append(lax.ppermute(x, 'tensor', pairs))]
    psum x1, waiting for transfers between devices: 98 us -> 71.5 us  [per_device(): slab = lax.psum(slab, 'dp').astype(jnp.float32)]
    ppermute x21 -> x15, starting transfers between devices: 36.4 us -> 26 us  [tensor_pieces(): parts.append(lax.ppermute(x, 'tensor', pairs))]
    ppermute x4 -> x2, waiting for transfers between devices: 26.9 us -> 35.6 us  [passed_along(): return lax.ppermute(x, axis, pairs)]
    unnamed x336 -> x179, local copies, waits for them, and re-layouts: 29.6 us -> 21.4 us
    dot_general x12 -> x8, matrix products: 18.4 us -> 10.7 us  [contract_cols(): lax.dot_general(left, right, (((1,), (1,)), ((), ())), preferred_element_...]
    ppermute x4 -> x2, starting transfers between devices: 15.1 us -> 8 us  [passed_along(): return lax.ppermute(x, axis, pairs)]
    select_n x4 -> x0, other arithmetic: 6 us -> none  [the longest x2 3.73 us: per_device(): jnp.where(leading, tick_outputs[block], tick_outputs[block + 1])]
  transfers between devices with their start and end apart: 26 -> 18, of which waited for: 16 -> 13; matrix products, arithmetic and copies ran while one was open for 11% -> 7% of each run, Pallas kernels for 0% -> 0%
where the time goes in v3:
time: 593 us; the launch traced here: 583 us
  waiting for transfers between devices  379 us (64%)
  matrix products  60.7 us (10%)
  local copies, waits for them, and re-layouts  53.6 us (9%)
  other arithmetic  40 us (7%)
  starting transfers between devices  34 us (6%)
  between operations  15.8 us (3%)
    ppermute x15, waiting for transfers between devices, tensor_pieces(): parts.append(lax.ppermute(x, 'tensor', pairs))  272 us
    psum x1, waiting for transfers between devices, per_device(): slab = lax.psum(slab, 'dp').astype(jnp.float32)  71.5 us
    ppermute x2, waiting for transfers between devices, passed_along(): return lax.ppermute(x, axis, pairs)  35.6 us
    ppermute x15, starting transfers between devices, tensor_pieces(): parts.append(lax.ppermute(x, 'tensor', pairs))  26 us
    unnamed x179, local copies, waits for them, and re-layouts  21.4 us
    dot_general x8, matrix products, contract_rows(): lax.dot_general(left, right, (((0,), (0,)), ((), ())), preferred_element_...  17.1 us
    dot_general x2, matrix products, per_device(): jnp.dot(forward_h_mlp, up_mat, preferred_element_type=jnp.float32) + up_add  17 us
  transfers between devices with their start and end apart: 18, of which 13 were waited for; matrix products, arithmetic and copies ran while one was open for 7% of the time, Pallas kernels for 0%

profile of v3, /device:TPU:0, one launch (start us, length us, event | category | flops | bytes accessed | tf_op | source)
XLA Modules:
  0.0 583.2 jit_solution(12594263754653309011)
XLA Ops:
  11.4 3.6 collective-permute-start.1
  19.9 2.6 copy.87
  25.4 12.5 %collective-permute-done.1 = bf16[1024,256]{1,0:T(8,128)(2,1)} collective-permute-done((bf16[1024,256]{1,0:T(8,128)(2,1)S(1)}, bf16[1024,256]{1,0:T(8,128)(2,1)}, u32[]{:S(2)}, u32[]{:S(2)}) %collective-permute-start.1) | collective-permute-done | bytes 524320 | tf_op jit(solution)/shard_map/ppermute | solution.py:28
  51.2 6.8 %fusion.15 = (bf16[512,1024]{1,0:T(8,128)(2,1)S(1)}, f32[512,1024]{1,0:T(8,128)}) fusion(f32[1024]{0:T(1024)S(1)} %bitcast.309, bf16[1,1024,1024]{2,1,0:T(8,128)(2,1)S(1)} %copy-done, f32[1024]{0:T(1024)S(1)} %bitcast.312, f32[1024]{0:T(1024)S(1)} %bitcast.298, f32[512]{0:T(512)S(1)} %add_rsqrt_fusion.1, f32[512]{0:T(512)S(1)} %broadcast_multiply_fusion.5, ...), kind=kOutput, calls=%fused_computation.30 | convolution fusion | flops 1112014848 | bytes 6307841 | tf_op jit(solution)/shard_map/dot_general | solution.py:238
  64.9 20.6 %collective-permute-done.3 = bf16[512,1024]{1,0:T(8,128)(2,1)S(1)} collective-permute-done((bf16[512,1024]{1,0:T(8,128)(2,1)S(1)}, bf16[512,1024]{1,0:T(8,128)(2,1)S(1)}, u32[]{:S(2)}, u32[]{:S(2)}) %collective-permute-start.3) | collective-permute-done | bytes 1048608 | tf_op jit(solution)/shard_map/ppermute | solution.py:28
  85.5 23.6 %collective-permute-done.4 = bf16[512,1024]{1,0:T(8,128)(2,1)S(1)} collective-permute-done((bf16[512,1024]{1,0:T(8,128)(2,1)S(1)}, bf16[512,1024]{1,0:T(8,128)(2,1)S(1)}, u32[]{:S(2)}, u32[]{:S(2)}) %collective-permute-start.4) | collective-permute-done | bytes 1048608 | tf_op jit(solution)/shard_map/ppermute | solution.py:28
  111.2 6.4 %collective-permute-start.6 = (bf16[512,1024]{1,0:T(8,128)(2,1)}, bf16[512,1024]{1,0:T(8,128)(2,1)}, u32[]{:S(2)}, u32[]{:S(2)}) collective-permute-start(bf16[512,1024]{1,0:T(8,128)(2,1)} %fusion.12), channel_id=1, source_target_pairs={{0,64},{1,65},{2,66},{3,67},{4,68},{5,69},{6,70},{7,71},{8,72},{9,... | collective-permute-start | bytes 3145736 | tf_op jit(solution)/shard_map/ppermute | solution.py:19
  119.2 18.9 %collective-permute-done.6 = bf16[512,1024]{1,0:T(8,128)(2,1)} collective-permute-done((bf16[512,1024]{1,0:T(8,128)(2,1)}, bf16[512,1024]{1,0:T(8,128)(2,1)}, u32[]{:S(2)}, u32[]{:S(2)}) %collective-permute-start.6) | collective-permute-done | bytes 1048608 | tf_op jit(solution)/shard_map/ppermute | solution.py:19
  138.1 2.7 fusion.145
  159.8 10.2 %fusion.19 = (f32[512,1024]{1,0:T(8,128)S(1)}, f32[512,1024]{1,0:T(8,128)S(1)}, bf16[512,1024]{1,0:T(8,128)(2,1)S(1)}) fusion(f32[512,1024]{1,0:T(8,128)S(1)} %copy-done.74, f32[1024]{0:T(1024)S(1)} %bitcast.310, pred[]{:T(512)S(6)} %eq.64, bf16[1,1024,1024]{2,1,0:T(8,128)(2,1)S(1)} %copy-done, bf16[512,1024]{1,0:T(8,128)(2,1)S(1)} %copy-done.10, ...), kind=kOutput, calls=%fused_computation.34 | convolution fusion | flops 1145044992 | bytes 10502145 | tf_op jit(solution)/shard_map/dot_general | solution.py:238
  178.3 2.8 collective-permute-start.11
  181.7 3.2 fusion.100
  184.9 40.3 %collective-permute-done.10 = bf16[512,2048]{1,0:T(8,128)(2,1)S(1)} collective-permute-done((bf16[512,2048]{1,0:T(8,128)(2,1)S(1)}, bf16[512,2048]{1,0:T(8,128)(2,1)S(1)}, u32[]{:S(2)}, u32[]{:S(2)}) %collective-permute-start.10) | collective-permute-done | bytes 2097184 | tf_op jit(solution)/shard_map/ppermute | solution.py:28
  225.2 45.4 %collective-permute-done.11 = bf16[512,2048]{1,0:T(8,128)(2,1)S(1)} collective-permute-done((bf16[512,2048]{1,0:T(8,128)(2,1)S(1)}, bf16[512,2048]{1,0:T(8,128)(2,1)S(1)}, u32[]{:S(2)}, u32[]{:S(2)}) %collective-permute-start.11) | collective-permute-done | bytes 2097184 | tf_op jit(solution)/shard_map/ppermute | solution.py:28
  270.7 2.6 convert_add_fusion.1
  279.9 3.1 fusion.102
  283.0 4.0 fusion.101
  287.0 16.7 %collective-permute-done.13 = bf16[512,1024]{1,0:T(8,128)(2,1)S(1)} collective-permute-done((bf16[512,1024]{1,0:T(8,128)(2,1)S(1)}, bf16[512,1024]{1,0:T(8,128)(2,1)S(1)}, u32[]{:S(2)}, u32[]{:S(2)}) %collective-permute-start.13) | collective-permute-done | bytes 1048608 | tf_op jit(solution)/shard_map/ppermute | solution.py:19
  324.3 2.8 collective-permute-start.15
  334.8 36.5 %collective-permute-done.14 = bf16[512,2048]{1,0:T(8,128)(2,1)S(1)} collective-permute-done((bf16[512,2048]{1,0:T(8,128)(2,1)S(1)}, bf16[512,2048]{1,0:T(8,128)(2,1)S(1)}, u32[]{:S(2)}, u32[]{:S(2)}) %collective-permute-start.14) | collective-permute-done | bytes 2097184 | tf_op jit(solution)/shard_map/ppermute | solution.py:28
  371.3 45.4 %collective-permute-done.15 = bf16[512,2048]{1,0:T(8,128)(2,1)S(1)} collective-permute-done((bf16[512,2048]{1,0:T(8,128)(2,1)S(1)}, bf16[512,2048]{1,0:T(8,128)(2,1)S(1)}, u32[]{:S(2)}, u32[]{:S(2)}) %collective-permute-start.15) | collective-permute-done | bytes 2097184 | tf_op jit(solution)/shard_map/ppermute | solution.py:28
  416.7 2.6 convert_add_fusion
  419.4 2.7 slice_reduce_fusion
  424.0 3.2 fusion.24
  428.6 2.8 collective-permute-start.8
  432.1 21.3 %collective-permute-done.7 = bf16[512,1024]{1,0:T(8,128)(2,1)} collective-permute-done((bf16[512,1024]{1,0:T(8,128)(2,1)S(1)}, bf16[512,1024]{1,0:T(8,128)(2,1)}, u32[]{:S(2)}, u32[]{:S(2)}) %collective-permute-start.7) | collective-permute-done | bytes 1048608 | tf_op jit(solution)/shard_map/ppermute | solution.py:28
  453.4 23.6 %collective-permute-done.8 = bf16[512,1024]{1,0:T(8,128)(2,1)} collective-permute-done((bf16[512,1024]{1,0:T(8,128)(2,1)S(1)}, bf16[512,1024]{1,0:T(8,128)(2,1)}, u32[]{:S(2)}, u32[]{:S(2)}) %collective-permute-start.8) | collective-permute-done | bytes 1048608 | tf_op jit(solution)/shard_map/ppermute | solution.py:28
  486.2 71.5 %all-reduce.3.cloned.1.call-done = bf16[3080,1024]{1,0:T(8,128)(2,1)} async-done(((bf16[3080,1024]{1,0:T(8,128)(2,1)}), bf16[3080,1024]{1,0:T(8,128)(2,1)}) %all-reduce.3.cloned.1.call-update) | async-done | bytes 6307856 | tf_op jit(solution)/shard_map/psum | solution.py:389
  557.7 4.3 convert_element_type.366
  563.7 4.2 slice_bitcast_fusion
  568.5 3.5 slice.278
  572.1 3.5 copy.133
  (331 shorter events, 113.1 us)
Async XLA Ops:
  7.2 43.6 %copy-start = (bf16[1,1024,1024]{2,1,0:T(8,128)(2,1)S(1)}, bf16[1,1024,1024]{2,1,0:T(8,128)(2,1)}, u32[]{:S(2)}) copy-start(bf16[1,1024,1024]{2,1,0:T(8,128)(2,1)} %param.19) | copy-start | bytes 6291460
  7.2 15.3 %copy-start.57 = (bf16[1,3,256]{2,1,0:T(4,128)(2,1)S(1)}, bf16[1,3,256]{2,1,0:T(4,128)(2,1)}, u32[]{:S(2)}) copy-start(bf16[1,3,256]{2,1,0:T(4,128)(2,1)} %param.17) | copy-start | bytes 4612
  7.2 550.5 %all-reduce.3.cloned.1.call-start = ((), (), s32[]{:S(2)}) async-start(), calls=%async_computation | async-start | bytes 12615680 | tf_op jit(solution)/shard_map/psum | solution.py:389
  9.3 16.1 %collective-permute-start = (bf16[1024,256]{1,0:T(8,128)(2,1)S(1)}, bf16[1024,256]{1,0:T(8,128)(2,1)S(1)}, u32[]{:S(2)}, u32[]{:S(2)}) collective-permute-start(bf16[1024,256]{1,0:T(8,128)(2,1)S(1)} %constant_dynamic-update-slice_fusion), channel_id=1, source_target_pairs={{0,16},{16,32},{32,48},{48,0},{1,17},{17,33},{33,49},{49,1},{2,18}... | collective-permute-start | bytes 1572872 | tf_op jit(solution)/shard_map/ppermute | solution.py:28
  11.4 26.6 %collective-permute-start.1 = (bf16[1024,256]{1,0:T(8,128)(2,1)S(1)}, bf16[1024,256]{1,0:T(8,128)(2,1)}, u32[]{:S(2)}, u32[]{:S(2)}) collective-permute-start(bf16[1024,256]{1,0:T(8,128)(2,1)S(1)} %constant_dynamic-update-slice_fusion), channel_id=1, source_target_pairs={{0,32},{16,48},{32,0},{48,16},{1,33},{17,49},{33,1},{49,17},{2,34}... | collective-permute-start | bytes 1572872 | tf_op jit(solution)/shard_map/ppermute | solution.py:28
  15.0 23.0 %collective-permute-start.2 = (bf16[1024,256]{1,0:T(8,128)(2,1)S(1)}, bf16[1024,256]{1,0:T(8,128)(2,1)}, u32[]{:S(2)}, u32[]{:S(2)}) collective-permute-start(bf16[1024,256]{1,0:T(8,128)(2,1)S(1)} %constant_dynamic-update-slice_fusion), channel_id=1, source_target_pairs={{0,48},{16,0},{32,16},{48,32},{1,49},{17,1},{33,17},{49,33},{2,50}... | collective-permute-start | bytes 1572872 | tf_op jit(solution)/shard_map/ppermute | solution.py:28
  18.3 32.5 %copy-start.48 = (f32[1,1024]{1,0:T(1,128)}, f32[1,1024]{1,0:T(1,128)S(1)}, u32[]{:S(2)}) copy-start(f32[1,1024]{1,0:T(1,128)S(1)} %add.336) | copy-start | bytes 12292
  19.1 21.5 %copy-start.54 = (f32[1,1,1024]{2,1,0:T(1,128)}, f32[1,1,1024]{2,1,0:T(1,128)S(1)}, u32[]{:S(2)}) copy-start(f32[1,1,1024]{2,1,0:T(1,128)S(1)} %get-tuple-element.118) | copy-start | bytes 12292
  19.1 31.7 %copy-start.51 = (f32[1,1,1024]{2,1,0:T(1,128)}, f32[1,1,1024]{2,1,0:T(1,128)S(1)}, u32[]{:S(2)}) copy-start(f32[1,1,1024]{2,1,0:T(1,128)S(1)} %get-tuple-element.119) | copy-start | bytes 12292
  22.5 18.1 %copy-start.46 = (f32[768]{0:T(1024)}, f32[768]{0:T(1024)S(1)}, u32[]{:S(2)}) copy-start(f32[768]{0:T(1024)S(1)} %reshape.423) | copy-start | bytes 9220
  59.9 25.6 %collective-permute-start.3 = (bf16[512,1024]{1,0:T(8,128)(2,1)S(1)}, bf16[512,1024]{1,0:T(8,128)(2,1)S(1)}, u32[]{:S(2)}, u32[]{:S(2)}) collective-permute-start(bf16[512,1024]{1,0:T(8,128)(2,1)S(1)} %add_convert_fusion.8), channel_id=1, source_target_pairs={{0,16},{16,32},{32,48},{48,0},{1,17},{17,33},{33,49},{49,1},{2,18}... | collective-permute-start | bytes 3145736 | tf_op jit(solution)/shard_map/ppermute | solution.py:28
  61.2 47.9 %collective-permute-start.4 = (bf16[512,1024]{1,0:T(8,128)(2,1)S(1)}, bf16[512,1024]{1,0:T(8,128)(2,1)S(1)}, u32[]{:S(2)}, u32[]{:S(2)}) collective-permute-start(bf16[512,1024]{1,0:T(8,128)(2,1)S(1)} %add_convert_fusion.8), channel_id=1, source_target_pairs={{0,32},{16,48},{32,0},{48,16},{1,33},{17,49},{33,1},{49,17},{2,34}... | collective-permute-start | bytes 3145736 | tf_op jit(solution)/shard_map/ppermute | solution.py:28
  63.6 45.5 %collective-permute-start.5 = (bf16[512,1024]{1,0:T(8,128)(2,1)S(1)}, bf16[512,1024]{1,0:T(8,128)(2,1)S(1)}, u32[]{:S(2)}, u32[]{:S(2)}) collective-permute-start(bf16[512,1024]{1,0:T(8,128)(2,1)S(1)} %add_convert_fusion.8), channel_id=1, source_target_pairs={{0,48},{16,0},{32,16},{48,32},{1,49},{17,1},{33,17},{49,33},{2,50}... | collective-permute-start | bytes 3145736 | tf_op jit(solution)/shard_map/ppermute | solution.py:28
  111.2 27.0 %collective-permute-start.6 = (bf16[512,1024]{1,0:T(8,128)(2,1)}, bf16[512,1024]{1,0:T(8,128)(2,1)}, u32[]{:S(2)}, u32[]{:S(2)}) collective-permute-start(bf16[512,1024]{1,0:T(8,128)(2,1)} %fusion.12), channel_id=1, source_target_pairs={{0,64},{1,65},{2,66},{3,67},{4,68},{5,69},{6,70},{7,71},{8,72},{9,... | collective-permute-start | bytes 3145736 | tf_op jit(solution)/shard_map/ppermute | solution.py:19
  159.8 10.2 %copy-start.3 = (bf16[1024,1024]{1,0:T(8,128)(2,1)S(1)}, bf16[1024,1024]{1,0:T(8,128)(2,1)}, u32[]{:S(2)}) copy-start(bf16[1024,1024]{1,0:T(8,128)(2,1)} %copy-done.1) | copy-start | bytes 6291460
  159.8 10.2 %copy-start.59 = (bf16[1,1024,1024]{2,1,0:T(8,128)(2,1)S(1)}, bf16[1,1024,1024]{2,1,0:T(8,128)(2,1)}, u32[]{:S(2)}) copy-start(bf16[1,1024,1024]{2,1,0:T(8,128)(2,1)} %param.21) | copy-start | bytes 6291460
  170.0 11.6 %copy-start.65 = (bf16[512,1024]{1,0:T(8,128)(2,1)}, bf16[512,1024]{1,0:T(8,128)(2,1)S(1)}, u32[]{:S(2)}) copy-start(bf16[512,1024]{1,0:T(8,128)(2,1)S(1)} %get-tuple-element.83) | copy-start | bytes 3145732
  176.6 48.7 %collective-permute-start.10 = (bf16[512,2048]{1,0:T(8,128)(2,1)S(1)}, bf16[512,2048]{1,0:T(8,128)(2,1)S(1)}, u32[]{:S(2)}, u32[]{:S(2)}) collective-permute-start(bf16[512,2048]{1,0:T(8,128)(2,1)S(1)} %pad_maximum_fusion.1), channel_id=1, source_target_pairs={{0,16},{16,32},{32,48},{48,0},{1,17},{17,33},{33,49},{49,1},{2,18}... | collective-permute-start | bytes 6291464 | tf_op jit(solution)/shard_map/ppermute | solution.py:28
  178.3 92.4 %collective-permute-start.11 = (bf16[512,2048]{1,0:T(8,128)(2,1)S(1)}, bf16[512,2048]{1,0:T(8,128)(2,1)S(1)}, u32[]{:S(2)}, u32[]{:S(2)}) collective-permute-start(bf16[512,2048]{1,0:T(8,128)(2,1)S(1)} %pad_maximum_fusion.1), channel_id=1, source_target_pairs={{0,32},{16,48},{32,0},{48,16},{1,33},{17,49},{33,1},{49,17},{2,34}... | collective-permute-start | bytes 6291464 | tf_op jit(solution)/shard_map/ppermute | solution.py:28
  181.1 89.6 %collective-permute-start.12 = (bf16[512,2048]{1,0:T(8,128)(2,1)S(1)}, bf16[512,2048]{1,0:T(8,128)(2,1)S(1)}, u32[]{:S(2)}, u32[]{:S(2)}) collective-permute-start(bf16[512,2048]{1,0:T(8,128)(2,1)S(1)} %pad_maximum_fusion.1), channel_id=1, source_target_pairs={{0,48},{16,0},{32,16},{48,32},{1,49},{17,1},{33,17},{49,33},{2,50}... | collective-permute-start | bytes 6291464 | tf_op jit(solution)/shard_map/ppermute | solution.py:28
  181.6 96.6 %copy-start.37 = (bf16[4,128,4,64]{1,0,3,2:T(4,128)(2,1)}, bf16[4,128,4,64]{1,0,3,2:T(4,128)(2,1)S(1)}, u32[]{:S(2)}) copy-start(bf16[4,128,4,64]{1,0,3,2:T(4,128)(2,1)S(1)} %copy.132) | copy-start | bytes 786436
  184.9 88.4 %copy-start.45 = (f32[512]{0:T(512)S(1)}, f32[512]{0:T(512)}, u32[]{:S(2)}) copy-start(f32[512]{0:T(512)} %copy-done.44) | copy-start | bytes 6148
  276.6 27.1 %collective-permute-start.13 = (bf16[512,1024]{1,0:T(8,128)(2,1)S(1)}, bf16[512,1024]{1,0:T(8,128)(2,1)S(1)}, u32[]{:S(2)}, u32[]{:S(2)}) collective-permute-start(bf16[512,1024]{1,0:T(8,128)(2,1)S(1)} %fusion.10), channel_id=1, source_target_pairs={{64,0},{65,1},{66,2},{67,3},{68,4},{69,5},{70,6},{71,7},{72,8},{73... | collective-permute-start | bytes 3145736 | tf_op jit(solution)/shard_map/ppermute | solution.py:19
  283.0 21.7 %copy-start.24 = (bf16[1,256,1024]{2,1,0:T(8,128)(2,1)S(1)}, bf16[1,256,1024]{2,1,0:T(8,128)(2,1)}, u32[]{:S(2)}) copy-start(bf16[1,256,1024]{2,1,0:T(8,128)(2,1)} %param.18) | copy-start | bytes 1572868
  321.9 49.4 %collective-permute-start.14 = (bf16[512,2048]{1,0:T(8,128)(2,1)S(1)}, bf16[512,2048]{1,0:T(8,128)(2,1)S(1)}, u32[]{:S(2)}, u32[]{:S(2)}) collective-permute-start(bf16[512,2048]{1,0:T(8,128)(2,1)S(1)} %pad_maximum_fusion.2), channel_id=1, source_target_pairs={{0,16},{16,32},{32,48},{48,0},{1,17},{17,33},{33,49},{49,1},{2,18}... | collective-permute-start | bytes 6291464 | tf_op jit(solution)/shard_map/ppermute | solution.py:28
  324.3 92.4 %collective-permute-start.15 = (bf16[512,2048]{1,0:T(8,128)(2,1)S(1)}, bf16[512,2048]{1,0:T(8,128)(2,1)S(1)}, u32[]{:S(2)}, u32[]{:S(2)}) collective-permute-start(bf16[512,2048]{1,0:T(8,128)(2,1)S(1)} %pad_maximum_fusion.2), channel_id=1, source_target_pairs={{0,32},{16,48},{32,0},{48,16},{1,33},{17,49},{33,1},{49,17},{2,34}... | collective-permute-start | bytes 6291464 | tf_op jit(solution)/shard_map/ppermute | solution.py:28
  327.1 89.6 %collective-permute-start.16 = (bf16[512,2048]{1,0:T(8,128)(2,1)S(1)}, bf16[512,2048]{1,0:T(8,128)(2,1)S(1)}, u32[]{:S(2)}, u32[]{:S(2)}) collective-permute-start(bf16[512,2048]{1,0:T(8,128)(2,1)S(1)} %pad_maximum_fusion.2), channel_id=1, source_target_pairs={{0,48},{16,0},{32,16},{48,32},{1,49},{17,1},{33,17},{49,33},{2,50}... | collective-permute-start | bytes 6291464 | tf_op jit(solution)/shard_map/ppermute | solution.py:28
  334.8 82.0 %copy-start.12 = (bf16[3080,1024]{1,0:T(8,128)(2,1)}, bf16[3080,1024]{1,0:T(8,128)(2,1)S(1)}, u32[]{:S(2)}) copy-start(bf16[3080,1024]{1,0:T(8,128)(2,1)S(1)} %fusion.56) | copy-start | bytes 18923524
  334.8 84.6 %copy-start.8 = (f32[512,1024]{1,0:T(8,128)S(1)}, f32[512,1024]{1,0:T(8,128)}, u32[]{:S(2)}) copy-start(f32[512,1024]{1,0:T(8,128)} %copy-done.7) | copy-start | bytes 6291460
  427.7 25.6 %collective-permute-start.7 = (bf16[512,1024]{1,0:T(8,128)(2,1)S(1)}, bf16[512,1024]{1,0:T(8,128)(2,1)}, u32[]{:S(2)}, u32[]{:S(2)}) collective-permute-start(bf16[512,1024]{1,0:T(8,128)(2,1)S(1)} %add_convert_fusion.5), channel_id=1, source_target_pairs={{0,16},{16,32},{32,48},{48,0},{1,17},{17,33},{33,49},{49,1},{2,18}... | collective-permute-start | bytes 3145736 | tf_op jit(solution)/shard_map/ppermute | solution.py:28
  428.6 48.4 %collective-permute-start.8 = (bf16[512,1024]{1,0:T(8,128)(2,1)S(1)}, bf16[512,1024]{1,0:T(8,128)(2,1)}, u32[]{:S(2)}, u32[]{:S(2)}) collective-permute-start(bf16[512,1024]{1,0:T(8,128)(2,1)S(1)} %add_convert_fusion.5), channel_id=1, source_target_pairs={{0,32},{16,48},{32,0},{48,16},{1,33},{17,49},{33,1},{49,17},{2,34}... | collective-permute-start | bytes 3145736 | tf_op jit(solution)/shard_map/ppermute | solution.py:28
  431.4 45.6 %collective-permute-start.9 = (bf16[512,1024]{1,0:T(8,128)(2,1)S(1)}, bf16[512,1024]{1,0:T(8,128)(2,1)}, u32[]{:S(2)}, u32[]{:S(2)}) collective-permute-start(bf16[512,1024]{1,0:T(8,128)(2,1)S(1)} %add_convert_fusion.5), channel_id=1, source_target_pairs={{0,48},{16,0},{32,16},{48,32},{1,49},{17,1},{33,17},{49,33},{2,50}... | collective-permute-start | bytes 3145736 | tf_op jit(solution)/shard_map/ppermute | solution.py:28
  (61 other events, 172.2 us)
Sparse Core Ops, SparseCore 0:
  423.0 134.6 all-reduce.2

commit v4 on v2

--- a/solution.py
+++ b/solution.py
@@ -348,15 +348,11 @@
         grad_joined_add = jnp.sum(d_joined.astype(jnp.float32), axis=0)
         backward_grad_joined = contract_rows(d_joined, h_attn)
         d_hattn = contract_cols(d_joined, joined_mat)
-        d_both = tensor_sum(
-            jnp.concatenate([d_hattn, d_hmlp], axis=1).astype(jnp.bfloat16)
-        )
-        d_hattn, d_hmlp = d_both[:, :model_width], d_both[:, model_width:]
         grad_gains = jnp.concatenate(
             [jnp.sum(d_hattn * normed, axis=0), jnp.sum(d_hmlp * normed, axis=0)]
         )
         grad_shifts = jnp.concatenate([jnp.sum(d_hattn, axis=0), jnp.sum(d_hmlp, axis=0)])
-        d_norm = d_hattn * ln_gains[0] + d_hmlp * ln_gains[1]
+        d_norm = tensor_sum((d_hattn * ln_gains[0] + d_hmlp * ln_gains[1]).astype(jnp.bfloat16))
         grad_input = grad_wide + inv_scale * (
             d_norm
             - jnp.mean(d_norm, axis=1, keepdims=True)
@@ -402,11 +398,10 @@
     grad_up = summed[2][None]
     grad_down = summed[3][None]
     small_sum = summed[4].reshape(-1)
-    offset = 0
-    grad_ln_gain = small_sum[offset : offset + 2 * model_width].reshape(1, 2, model_width)
-    offset = offset + 2 * model_width
-    grad_ln_bias = small_sum[offset : offset + 2 * model_width].reshape(1, 2, model_width)
-    offset = offset + 2 * model_width
+    ln_sum = tensor_sum(small_sum[: 4 * model_width])
+    grad_ln_gain = ln_sum[: 2 * model_width].reshape(1, 2, model_width)
+    grad_ln_bias = ln_sum[2 * model_width :].reshape(1, 2, model_width)
+    offset = 4 * model_width
     grad_output_bias = small_sum[offset : offset + 2 * model_width].reshape(1, 2, model_width)
     offset = offset + 2 * model_width
     grad_joined_bias = small_sum[offset : offset + 3 * local_width].reshape(1, 3, local_width)

time: 549 us -> 485 us (0.88)
  waiting for transfers between devices: 287 us -> 219 us
    ppermute x21 -> x24, waiting for transfers between devices: 162 us -> 105 us  [tensor_pieces(): parts.append(lax.ppermute(x, 'tensor', pairs))]
    ppermute x4, waiting for transfers between devices: 26.9 us -> 16.8 us  [passed_along(): return lax.ppermute(x, axis, pairs)]
    ppermute x21 -> x24, starting transfers between devices: 36.4 us -> 40 us  [tensor_pieces(): parts.append(lax.ppermute(x, 'tensor', pairs))]
    unnamed x336 -> x337, local copies, waits for them, and re-layouts: 29.6 us -> 29.9 us
  transfers between devices with their start and end apart: 26 -> 29, of which waited for: 16 -> 17; matrix products, arithmetic and copies ran while one was open for 11% -> 17% of each run, Pallas kernels for 0% -> 0%
where the time goes in v4:
time: 485 us; the launch traced here: 476 us
  waiting for transfers between devices  219 us (45%)
  local copies, waits for them, and re-layouts  78.4 us (16%)
  matrix products  70.6 us (15%)
  starting transfers between devices  54.9 us (11%)
  other arithmetic  36 us (7%)
  between operations  16.7 us (3%)
    ppermute x24, waiting for transfers between devices, tensor_pieces(): parts.append(lax.ppermute(x, 'tensor', pairs))  105 us
    psum x1, waiting for transfers between devices, per_device(): slab = lax.psum(slab, 'dp').astype(jnp.float32)  98 us
    ppermute x24, starting transfers between devices, tensor_pieces(): parts.append(lax.ppermute(x, 'tensor', pairs))  40 us
    unnamed x337, local copies, waits for them, and re-layouts  29.9 us
    dot_general x12, matrix products, contract_rows(): lax.dot_general(left, right, (((0,), (0,)), ((), ())), preferred_element_...  21.7 us
    dot_general x12, matrix products, contract_cols(): lax.dot_general(left, right, (((1,), (1,)), ((), ())), preferred_element_...  18.4 us
    ppermute x4, waiting for transfers between devices, passed_along(): return lax.ppermute(x, axis, pairs)  16.8 us
    ppermute x4, starting transfers between devices, passed_along(): return lax.ppermute(x, axis, pairs)  14.8 us
  transfers between devices with their start and end apart: 29, of which 17 were waited for; matrix products, arithmetic and copies ran while one was open for 17% of the time, Pallas kernels for 0%

profile of v4, /device:TPU:0, one launch (start us, length us, event | category | flops | bytes accessed | tf_op | source)
XLA Modules:
  0.0 476.0 jit_solution(2134331682735722926)
XLA Ops:
  11.4 3.6 collective-permute-start.1
  25.5 12.5 %collective-permute-done.1 = bf16[1024,256]{1,0:T(8,128)(2,1)} collective-permute-done((bf16[1024,256]{1,0:T(8,128)(2,1)S(1)}, bf16[1024,256]{1,0:T(8,128)(2,1)}, u32[]{:S(2)}, u32[]{:S(2)}) %collective-permute-start.1) | collective-permute-done | bytes 524320 | tf_op jit(solution)/shard_map/ppermute | solution.py:28
  44.7 3.8 fusion.99
  55.0 9.4 %collective-permute-done.3 = bf16[256,1024]{1,0:T(8,128)(2,1)S(1)} collective-permute-done((bf16[256,1024]{1,0:T(8,128)(2,1)S(1)}, bf16[256,1024]{1,0:T(8,128)(2,1)S(1)}, u32[]{:S(2)}, u32[]{:S(2)}) %collective-permute-start.3) | collective-permute-done | bytes 524320 | tf_op jit(solution)/shard_map/ppermute | solution.py:28
  64.4 12.4 %collective-permute-done.4 = bf16[256,1024]{1,0:T(8,128)(2,1)S(1)} collective-permute-done((bf16[256,1024]{1,0:T(8,128)(2,1)S(1)}, bf16[256,1024]{1,0:T(8,128)(2,1)S(1)}, u32[]{:S(2)}, u32[]{:S(2)}) %collective-permute-start.4) | collective-permute-done | bytes 524320 | tf_op jit(solution)/shard_map/ppermute | solution.py:28
  77.4 5.9 %collective-permute-start.6 = (bf16[256,1024]{1,0:T(8,128)(2,1)S(1)}, bf16[256,1024]{1,0:T(8,128)(2,1)}, u32[]{:S(2)}, u32[]{:S(2)}) collective-permute-start(bf16[256,1024]{1,0:T(8,128)(2,1)S(1)} %fusion.96), channel_id=1, source_target_pairs={{0,64},{1,65},{2,66},{3,67},{4,68},{5,69},{6,70},{7,71},{8,72},{9,... | collective-permute-start | bytes 1572872 | tf_op jit(solution)/shard_map/ppermute | solution.py:19
  87.0 5.9 %collective-permute-done.6 = bf16[256,1024]{1,0:T(8,128)(2,1)} collective-permute-done((bf16[256,1024]{1,0:T(8,128)(2,1)S(1)}, bf16[256,1024]{1,0:T(8,128)(2,1)}, u32[]{:S(2)}, u32[]{:S(2)}) %collective-permute-start.6) | collective-permute-done | bytes 524320 | tf_op jit(solution)/shard_map/ppermute | solution.py:19
  95.0 3.8 fusion.104
  121.9 4.4 convert_reduce_fusion.8
  134.4 3.1 fusion.189
  137.5 15.2 %collective-permute-done.14 = bf16[256,1024]{1,0:T(8,128)(2,1)S(1)} collective-permute-done((bf16[256,1024]{1,0:T(8,128)(2,1)S(1)}, bf16[256,1024]{1,0:T(8,128)(2,1)S(1)}, u32[]{:S(2)}, u32[]{:S(2)}) %collective-permute-start.14) | collective-permute-done | bytes 524320 | tf_op jit(solution)/shard_map/ppermute | solution.py:28
  154.4 8.8 %collective-permute-done.15 = bf16[256,1024]{1,0:T(8,128)(2,1)S(1)} collective-permute-done((bf16[256,1024]{1,0:T(8,128)(2,1)S(1)}, bf16[256,1024]{1,0:T(8,128)(2,1)S(1)}, u32[]{:S(2)}, u32[]{:S(2)}) %collective-permute-start.15) | collective-permute-done | bytes 524320 | tf_op jit(solution)/shard_map/ppermute | solution.py:28
  168.5 6.2 %collective-permute-start.10 = (bf16[256,1024]{1,0:T(8,128)(2,1)S(1)}, bf16[256,1024]{1,0:T(8,128)(2,1)S(1)}, u32[]{:S(2)}, u32[]{:S(2)}) collective-permute-start(bf16[256,1024]{1,0:T(8,128)(2,1)S(1)} %get-tuple-element.73), channel_id=1, source_target_pairs={{0,64},{1,65},{2,66},{3,67},{4,68},{5,69},{6,70},{7,71},{8,72},{9,... | collective-permute-start | bytes 1572872 | tf_op jit(solution)/shard_map/ppermute | solution.py:19
  178.1 3.4 collective-permute-done.17
  186.9 3.9 fusion.109
  213.7 3.2 convert_reduce_fusion.7
  225.9 2.8 fusion.182
  230.9 3.1 fusion.187
  234.1 8.1 %collective-permute-done.18 = bf16[256,1024]{1,0:T(8,128)(2,1)S(1)} collective-permute-done((bf16[256,1024]{1,0:T(8,128)(2,1)S(1)}, bf16[256,1024]{1,0:T(8,128)(2,1)S(1)}, u32[]{:S(2)}, u32[]{:S(2)}) %collective-permute-start.18) | collective-permute-done | bytes 524320 | tf_op jit(solution)/shard_map/ppermute | solution.py:28
  257.5 4.8 %collective-permute-done.21 = bf16[256,1024]{1,0:T(8,128)(2,1)S(1)} collective-permute-done((bf16[256,1024]{1,0:T(8,128)(2,1)S(1)}, bf16[256,1024]{1,0:T(8,128)(2,1)S(1)}, u32[]{:S(2)}, u32[]{:S(2)}) %collective-permute-start.21) | collective-permute-done | bytes 524320 | tf_op jit(solution)/shard_map/ppermute | solution.py:19
  273.6 3.2 convert_reduce_fusion.6
  279.3 3.6 collective-permute-start.23
  293.3 11.7 %collective-permute-done.23 = bf16[256,1024]{1,0:T(8,128)(2,1)S(1)} collective-permute-done((bf16[256,1024]{1,0:T(8,128)(2,1)S(1)}, bf16[256,1024]{1,0:T(8,128)(2,1)S(1)}, u32[]{:S(2)}, u32[]{:S(2)}) %collective-permute-start.23) | collective-permute-done | bytes 524320 | tf_op jit(solution)/shard_map/ppermute | solution.py:28
  313.7 3.4 collective-permute-start.12
  317.2 10.9 %collective-permute-done.11 = bf16[256,1024]{1,0:T(8,128)(2,1)} collective-permute-done((bf16[256,1024]{1,0:T(8,128)(2,1)}, bf16[256,1024]{1,0:T(8,128)(2,1)}, u32[]{:S(2)}, u32[]{:S(2)}) %collective-permute-start.11) | collective-permute-done | bytes 524320 | tf_op jit(solution)/shard_map/ppermute | solution.py:28
  328.1 12.4 %collective-permute-done.12 = bf16[256,1024]{1,0:T(8,128)(2,1)} collective-permute-done((bf16[256,1024]{1,0:T(8,128)(2,1)}, bf16[256,1024]{1,0:T(8,128)(2,1)}, u32[]{:S(2)}, u32[]{:S(2)}) %collective-permute-start.12) | collective-permute-done | bytes 524320 | tf_op jit(solution)/shard_map/ppermute | solution.py:28
  345.4 98.0 %all-reduce.3.cloned.1.call-done = bf16[3080,1024]{1,0:T(8,128)(2,1)} async-done(((bf16[3080,1024]{1,0:T(8,128)(2,1)}), bf16[3080,1024]{1,0:T(8,128)(2,1)}) %all-reduce.3.cloned.1.call-update) | async-done | bytes 6307856 | tf_op jit(solution)/shard_map/psum | solution.py:385
  443.3 4.3 convert_element_type.521
  449.3 2.9 collective-permute-start.26
  454.6 4.2 slice_bitcast_fusion
  460.0 3.5 slice.435
  463.5 3.5 copy.198
  (566 shorter events, 173.2 us)
Async XLA Ops:
  7.2 37.3 %copy-start = (bf16[1,1024,1024]{2,1,0:T(8,128)(2,1)S(1)}, bf16[1,1024,1024]{2,1,0:T(8,128)(2,1)}, u32[]{:S(2)}) copy-start(bf16[1,1024,1024]{2,1,0:T(8,128)(2,1)} %param.19) | copy-start | bytes 6291460
  7.2 436.1 %all-reduce.3.cloned.1.call-start = ((), (), s32[]{:S(2)}) async-start(), calls=%async_computation | async-start | bytes 12615680 | tf_op jit(solution)/shard_map/psum | solution.py:385
  9.3 16.1 %collective-permute-start = (bf16[1024,256]{1,0:T(8,128)(2,1)S(1)}, bf16[1024,256]{1,0:T(8,128)(2,1)S(1)}, u32[]{:S(2)}, u32[]{:S(2)}) collective-permute-start(bf16[1024,256]{1,0:T(8,128)(2,1)S(1)} %constant_dynamic-update-slice_fusion), channel_id=1, source_target_pairs={{0,16},{16,32},{32,48},{48,0},{1,17},{17,33},{33,49},{49,1},{2,18}... | collective-permute-start | bytes 1572872 | tf_op jit(solution)/shard_map/ppermute | solution.py:28
  11.4 26.6 %collective-permute-start.1 = (bf16[1024,256]{1,0:T(8,128)(2,1)S(1)}, bf16[1024,256]{1,0:T(8,128)(2,1)}, u32[]{:S(2)}, u32[]{:S(2)}) collective-permute-start(bf16[1024,256]{1,0:T(8,128)(2,1)S(1)} %constant_dynamic-update-slice_fusion), channel_id=1, source_target_pairs={{0,32},{16,48},{32,0},{48,16},{1,33},{17,49},{33,1},{49,17},{2,34}... | collective-permute-start | bytes 1572872 | tf_op jit(solution)/shard_map/ppermute | solution.py:28
  15.0 23.0 %collective-permute-start.2 = (bf16[1024,256]{1,0:T(8,128)(2,1)S(1)}, bf16[1024,256]{1,0:T(8,128)(2,1)}, u32[]{:S(2)}, u32[]{:S(2)}) collective-permute-start(bf16[1024,256]{1,0:T(8,128)(2,1)S(1)} %constant_dynamic-update-slice_fusion), channel_id=1, source_target_pairs={{0,48},{16,0},{32,16},{48,32},{1,49},{17,1},{33,17},{49,33},{2,50}... | collective-permute-start | bytes 1572872 | tf_op jit(solution)/shard_map/ppermute | solution.py:28
  19.7 114.7 %copy-start.80 = (f32[1,1,1024]{2,1,0:T(1,128)}, f32[1,1,1024]{2,1,0:T(1,128)S(1)}, u32[]{:S(2)}) copy-start(f32[1,1,1024]{2,1,0:T(1,128)S(1)} %get-tuple-element.154) | copy-start | bytes 12292
  43.1 76.5 %copy-start.38 = (bf16[2,128,4,64]{1,3,2,0:T(8,128)(2,1)}, bf16[2,128,4,64]{1,3,2,0:T(8,128)(2,1)S(1)}, u32[]{:S(2)}) copy-start(bf16[2,128,4,64]{1,3,2,0:T(8,128)(2,1)S(1)} %bitcast_dynamic-update-slice_fusion.5) | copy-start | bytes 393220
  50.1 14.3 %collective-permute-start.3 = (bf16[256,1024]{1,0:T(8,128)(2,1)S(1)}, bf16[256,1024]{1,0:T(8,128)(2,1)S(1)}, u32[]{:S(2)}, u32[]{:S(2)}) collective-permute-start(bf16[256,1024]{1,0:T(8,128)(2,1)S(1)} %fusion.36), channel_id=1, source_target_pairs={{0,16},{16,32},{32,48},{48,0},{1,17},{17,33},{33,49},{49,1},{2,18}... | collective-permute-start | bytes 1572872 | tf_op jit(solution)/shard_map/ppermute | solution.py:28
  51.4 25.4 %collective-permute-start.4 = (bf16[256,1024]{1,0:T(8,128)(2,1)S(1)}, bf16[256,1024]{1,0:T(8,128)(2,1)S(1)}, u32[]{:S(2)}, u32[]{:S(2)}) collective-permute-start(bf16[256,1024]{1,0:T(8,128)(2,1)S(1)} %fusion.36), channel_id=1, source_target_pairs={{0,32},{16,48},{32,0},{48,16},{1,33},{17,49},{33,1},{49,17},{2,34}... | collective-permute-start | bytes 1572872 | tf_op jit(solution)/shard_map/ppermute | solution.py:28
  53.8 23.1 %collective-permute-start.5 = (bf16[256,1024]{1,0:T(8,128)(2,1)S(1)}, bf16[256,1024]{1,0:T(8,128)(2,1)S(1)}, u32[]{:S(2)}, u32[]{:S(2)}) collective-permute-start(bf16[256,1024]{1,0:T(8,128)(2,1)S(1)} %fusion.36), channel_id=1, source_target_pairs={{0,48},{16,0},{32,16},{48,32},{1,49},{17,1},{33,17},{49,33},{2,50}... | collective-permute-start | bytes 1572872 | tf_op jit(solution)/shard_map/ppermute | solution.py:28
  77.4 15.4 %collective-permute-start.6 = (bf16[256,1024]{1,0:T(8,128)(2,1)S(1)}, bf16[256,1024]{1,0:T(8,128)(2,1)}, u32[]{:S(2)}, u32[]{:S(2)}) collective-permute-start(bf16[256,1024]{1,0:T(8,128)(2,1)S(1)} %fusion.96), channel_id=1, source_target_pairs={{0,64},{1,65},{2,66},{3,67},{4,68},{5,69},{6,70},{7,71},{8,72},{9,... | collective-permute-start | bytes 1572872 | tf_op jit(solution)/shard_map/ppermute | solution.py:19
  114.0 53.0 %collective-permute-start.7 = (bf16[256,1024]{1,0:T(8,128)(2,1)S(1)}, bf16[256,1024]{1,0:T(8,128)(2,1)S(1)}, u32[]{:S(2)}, u32[]{:S(2)}) collective-permute-start(bf16[256,1024]{1,0:T(8,128)(2,1)S(1)} %fusion.37), channel_id=1, source_target_pairs={{0,16},{16,32},{32,48},{48,0},{1,17},{17,33},{33,49},{49,1},{2,18}... | collective-permute-start | bytes 1572872 | tf_op jit(solution)/shard_map/ppermute | solution.py:28
  115.7 51.3 %collective-permute-start.8 = (bf16[256,1024]{1,0:T(8,128)(2,1)S(1)}, bf16[256,1024]{1,0:T(8,128)(2,1)S(1)}, u32[]{:S(2)}, u32[]{:S(2)}) collective-permute-start(bf16[256,1024]{1,0:T(8,128)(2,1)S(1)} %fusion.37), channel_id=1, source_target_pairs={{0,32},{16,48},{32,0},{48,16},{1,33},{17,49},{33,1},{49,17},{2,34}... | collective-permute-start | bytes 1572872 | tf_op jit(solution)/shard_map/ppermute | solution.py:28
  127.8 24.9 %collective-permute-start.14 = (bf16[256,1024]{1,0:T(8,128)(2,1)S(1)}, bf16[256,1024]{1,0:T(8,128)(2,1)S(1)}, u32[]{:S(2)}, u32[]{:S(2)}) collective-permute-start(bf16[256,1024]{1,0:T(8,128)(2,1)S(1)} %get-tuple-element.178), channel_id=1, source_target_pairs={{0,16},{16,32},{32,48},{48,0},{1,17},{17,33},{33,49},{49,1},{2,18}... | collective-permute-start | bytes 1572872 | tf_op jit(solution)/shard_map/ppermute | solution.py:28
  127.9 35.3 %collective-permute-start.15 = (bf16[256,1024]{1,0:T(8,128)(2,1)S(1)}, bf16[256,1024]{1,0:T(8,128)(2,1)S(1)}, u32[]{:S(2)}, u32[]{:S(2)}) collective-permute-start(bf16[256,1024]{1,0:T(8,128)(2,1)S(1)} %get-tuple-element.178), channel_id=1, source_target_pairs={{0,32},{16,48},{32,0},{48,16},{1,33},{17,49},{33,1},{49,17},{2,34}... | collective-permute-start | bytes 1572872 | tf_op jit(solution)/shard_map/ppermute | solution.py:28
  129.3 33.9 %collective-permute-start.16 = (bf16[256,1024]{1,0:T(8,128)(2,1)S(1)}, bf16[256,1024]{1,0:T(8,128)(2,1)S(1)}, u32[]{:S(2)}, u32[]{:S(2)}) collective-permute-start(bf16[256,1024]{1,0:T(8,128)(2,1)S(1)} %get-tuple-element.178), channel_id=1, source_target_pairs={{0,48},{16,0},{32,16},{48,32},{1,49},{17,1},{33,17},{49,33},{2,50}... | collective-permute-start | bytes 1572872 | tf_op jit(solution)/shard_map/ppermute | solution.py:28
  152.7 14.3 %collective-permute-start.9 = (bf16[256,1024]{1,0:T(8,128)(2,1)S(1)}, bf16[256,1024]{1,0:T(8,128)(2,1)S(1)}, u32[]{:S(2)}, u32[]{:S(2)}) collective-permute-start(bf16[256,1024]{1,0:T(8,128)(2,1)S(1)} %fusion.37), channel_id=1, source_target_pairs={{0,48},{16,0},{32,16},{48,32},{1,49},{17,1},{33,17},{49,33},{2,50}... | collective-permute-start | bytes 1572872 | tf_op jit(solution)/shard_map/ppermute | solution.py:28
  165.7 15.9 %collective-permute-start.17 = (bf16[256,1024]{1,0:T(8,128)(2,1)S(1)}, bf16[256,1024]{1,0:T(8,128)(2,1)S(1)}, u32[]{:S(2)}, u32[]{:S(2)}) collective-permute-start(bf16[256,1024]{1,0:T(8,128)(2,1)S(1)} %fusion.92), channel_id=1, source_target_pairs={{64,0},{65,1},{66,2},{67,3},{68,4},{69,5},{70,6},{71,7},{72,8},{73... | collective-permute-start | bytes 1572872 | tf_op jit(solution)/shard_map/ppermute | solution.py:19
  168.5 15.8 %collective-permute-start.10 = (bf16[256,1024]{1,0:T(8,128)(2,1)S(1)}, bf16[256,1024]{1,0:T(8,128)(2,1)S(1)}, u32[]{:S(2)}, u32[]{:S(2)}) collective-permute-start(bf16[256,1024]{1,0:T(8,128)(2,1)S(1)} %get-tuple-element.73), channel_id=1, source_target_pairs={{0,64},{1,65},{2,66},{3,67},{4,68},{5,69},{6,70},{7,71},{8,72},{9,... | collective-permute-start | bytes 1572872 | tf_op jit(solution)/shard_map/ppermute | solution.py:19
  218.5 23.7 %collective-permute-start.18 = (bf16[256,1024]{1,0:T(8,128)(2,1)S(1)}, bf16[256,1024]{1,0:T(8,128)(2,1)S(1)}, u32[]{:S(2)}, u32[]{:S(2)}) collective-permute-start(bf16[256,1024]{1,0:T(8,128)(2,1)S(1)} %get-tuple-element.186), channel_id=1, source_target_pairs={{0,16},{16,32},{32,48},{48,0},{1,17},{17,33},{33,49},{49,1},{2,18}... | collective-permute-start | bytes 1572872 | tf_op jit(solution)/shard_map/ppermute | solution.py:28
  218.5 23.6 %collective-permute-start.19 = (bf16[256,1024]{1,0:T(8,128)(2,1)S(1)}, bf16[256,1024]{1,0:T(8,128)(2,1)S(1)}, u32[]{:S(2)}, u32[]{:S(2)}) collective-permute-start(bf16[256,1024]{1,0:T(8,128)(2,1)S(1)} %get-tuple-element.186), channel_id=1, source_target_pairs={{0,32},{16,48},{32,0},{48,16},{1,33},{17,49},{33,1},{49,17},{2,34}... | collective-permute-start | bytes 1572872 | tf_op jit(solution)/shard_map/ppermute | solution.py:28
  219.4 23.4 %collective-permute-start.20 = (bf16[256,1024]{1,0:T(8,128)(2,1)S(1)}, bf16[256,1024]{1,0:T(8,128)(2,1)S(1)}, u32[]{:S(2)}, u32[]{:S(2)}) collective-permute-start(bf16[256,1024]{1,0:T(8,128)(2,1)S(1)} %get-tuple-element.186), channel_id=1, source_target_pairs={{0,48},{16,0},{32,16},{48,32},{1,49},{17,1},{33,17},{49,33},{2,50}... | collective-permute-start | bytes 1572872 | tf_op jit(solution)/shard_map/ppermute | solution.py:28
  246.2 16.1 %collective-permute-start.21 = (bf16[256,1024]{1,0:T(8,128)(2,1)S(1)}, bf16[256,1024]{1,0:T(8,128)(2,1)S(1)}, u32[]{:S(2)}, u32[]{:S(2)}) collective-permute-start(bf16[256,1024]{1,0:T(8,128)(2,1)S(1)} %get-tuple-element.67), channel_id=1, source_target_pairs={{64,0},{65,1},{66,2},{67,3},{68,4},{69,5},{70,6},{71,7},{72,8},{73... | collective-permute-start | bytes 1572872 | tf_op jit(solution)/shard_map/ppermute | solution.py:19
  277.6 15.7 %collective-permute-start.22 = (bf16[256,1024]{1,0:T(8,128)(2,1)S(1)}, bf16[256,1024]{1,0:T(8,128)(2,1)S(1)}, u32[]{:S(2)}, u32[]{:S(2)}) collective-permute-start(bf16[256,1024]{1,0:T(8,128)(2,1)S(1)} %get-tuple-element.190), channel_id=1, source_target_pairs={{0,16},{16,32},{32,48},{48,0},{1,17},{17,33},{33,49},{49,1},{2,18}... | collective-permute-start | bytes 1572872 | tf_op jit(solution)/shard_map/ppermute | solution.py:28
  279.3 25.8 %collective-permute-start.23 = (bf16[256,1024]{1,0:T(8,128)(2,1)S(1)}, bf16[256,1024]{1,0:T(8,128)(2,1)S(1)}, u32[]{:S(2)}, u32[]{:S(2)}) collective-permute-start(bf16[256,1024]{1,0:T(8,128)(2,1)S(1)} %get-tuple-element.190), channel_id=1, source_target_pairs={{0,32},{16,48},{32,0},{48,16},{1,33},{17,49},{33,1},{49,17},{2,34}... | collective-permute-start | bytes 1572872 | tf_op jit(solution)/shard_map/ppermute | solution.py:28
  282.8 22.2 %collective-permute-start.24 = (bf16[256,1024]{1,0:T(8,128)(2,1)S(1)}, bf16[256,1024]{1,0:T(8,128)(2,1)S(1)}, u32[]{:S(2)}, u32[]{:S(2)}) collective-permute-start(bf16[256,1024]{1,0:T(8,128)(2,1)S(1)} %get-tuple-element.190), channel_id=1, source_target_pairs={{0,48},{16,0},{32,16},{48,32},{1,49},{17,1},{33,17},{49,33},{2,50}... | collective-permute-start | bytes 1572872 | tf_op jit(solution)/shard_map/ppermute | solution.py:28
  313.5 14.6 %collective-permute-start.11 = (bf16[256,1024]{1,0:T(8,128)(2,1)}, bf16[256,1024]{1,0:T(8,128)(2,1)}, u32[]{:S(2)}, u32[]{:S(2)}) collective-permute-start(bf16[256,1024]{1,0:T(8,128)(2,1)} %fusion.38), channel_id=1, source_target_pairs={{0,16},{16,32},{32,48},{48,0},{1,17},{17,33},{33,49},{49,1},{2,18}... | collective-permute-start | bytes 1572872 | tf_op jit(solution)/shard_map/ppermute | solution.py:28
  313.7 26.8 %collective-permute-start.12 = (bf16[256,1024]{1,0:T(8,128)(2,1)}, bf16[256,1024]{1,0:T(8,128)(2,1)}, u32[]{:S(2)}, u32[]{:S(2)}) collective-permute-start(bf16[256,1024]{1,0:T(8,128)(2,1)} %fusion.38), channel_id=1, source_target_pairs={{0,32},{16,48},{32,0},{48,16},{1,33},{17,49},{33,1},{49,17},{2,34}... | collective-permute-start | bytes 1572872 | tf_op jit(solution)/shard_map/ppermute | solution.py:28
  317.1 23.4 %collective-permute-start.13 = (bf16[256,1024]{1,0:T(8,128)(2,1)}, bf16[256,1024]{1,0:T(8,128)(2,1)}, u32[]{:S(2)}, u32[]{:S(2)}) collective-permute-start(bf16[256,1024]{1,0:T(8,128)(2,1)} %fusion.38), channel_id=1, source_target_pairs={{0,48},{16,0},{32,16},{48,32},{1,49},{17,1},{33,17},{49,33},{2,50}... | collective-permute-start | bytes 1572872 | tf_op jit(solution)/shard_map/ppermute | solution.py:28
  447.7 20.0 %collective-permute-start.25 = (f32[4096]{0:T(1024)S(1)}, f32[4096]{0:T(1024)S(1)}, u32[]{:S(2)}, u32[]{:S(2)}) collective-permute-start(f32[4096]{0:T(1024)S(1)} %bitcast.519), channel_id=1, source_target_pairs={{0,16},{16,32},{32,48},{48,0},{1,17},{17,33},{33,49},{49,1},{2,18}... | collective-permute-start | bytes 49160 | tf_op jit(solution)/shard_map/ppermute | solution.py:28
  449.3 18.4 %collective-permute-start.26 = (f32[4096]{0:T(1024)S(1)}, f32[4096]{0:T(1024)S(1)}, u32[]{:S(2)}, u32[]{:S(2)}) collective-permute-start(f32[4096]{0:T(1024)S(1)} %bitcast.520), channel_id=1, source_target_pairs={{0,32},{16,48},{32,0},{48,16},{1,33},{17,49},{33,1},{49,17},{2,34}... | collective-permute-start | bytes 49160 | tf_op jit(solution)/shard_map/ppermute | solution.py:28
  452.1 15.5 %collective-permute-start.27 = (f32[4096]{0:T(1024)S(1)}, f32[4096]{0:T(1024)S(1)}, u32[]{:S(2)}, u32[]{:S(2)}) collective-permute-start(f32[4096]{0:T(1024)S(1)} %bitcast.521), channel_id=1, source_target_pairs={{0,48},{16,0},{32,16},{48,32},{1,49},{17,1},{33,17},{49,33},{2,50}... | collective-permute-start | bytes 49160 | tf_op jit(solution)/shard_map/ppermute | solution.py:28
  (144 other events, 945.5 us)
Sparse Core Ops, SparseCore 0:
  309.0 134.2 all-reduce.2

commit v5 on v4

--- a/solution.py
+++ b/solution.py
@@ -42,6 +42,50 @@
     for piece in pieces[1:]:
         total = total + piece.astype(jnp.float32)
     return total
+
+def ordered_by_owner(parts, me, peers):
+    ordered = []
+    for owner in range(peers):
+        slot = (me - owner) % peers
+        chosen = parts[peers - 1]
+        for k in range(peers - 2, -1, -1):
+            chosen = jnp.where(slot == k, parts[k], chosen)
+        ordered.append(chosen)
+    return ordered
+
+
+def tensor_scatter_sum(x):
+    peers = lax.axis_size("tensor")
+    me = lax.axis_index("tensor")
+    width = x.shape[1] // peers
+
+    def piece_for(owner):
+        return lax.dynamic_slice_in_dim(x, owner * width, width, 1)
+
+    parts = [piece_for(me)]
+    for shift in range(1, peers):
+        pairs = [(i, (i + shift) % peers) for i in range(peers)]
+        parts.append(lax.ppermute(piece_for((me + shift) % peers), "tensor", pairs))
+    ordered = ordered_by_owner(parts, me, peers)
+    total = ordered[0].astype(jnp.float32)
+    for piece in ordered[1:]:
+        total = total + piece.astype(jnp.float32)
+    return total
+
+
+def cross_gather(x, source_stage):
+    peers = lax.axis_size("tensor")
+    me = lax.axis_index("tensor")
+    target_stage = 1 - source_stage
+    parts = []
+    for shift in range(peers):
+        pairs = [
+            (source_stage * peers + i, target_stage * peers + (i + shift) % peers)
+            for i in range(peers)
+        ]
+        parts.append(lax.ppermute(x, ("pipe", "tensor"), pairs))
+    return jnp.concatenate(ordered_by_owner(parts, me, peers), axis=1)
+
 
 def as_sent(x):
     return jax.tree.map(lambda a: a.astype(jnp.bfloat16) if a.dtype == jnp.float32 else a, x)
@@ -242,8 +286,11 @@
         partial_value = partial_value + jnp.dot(
             forward_activated, down_mat, preferred_element_type=jnp.float32
         )
-        branches = tensor_sum(partial_value.astype(jnp.bfloat16))
-        result = inputs + branches + bias_sum
+        branches = tensor_scatter_sum(partial_value.astype(jnp.bfloat16))
+        column_start = lax.axis_index("tensor") * quarter
+        own_inputs = lax.dynamic_slice_in_dim(inputs, column_start, quarter, 1)
+        own_bias = lax.dynamic_slice_in_dim(bias_sum, column_start, quarter, 0)
+        result = own_inputs + branches + own_bias
         forward_stored = (
             forward_normed,
             forward_inv_scale,
@@ -262,13 +309,12 @@
         tick_outputs.append(result_low)
         tick_stored.append((stored, segment, cosv, sinv))
         if section_tick < NMB:
-            received = passed_along(result_low, "pipe", 1)
-    column_start = lax.axis_index("tensor") * quarter
+            received = cross_gather(result_low, 0)
     section_rows = jnp.concatenate(
         [jnp.where(leading, tick_outputs[block], tick_outputs[block + 1]) for block in range(NMB)],
         axis=0,
     )
-    section_out = lax.dynamic_slice_in_dim(section_rows, column_start, quarter, 1)[None]
+    section_out = section_rows[None]
     returned = jnp.zeros((tick_rows, model_width), jnp.bfloat16)
     tick_grads = []
     totals = None
@@ -352,11 +398,23 @@
             [jnp.sum(d_hattn * normed, axis=0), jnp.sum(d_hmlp * normed, axis=0)]
         )
         grad_shifts = jnp.concatenate([jnp.sum(d_hattn, axis=0), jnp.sum(d_hmlp, axis=0)])
-        d_norm = tensor_sum((d_hattn * ln_gains[0] + d_hmlp * ln_gains[1]).astype(jnp.bfloat16))
-        grad_input = grad_wide + inv_scale * (
-            d_norm
-            - jnp.mean(d_norm, axis=1, keepdims=True)
-            - normed * jnp.mean(d_norm * normed, axis=1, keepdims=True)
+        d_norm = tensor_scatter_sum(
+            (d_hattn * ln_gains[0] + d_hmlp * ln_gains[1]).astype(jnp.bfloat16)
+        )
+        column_start = lax.axis_index("tensor") * quarter
+        own_normed = lax.dynamic_slice_in_dim(normed, column_start, quarter, 1)
+        own_grad = lax.dynamic_slice_in_dim(grad_wide, column_start, quarter, 1)
+        row_stats = tensor_sum(
+            jnp.concatenate(
+                [
+                    jnp.sum(d_norm, axis=1, keepdims=True),
+                    jnp.sum(d_norm * own_normed, axis=1, keepdims=True),
+                ],
+                axis=1,
+            )
+        ) / model_width
+        grad_input = own_grad + inv_scale * (
+            d_norm - row_stats[:, 0:1] - own_normed * row_stats[:, 1:2]
         )
         small_terms = jnp.concatenate(
             [grad_gains, grad_shifts, column_sum, column_sum, grad_joined_add, grad_up_add]
@@ -376,7 +434,7 @@
         else:
             totals = jax.tree.map(lambda older, newer: older + newer, totals, terms)
         if section_tick < NMB:
-            returned = passed_along(grad_low, "pipe", -1)
+            returned = cross_gather(grad_low, 1)
     small_rows = totals[4][0]
     small_pad = (-small_rows.shape[0]) % model_width
     small_rows = jnp.pad(small_rows, (0, small_pad)).reshape(-1, model_width)
@@ -392,7 +450,7 @@
         [jnp.where(leading, tick_grads[block + 1], tick_grads[block]) for block in range(NMB)],
         axis=0,
     )
-    input_grad = lax.dynamic_slice_in_dim(grad_rows_all, column_start, quarter, 1)[None]
+    input_grad = grad_rows_all[None]
     grad_joined = summed[0].T.reshape(1, model_width, 3, local_width)
     grad_dense = summed[1][None]
     grad_up = summed[2][None]

time: 485 us -> 439 us (0.905)
  waiting for transfers between devices: 219 us -> 165 us
  starting transfers between devices: 54.9 us -> 73.7 us
  local copies, waits for them, and re-layouts: 78.4 us -> 67 us
  matrix products: 70.6 us -> 78.4 us
  other arithmetic: 36 us -> 29 us
    ppermute x24 -> x15, waiting for transfers between devices: 105 us -> 19.8 us  [tensor_pieces(): parts.append(lax.ppermute(x, 'tensor', pairs))]
    ppermute x4 -> x34, starting transfers between devices: 14.8 us -> 55.4 us  [the longest x16 34.8 us: cross_gather(): parts.append(lax.ppermute(x, ('pipe', 'tensor'), pairs))]
    ppermute x24 -> x15, starting transfers between devices: 40 us -> 18.2 us  [tensor_pieces(): parts.append(lax.ppermute(x, 'tensor', pairs))]
    ppermute x4 -> x34, waiting for transfers between devices: 16.8 us -> 36.5 us  [the longest x16 19.7 us: cross_gather(): parts.append(lax.ppermute(x, ('pipe', 'tensor'), pairs))]
    unnamed x337 -> x347, local copies, waits for them, and re-layouts: 29.9 us -> 18.2 us
    psum x1, waiting for transfers between devices: 98 us -> 108 us  [per_device(): slab = lax.psum(slab, 'dp').astype(jnp.float32)]
    dot_general x12, matrix products: 21.7 us -> 30.7 us  [contract_rows(): lax.dot_general(left, right, (((0,), (0,)), ((), ())), preferred_element_...]
    reduce_sum x3, other arithmetic: 5.86 us -> 0.86 us  [per_device(): jnp.sum(d_norm, axis=1, keepdims=True)]
  transfers between devices with their start and end apart: 29 -> 50, of which waited for: 17 -> 28; matrix products, arithmetic and copies ran while one was open for 17% -> 10% of each run, Pallas kernels for 0% -> 0%
where the time goes in v5:
time: 439 us; the launch traced here: 430 us
  waiting for transfers between devices  165 us (38%)
  matrix products  78.4 us (18%)
  starting transfers between devices  73.7 us (17%)
  local copies, waits for them, and re-layouts  67 us (15%)
  other arithmetic  29 us (7%)
  between operations  17.4 us (4%)
    psum x1, waiting for transfers between devices, per_device(): slab = lax.psum(slab, 'dp').astype(jnp.float32)  108 us
    ppermute x16, starting transfers between devices, cross_gather(): parts.append(lax.ppermute(x, ('pipe', 'tensor'), pairs))  34.8 us
    dot_general x12, matrix products, contract_rows(): lax.dot_general(left, right, (((0,), (0,)), ((), ())), preferred_element_...  30.7 us
    dot_general x12, matrix products, contract_cols(): lax.dot_general(left, right, (((1,), (1,)), ((), ())), preferred_element_...  21 us
    ppermute x18, starting transfers between devices, tensor_scatter_sum(): parts.append(lax.ppermute(piece_for((me + shift) % peers), 'tensor', pairs))  20.6 us
    ppermute x15, waiting for transfers between devices, tensor_pieces(): parts.append(lax.ppermute(x, 'tensor', pairs))  19.8 us
    ppermute x16, waiting for transfers between devices, cross_gather(): parts.append(lax.ppermute(x, ('pipe', 'tensor'), pairs))  19.7 us
    ppermute x15, starting transfers between devices, tensor_pieces(): parts.append(lax.ppermute(x, 'tensor', pairs))  18.2 us
  transfers between devices with their start and end apart: 50, of which 28 were waited for; matrix products, arithmetic and copies ran while one was open for 10% of the time, Pallas kernels for 0%

profile of v5, /device:TPU:0, one launch (start us, length us, event | category | flops | bytes accessed | tf_op | source)
XLA Modules:
  0.0 430.2 jit_solution(581017666313203114)
XLA Ops:
  9.3 4.2 collective-permute-start.2
  20.9 2.6 copy.125
  26.3 9.6 %collective-permute-done.2 = bf16[1024,256]{1,0:T(8,128)(2,1)S(1)} collective-permute-done((bf16[1024,256]{1,0:T(8,128)(2,1)S(1)}, bf16[1024,256]{1,0:T(8,128)(2,1)S(1)}, u32[]{:S(2)}, u32[]{:S(2)}) %collective-permute-start.2) | collective-permute-done | bytes 524320 | tf_op jit(solution)/shard_map/ppermute | solution.py:28
  36.7 2.7 collective-permute-done
  46.0 3.9 fusion.64
  54.7 3.3 collective-permute-done.5
  61.3 5.5 %collective-permute-start.9 = (bf16[256,256]{1,0:T(8,128)(2,1)S(1)}, bf16[256,256]{1,0:T(8,128)(2,1)S(1)}, u32[]{:S(2)}, u32[]{:S(2)}) collective-permute-start(bf16[256,256]{1,0:T(8,128)(2,1)S(1)} %add_convert_fusion.17), channel_id=1, source_target_pairs={{0,112},{16,64},{32,80},{48,96},{1,113},{17,65},{33,81},{49,97},{2... | collective-permute-start | bytes 393224 | tf_op jit(solution)/shard_map/ppermute | solution.py:86
  96.4 2.9 fusion.67
  99.5 2.6 fusion.156
  103.1 2.8 fusion.146
  106.1 4.2 convert_reduce_fusion.2
  110.3 3.1 fusion.151
  118.4 3.3 collective-permute-start.12
  123.5 3.0 collective-permute-done.20
  130.6 8.4 %collective-permute-start.16 = (bf16[256,256]{1,0:T(8,128)(2,1)S(1)}, bf16[256,256]{1,0:T(8,128)(2,1)S(1)}, u32[]{:S(2)}, u32[]{:S(2)}) collective-permute-start(bf16[256,256]{1,0:T(8,128)(2,1)S(1)} %get-tuple-element.75), channel_id=1, source_target_pairs={{0,112},{16,64},{32,80},{48,96},{1,113},{17,65},{33,81},{49,97},{2... | collective-permute-start | bytes 393224 | tf_op jit(solution)/shard_map/ppermute | solution.py:86
  150.1 5.2 %collective-permute-done.29 = bf16[256,256]{1,0:T(8,128)(2,1)S(1)} collective-permute-done((bf16[256,256]{1,0:T(8,128)(2,1)S(1)}, bf16[256,256]{1,0:T(8,128)(2,1)S(1)}, u32[]{:S(2)}, u32[]{:S(2)}) %collective-permute-start.29) | collective-permute-done | bytes 131104 | tf_op jit(solution)/shard_map/ppermute | solution.py:86
  181.4 2.9 fusion.70
  186.7 2.6 fusion.154
  191.0 3.4 convert_reduce_fusion.1
  194.4 3.1 fusion.149
  201.6 2.7 fusion.144
  222.0 3.3 collective-permute-done.39
  225.2 3.2 collective-permute-done.38
  229.6 5.4 %convert_reduce_fusion = (f32[1024]{0:T(1024)}, bf16[256,1024]{1,0:T(8,128)(2,1)}) fusion(bf16[1,1024,1024]{2,1,0:T(8,128)(2,1)S(1)} %copy-done.12, bf16[256,256]{1,0:T(8,128)(2,1)S(1)} %get-tuple-element.103, bf16[256,256]{1,0:T(8,128)(2,1)S(1)} %get-tuple-element.104, bf16[256,256]{1,0:T(8,128)(2,1)S(1)} %get-tuple-element.105, ...), kind=kOutput, calls=%fused_computation.122 | convolution fusion | flops 558889984 | bytes 5246977 | tf_op jit(solution)/shard_map/dot_general | solution.py:163
  249.1 5.2 %fusion.26 = bf16[3080,1024]{1,0:T(8,128)(2,1)} fusion(f32[768,1024]{1,0:T(8,128)} %fusion.156, f32[768,1024]{1,0:T(8,128)} %fusion.154, pred[]{:T(512)S(6)} %eq.171, bf16[256,256]{0,1:T(8,128)(2,1)S(1)} %bitcast.422, bf16[256,256]{0,1:T(8,128)(2,1)S(1)} %bitcast.428, bf16[256,256]{0,1:T(8,128)(2,1)S(1)} %bitcast.425, ...), kind=kOutput, calls=%fused_computation.32 | convolution fusion | flops 409600000 | bytes 9318401 | tf_op jit(solution)/shard_map/dot_general | solution.py:157
  271.6 2.7 collective-permute-start.42
  289.9 108.5 %all-reduce.3.cloned.1.call-done = bf16[3080,1024]{1,0:T(8,128)(2,1)} async-done(((bf16[3080,1024]{1,0:T(8,128)(2,1)}), bf16[3080,1024]{1,0:T(8,128)(2,1)}) %all-reduce.3.cloned.1.call-update) | async-done | bytes 6307856 | tf_op jit(solution)/shard_map/psum | solution.py:443
  398.4 4.3 %convert_element_type.513 = f32[3080,1024]{1,0:T(8,128)S(1)} convert(bf16[3080,1024]{1,0:T(8,128)(2,1)} %all-reduce.3.cloned.1.call-done) | non-fusion elementwise | flops 3153920 | bytes 18923520 | tf_op jit(solution)/shard_map/convert_element_type | solution.py:443
  402.8 3.0 collective-permute-start.48
  408.5 4.2 slice_bitcast_fusion
  413.9 3.6 slice.465
  417.5 3.5 copy.198
  (637 shorter events, 183.6 us)
Async XLA Ops:
  7.2 391.2 %all-reduce.3.cloned.1.call-start = ((), (), s32[]{:S(2)}) async-start(), calls=%async_computation | async-start | bytes 12615680 | tf_op jit(solution)/shard_map/psum | solution.py:443
  9.3 26.6 %collective-permute-start.2 = (bf16[1024,256]{1,0:T(8,128)(2,1)S(1)}, bf16[1024,256]{1,0:T(8,128)(2,1)S(1)}, u32[]{:S(2)}, u32[]{:S(2)}) collective-permute-start(bf16[1024,256]{1,0:T(8,128)(2,1)S(1)} %constant_dynamic-update-slice_fusion), channel_id=1, source_target_pairs={{0,48},{16,0},{32,16},{48,32},{1,49},{17,1},{33,17},{49,33},{2,50}... | collective-permute-start | bytes 1572872 | tf_op jit(solution)/shard_map/ppermute | solution.py:28
  13.5 22.4 %collective-permute-start.1 = (bf16[1024,256]{1,0:T(8,128)(2,1)S(1)}, bf16[1024,256]{1,0:T(8,128)(2,1)}, u32[]{:S(2)}, u32[]{:S(2)}) collective-permute-start(bf16[1024,256]{1,0:T(8,128)(2,1)S(1)} %constant_dynamic-update-slice_fusion), channel_id=1, source_target_pairs={{0,32},{16,48},{32,0},{48,16},{1,33},{17,49},{33,1},{49,17},{2,34}... | collective-permute-start | bytes 1572872 | tf_op jit(solution)/shard_map/ppermute | solution.py:28
  13.5 25.9 %collective-permute-start = (bf16[1024,256]{1,0:T(8,128)(2,1)S(1)}, bf16[1024,256]{1,0:T(8,128)(2,1)}, u32[]{:S(2)}, u32[]{:S(2)}) collective-permute-start(bf16[1024,256]{1,0:T(8,128)(2,1)S(1)} %constant_dynamic-update-slice_fusion), channel_id=1, source_target_pairs={{0,16},{16,32},{32,48},{48,0},{1,17},{17,33},{33,49},{49,1},{2,18}... | collective-permute-start | bytes 1572872 | tf_op jit(solution)/shard_map/ppermute | solution.py:28
  52.5 7.7 %collective-permute-start.4 = (bf16[256,256]{1,0:T(8,128)(2,1)S(1)}, bf16[256,256]{1,0:T(8,128)(2,1)S(1)}, u32[]{:S(2)}, u32[]{:S(2)}) collective-permute-start(bf16[256,256]{1,0:T(8,128)(2,1)S(1)} %get-tuple-element.131), channel_id=1, source_target_pairs={{0,32},{16,48},{32,0},{48,16},{1,33},{17,49},{33,1},{49,17},{2,34}... | collective-permute-start | bytes 393224 | tf_op jit(solution)/shard_map/ppermute | solution.py:68
  52.8 8.3 %collective-permute-start.3 = (bf16[256,256]{1,0:T(8,128)(2,1)S(1)}, bf16[256,256]{1,0:T(8,128)(2,1)S(1)}, u32[]{:S(2)}, u32[]{:S(2)}) collective-permute-start(bf16[256,256]{1,0:T(8,128)(2,1)S(1)} %get-tuple-element.132), channel_id=1, source_target_pairs={{0,16},{16,32},{32,48},{48,0},{1,17},{17,33},{33,49},{49,1},{2,18}... | collective-permute-start | bytes 393224 | tf_op jit(solution)/shard_map/ppermute | solution.py:68
  61.3 12.9 %collective-permute-start.9 = (bf16[256,256]{1,0:T(8,128)(2,1)S(1)}, bf16[256,256]{1,0:T(8,128)(2,1)S(1)}, u32[]{:S(2)}, u32[]{:S(2)}) collective-permute-start(bf16[256,256]{1,0:T(8,128)(2,1)S(1)} %add_convert_fusion.17), channel_id=1, source_target_pairs={{0,112},{16,64},{32,80},{48,96},{1,113},{17,65},{33,81},{49,97},{2... | collective-permute-start | bytes 393224 | tf_op jit(solution)/shard_map/ppermute | solution.py:86
  66.8 7.4 %collective-permute-start.8 = (bf16[256,256]{1,0:T(8,128)(2,1)S(1)}, bf16[256,256]{1,0:T(8,128)(2,1)}, u32[]{:S(2)}, u32[]{:S(2)}) collective-permute-start(bf16[256,256]{1,0:T(8,128)(2,1)S(1)} %add_convert_fusion.17), channel_id=1, source_target_pairs={{0,96},{16,112},{32,64},{48,80},{1,97},{17,113},{33,65},{49,81},{2... | collective-permute-start | bytes 393224 | tf_op jit(solution)/shard_map/ppermute | solution.py:86
  115.6 8.0 %collective-permute-start.21 = (bf16[256,256]{1,0:T(8,128)(2,1)S(1)}, bf16[256,256]{1,0:T(8,128)(2,1)S(1)}, u32[]{:S(2)}, u32[]{:S(2)}) collective-permute-start(bf16[256,256]{1,0:T(8,128)(2,1)S(1)} %get-tuple-element.114), channel_id=1, source_target_pairs={{0,32},{16,48},{32,0},{48,16},{1,33},{17,49},{33,1},{49,17},{2,34}... | collective-permute-start | bytes 393224 | tf_op jit(solution)/shard_map/ppermute | solution.py:68
  117.9 8.6 %collective-permute-start.20 = (bf16[256,256]{1,0:T(8,128)(2,1)S(1)}, bf16[256,256]{1,0:T(8,128)(2,1)S(1)}, u32[]{:S(2)}, u32[]{:S(2)}) collective-permute-start(bf16[256,256]{1,0:T(8,128)(2,1)S(1)} %get-tuple-element.115), channel_id=1, source_target_pairs={{0,16},{16,32},{32,48},{48,0},{1,17},{17,33},{33,49},{49,1},{2,18}... | collective-permute-start | bytes 393224 | tf_op jit(solution)/shard_map/ppermute | solution.py:68
  118.4 11.0 %collective-permute-start.12 = (bf16[256,256]{1,0:T(8,128)(2,1)S(1)}, bf16[256,256]{1,0:T(8,128)(2,1)S(1)}, u32[]{:S(2)}, u32[]{:S(2)}) collective-permute-start(bf16[256,256]{1,0:T(8,128)(2,1)S(1)} %get-tuple-element.123), channel_id=1, source_target_pairs={{0,48},{16,0},{32,16},{48,32},{1,49},{17,1},{33,17},{49,33},{2,50}... | collective-permute-start | bytes 393224 | tf_op jit(solution)/shard_map/ppermute | solution.py:68
  121.7 7.9 %collective-permute-start.11 = (bf16[256,256]{1,0:T(8,128)(2,1)S(1)}, bf16[256,256]{1,0:T(8,128)(2,1)S(1)}, u32[]{:S(2)}, u32[]{:S(2)}) collective-permute-start(bf16[256,256]{1,0:T(8,128)(2,1)S(1)} %get-tuple-element.124), channel_id=1, source_target_pairs={{0,32},{16,48},{32,0},{48,16},{1,33},{17,49},{33,1},{49,17},{2,34}... | collective-permute-start | bytes 393224 | tf_op jit(solution)/shard_map/ppermute | solution.py:68
  122.3 7.4 %collective-permute-start.10 = (bf16[256,256]{1,0:T(8,128)(2,1)S(1)}, bf16[256,256]{1,0:T(8,128)(2,1)S(1)}, u32[]{:S(2)}, u32[]{:S(2)}) collective-permute-start(bf16[256,256]{1,0:T(8,128)(2,1)S(1)} %get-tuple-element.125), channel_id=1, source_target_pairs={{0,16},{16,32},{32,48},{48,0},{1,17},{17,33},{33,49},{49,1},{2,18}... | collective-permute-start | bytes 393224 | tf_op jit(solution)/shard_map/ppermute | solution.py:68
  126.9 13.9 %collective-permute-start.25 = (f32[256,2]{0,1:T(2,128)S(1)}, f32[256,2]{0,1:T(2,128)S(1)}, u32[]{:S(2)}, u32[]{:S(2)}) collective-permute-start(f32[256,2]{0,1:T(2,128)S(1)} %pad_maximum_fusion.10), channel_id=1, source_target_pairs={{0,48},{16,0},{32,16},{48,32},{1,49},{17,1},{33,17},{49,33},{2,50}... | collective-permute-start | bytes 6152 | tf_op jit(solution)/shard_map/ppermute | solution.py:28
  127.0 15.1 %collective-permute-start.24 = (f32[256,2]{0,1:T(2,128)S(1)}, f32[256,2]{0,1:T(2,128)S(1)}, u32[]{:S(2)}, u32[]{:S(2)}) collective-permute-start(f32[256,2]{0,1:T(2,128)S(1)} %pad_maximum_fusion.10), channel_id=1, source_target_pairs={{0,32},{16,48},{32,0},{48,16},{1,33},{17,49},{33,1},{49,17},{2,34}... | collective-permute-start | bytes 6152 | tf_op jit(solution)/shard_map/ppermute | solution.py:28
  129.4 14.0 %collective-permute-start.23 = (f32[256,2]{0,1:T(2,128)S(1)}, f32[256,2]{0,1:T(2,128)S(1)}, u32[]{:S(2)}, u32[]{:S(2)}) collective-permute-start(f32[256,2]{0,1:T(2,128)S(1)} %pad_maximum_fusion.10), channel_id=1, source_target_pairs={{0,16},{16,32},{32,48},{48,0},{1,17},{17,33},{33,49},{49,1},{2,18}... | collective-permute-start | bytes 6152 | tf_op jit(solution)/shard_map/ppermute | solution.py:28
  130.6 15.3 %collective-permute-start.16 = (bf16[256,256]{1,0:T(8,128)(2,1)S(1)}, bf16[256,256]{1,0:T(8,128)(2,1)S(1)}, u32[]{:S(2)}, u32[]{:S(2)}) collective-permute-start(bf16[256,256]{1,0:T(8,128)(2,1)S(1)} %get-tuple-element.75), channel_id=1, source_target_pairs={{0,112},{16,64},{32,80},{48,96},{1,113},{17,65},{33,81},{49,97},{2... | collective-permute-start | bytes 393224 | tf_op jit(solution)/shard_map/ppermute | solution.py:86
  139.0 8.2 %collective-permute-start.15 = (bf16[256,256]{1,0:T(8,128)(2,1)S(1)}, bf16[256,256]{1,0:T(8,128)(2,1)S(1)}, u32[]{:S(2)}, u32[]{:S(2)}) collective-permute-start(bf16[256,256]{1,0:T(8,128)(2,1)S(1)} %get-tuple-element.75), channel_id=1, source_target_pairs={{0,96},{16,112},{32,64},{48,80},{1,97},{17,113},{33,65},{49,81},{2... | collective-permute-start | bytes 393224 | tf_op jit(solution)/shard_map/ppermute | solution.py:86
  140.8 7.8 %collective-permute-start.14 = (bf16[256,256]{1,0:T(8,128)(2,1)S(1)}, bf16[256,256]{1,0:T(8,128)(2,1)S(1)}, u32[]{:S(2)}, u32[]{:S(2)}) collective-permute-start(bf16[256,256]{1,0:T(8,128)(2,1)S(1)} %get-tuple-element.75), channel_id=1, source_target_pairs={{0,80},{16,96},{32,112},{48,64},{1,81},{17,97},{33,113},{49,65},{2... | collective-permute-start | bytes 393224 | tf_op jit(solution)/shard_map/ppermute | solution.py:86
  142.1 7.9 %collective-permute-start.13 = (bf16[256,256]{1,0:T(8,128)(2,1)S(1)}, bf16[256,256]{1,0:T(8,128)(2,1)S(1)}, u32[]{:S(2)}, u32[]{:S(2)}) collective-permute-start(bf16[256,256]{1,0:T(8,128)(2,1)S(1)} %get-tuple-element.75), channel_id=1, source_target_pairs={{0,64},{16,80},{32,96},{48,112},{1,65},{17,81},{33,97},{49,113},{2... | collective-permute-start | bytes 393224 | tf_op jit(solution)/shard_map/ppermute | solution.py:86
  144.6 10.7 %collective-permute-start.29 = (bf16[256,256]{1,0:T(8,128)(2,1)S(1)}, bf16[256,256]{1,0:T(8,128)(2,1)S(1)}, u32[]{:S(2)}, u32[]{:S(2)}) collective-permute-start(bf16[256,256]{1,0:T(8,128)(2,1)S(1)} %add_convert_fusion.14), channel_id=1, source_target_pairs={{64,48},{80,0},{96,16},{112,32},{65,49},{81,1},{97,17},{113,33},{6... | collective-permute-start | bytes 393224 | tf_op jit(solution)/shard_map/ppermute | solution.py:86
  145.9 11.4 %collective-permute-start.28 = (bf16[256,256]{1,0:T(8,128)(2,1)S(1)}, bf16[256,256]{1,0:T(8,128)(2,1)S(1)}, u32[]{:S(2)}, u32[]{:S(2)}) collective-permute-start(bf16[256,256]{1,0:T(8,128)(2,1)S(1)} %add_convert_fusion.14), channel_id=1, source_target_pairs={{64,32},{80,48},{96,0},{112,16},{65,33},{81,49},{97,1},{113,17},{6... | collective-permute-start | bytes 393224 | tf_op jit(solution)/shard_map/ppermute | solution.py:86
  147.2 11.6 %collective-permute-start.27 = (bf16[256,256]{1,0:T(8,128)(2,1)S(1)}, bf16[256,256]{1,0:T(8,128)(2,1)S(1)}, u32[]{:S(2)}, u32[]{:S(2)}) collective-permute-start(bf16[256,256]{1,0:T(8,128)(2,1)S(1)} %add_convert_fusion.14), channel_id=1, source_target_pairs={{64,16},{80,32},{96,48},{112,0},{65,17},{81,33},{97,49},{113,1},{6... | collective-permute-start | bytes 393224 | tf_op jit(solution)/shard_map/ppermute | solution.py:86
  148.5 11.1 %collective-permute-start.26 = (bf16[256,256]{1,0:T(8,128)(2,1)S(1)}, bf16[256,256]{1,0:T(8,128)(2,1)S(1)}, u32[]{:S(2)}, u32[]{:S(2)}) collective-permute-start(bf16[256,256]{1,0:T(8,128)(2,1)S(1)} %add_convert_fusion.14), channel_id=1, source_target_pairs={{64,0},{80,16},{96,32},{112,48},{65,1},{81,17},{97,33},{113,49},{6... | collective-permute-start | bytes 393224 | tf_op jit(solution)/shard_map/ppermute | solution.py:86
  216.0 9.3 %collective-permute-start.39 = (bf16[256,256]{1,0:T(8,128)(2,1)S(1)}, bf16[256,256]{1,0:T(8,128)(2,1)S(1)}, u32[]{:S(2)}, u32[]{:S(2)}) collective-permute-start(bf16[256,256]{1,0:T(8,128)(2,1)S(1)} %get-tuple-element.70), channel_id=1, source_target_pairs={{64,48},{80,0},{96,16},{112,32},{65,49},{81,1},{97,17},{113,33},{6... | collective-permute-start | bytes 393224 | tf_op jit(solution)/shard_map/ppermute | solution.py:86
  217.3 11.2 %collective-permute-start.38 = (bf16[256,256]{1,0:T(8,128)(2,1)S(1)}, bf16[256,256]{1,0:T(8,128)(2,1)S(1)}, u32[]{:S(2)}, u32[]{:S(2)}) collective-permute-start(bf16[256,256]{1,0:T(8,128)(2,1)S(1)} %get-tuple-element.70), channel_id=1, source_target_pairs={{64,32},{80,48},{96,0},{112,16},{65,33},{81,49},{97,1},{113,17},{6... | collective-permute-start | bytes 393224 | tf_op jit(solution)/shard_map/ppermute | solution.py:86
  218.6 10.9 %collective-permute-start.37 = (bf16[256,256]{1,0:T(8,128)(2,1)S(1)}, bf16[256,256]{1,0:T(8,128)(2,1)S(1)}, u32[]{:S(2)}, u32[]{:S(2)}) collective-permute-start(bf16[256,256]{1,0:T(8,128)(2,1)S(1)} %get-tuple-element.70), channel_id=1, source_target_pairs={{64,16},{80,32},{96,48},{112,0},{65,17},{81,33},{97,49},{113,1},{6... | collective-permute-start | bytes 393224 | tf_op jit(solution)/shard_map/ppermute | solution.py:86
  219.9 9.6 %collective-permute-start.36 = (bf16[256,256]{1,0:T(8,128)(2,1)S(1)}, bf16[256,256]{1,0:T(8,128)(2,1)S(1)}, u32[]{:S(2)}, u32[]{:S(2)}) collective-permute-start(bf16[256,256]{1,0:T(8,128)(2,1)S(1)} %get-tuple-element.70), channel_id=1, source_target_pairs={{64,0},{80,16},{96,32},{112,48},{65,1},{81,17},{97,33},{113,49},{6... | collective-permute-start | bytes 393224 | tf_op jit(solution)/shard_map/ppermute | solution.py:86
  267.9 7.5 %collective-permute-start.19 = (bf16[256,256]{1,0:T(8,128)(2,1)S(1)}, bf16[256,256]{1,0:T(8,128)(2,1)S(1)}, u32[]{:S(2)}, u32[]{:S(2)}) collective-permute-start(bf16[256,256]{1,0:T(8,128)(2,1)S(1)} %get-tuple-element.116), channel_id=1, source_target_pairs={{0,48},{16,0},{32,16},{48,32},{1,49},{17,1},{33,17},{49,33},{2,50}... | collective-permute-start | bytes 393224 | tf_op jit(solution)/shard_map/ppermute | solution.py:68
  402.8 18.8 %collective-permute-start.48 = (f32[4096]{0:T(1024)S(1)}, f32[4096]{0:T(1024)S(1)}, u32[]{:S(2)}, u32[]{:S(2)}) collective-permute-start(f32[4096]{0:T(1024)S(1)} %bitcast.528), channel_id=1, source_target_pairs={{0,48},{16,0},{32,16},{48,32},{1,49},{17,1},{33,17},{49,33},{2,50}... | collective-permute-start | bytes 49160 | tf_op jit(solution)/shard_map/ppermute | solution.py:28
  405.8 15.8 %collective-permute-start.47 = (f32[4096]{0:T(1024)S(1)}, f32[4096]{0:T(1024)S(1)}, u32[]{:S(2)}, u32[]{:S(2)}) collective-permute-start(f32[4096]{0:T(1024)S(1)} %bitcast.529), channel_id=1, source_target_pairs={{0,32},{16,48},{32,0},{48,16},{1,33},{17,49},{33,1},{49,17},{2,34}... | collective-permute-start | bytes 49160 | tf_op jit(solution)/shard_map/ppermute | solution.py:28
  406.5 15.2 %collective-permute-start.46 = (f32[4096]{0:T(1024)S(1)}, f32[4096]{0:T(1024)S(1)}, u32[]{:S(2)}, u32[]{:S(2)}) collective-permute-start(f32[4096]{0:T(1024)S(1)} %bitcast.530), channel_id=1, source_target_pairs={{0,16},{16,32},{32,48},{48,0},{1,17},{17,33},{33,49},{49,1},{2,18}... | collective-permute-start | bytes 49160 | tf_op jit(solution)/shard_map/ppermute | solution.py:28
  (170 other events, 1024.2 us)
Sparse Core Ops, SparseCore 0:
  264.0 134.3 all-reduce.2

commit v6 on v5

--- a/solution.py
+++ b/solution.py
@@ -6,7 +6,7 @@
 HD = 64
 ROT = 16
 MB = 128
-NMB = 2
+NMB = 4
 
 
 EPSILON = 1e-05

time: 439 us -> 602 us (1.37)
  starting transfers between devices: 73.7 us -> 143 us
  matrix products: 78.4 us -> 134 us
  other arithmetic: 29 us -> 50.9 us
  waiting for transfers between devices: 165 us -> 172 us
  local copies, waits for them, and re-layouts: 67 us -> 73.3 us
    ppermute x18 -> x30, starting transfers between devices: 20.6 us -> 52.9 us  [tensor_scatter_sum(): parts.append(lax.ppermute(piece_for((me + shift) % peers), 'tensor', pairs))]
    dot_general x12 -> x20, matrix products: 30.7 us -> 62.5 us  [contract_rows(): lax.dot_general(left, right, (((0,), (0,)), ((), ())), preferred_element_...]
    ppermute x16 -> x32, starting transfers between devices: 34.8 us -> 55.4 us  [cross_gather(): parts.append(lax.ppermute(x, ('pipe', 'tensor'), pairs))]
    ppermute x15 -> x21, starting transfers between devices: 18.2 us -> 34.6 us  [tensor_pieces(): parts.append(lax.ppermute(x, 'tensor', pairs))]
    ppermute x16 -> x32, waiting for transfers between devices: 19.7 us -> 33.9 us  [cross_gather(): parts.append(lax.ppermute(x, ('pipe', 'tensor'), pairs))]
    slice x5 -> x12, local copies, waits for them, and re-layouts: 1.56 us -> 11.6 us  [the longest x10 11.6 us: rotate(): heads_in[..., ROT:]]
    select_n x7 -> x13, other arithmetic: 2.49 us -> 10.4 us  [pick(): jnp.where(leading, upper_val, lower_val)]
    reshape x12 -> x0, local copies, waits for them, and re-layouts: 7.24 us -> none  [the longest x6 7.13 us: per_device(): d_context3 = d_context.reshape(blocked)]
  transfers between devices with their start and end apart: 50 -> 84, of which waited for: 28 -> 37; matrix products, arithmetic and copies ran while one was open for 10% -> 9% of each run, Pallas kernels for 0% -> 0%
where the time goes in v6:
time: 602 us; the launch traced here: 593 us
  waiting for transfers between devices  172 us (29%)
  starting transfers between devices  143 us (24%)
  matrix products  134 us (22%)
  local copies, waits for them, and re-layouts  73.3 us (12%)
  other arithmetic  50.9 us (8%)
  between operations  19.2 us (3%)
    psum x1, waiting for transfers between devices, per_device(): slab = lax.psum(slab, 'dp').astype(jnp.float32)  105 us
    dot_general x20, matrix products, contract_rows(): lax.dot_general(left, right, (((0,), (0,)), ((), ())), preferred_element_...  62.5 us
    ppermute x32, starting transfers between devices, cross_gather(): parts.append(lax.ppermute(x, ('pipe', 'tensor'), pairs))  55.4 us
    ppermute x30, starting transfers between devices, tensor_scatter_sum(): parts.append(lax.ppermute(piece_for((me + shift) % peers), 'tensor', pairs))  52.9 us
    ppermute x21, starting transfers between devices, tensor_pieces(): parts.append(lax.ppermute(x, 'tensor', pairs))  34.6 us
    ppermute x32, waiting for transfers between devices, cross_gather(): parts.append(lax.ppermute(x, ('pipe', 'tensor'), pairs))  33.9 us
    dot_general x20, matrix products, contract_cols(): lax.dot_general(left, right, (((1,), (1,)), ((), ())), preferred_element_...  22.1 us
    ppermute x30, waiting for transfers between devices, tensor_scatter_sum(): parts.append(lax.ppermute(piece_for((me + shift) % peers), 'tensor', pairs))  18.3 us
  transfers between devices with their start and end apart: 84, of which 37 were waited for; matrix products, arithmetic and copies ran while one was open for 9% of the time, Pallas kernels for 0%

profile of v6, /device:TPU:0, one launch (start us, length us, event | category | flops | bytes accessed | tf_op | source)
XLA Modules:
  0.0 592.8 jit_solution(2221404189313413333)
XLA Ops:
  11.5 3.6 collective-permute-start.1
  29.2 8.8 %collective-permute-done.1 = bf16[1024,256]{1,0:T(8,128)(2,1)} collective-permute-done((bf16[1024,256]{1,0:T(8,128)(2,1)S(1)}, bf16[1024,256]{1,0:T(8,128)(2,1)}, u32[]{:S(2)}, u32[]{:S(2)}) %collective-permute-start.1) | collective-permute-done | bytes 524320 | tf_op jit(solution)/shard_map/ppermute | solution.py:28
  54.9 4.9 collective-permute-start.6
  63.3 3.1 collective-permute-start.9
  96.1 4.4 fusion.267
  112.1 13.2 %collective-permute-start.36 = (bf16[128,256]{1,0:T(8,128)(2,1)S(1)}, bf16[128,256]{1,0:T(8,128)(2,1)S(1)}, u32[]{:S(2)}, u32[]{:S(2)}) collective-permute-start(bf16[128,256]{1,0:T(8,128)(2,1)S(1)} %get-tuple-element.181), channel_id=1, source_target_pairs={{0,48},{16,0},{32,16},{48,32},{1,49},{17,1},{33,17},{49,33},{2,50}... | collective-permute-start | bytes 196616 | tf_op jit(solution)/shard_map/ppermute | solution.py:68
  129.4 3.2 collective-permute-start.38
  134.7 6.6 %collective-permute-start.13 = (bf16[128,256]{1,0:T(8,128)(2,1)S(1)}, bf16[128,256]{1,0:T(8,128)(2,1)S(1)}, u32[]{:S(2)}, u32[]{:S(2)}) collective-permute-start(bf16[128,256]{1,0:T(8,128)(2,1)S(1)} %get-tuple-element.111), channel_id=1, source_target_pairs={{0,64},{16,80},{32,96},{48,112},{1,65},{17,81},{33,97},{49,113},{2... | collective-permute-start | bytes 196616 | tf_op jit(solution)/shard_map/ppermute | solution.py:86
  153.9 3.4 collective-permute-done.41
  191.1 4.4 fusion.265
  198.1 3.3 collective-permute-start.18
  201.3 3.0 fusion.274
  232.6 3.4 collective-permute-done.51
  272.2 4.4 fusion.263
  279.4 3.1 collective-permute-start.25
  282.5 2.9 fusion.272
  313.9 3.4 collective-permute-done.61
  350.7 4.4 fusion.261
  355.2 2.9 fusion.270
  360.0 3.1 collective-permute-start.65
  383.0 3.4 collective-permute-done.71
  402.8 6.9 %fusion.42 = bf16[3080,1024]{1,0:T(8,128)(2,1)} fusion(f32[768,1024]{1,0:T(8,128)} %fusion.279, f32[768,1024]{1,0:T(8,128)} %fusion.281, f32[768,1024]{1,0:T(8,128)} %fusion.285, f32[768,1024]{1,0:T(8,128)} %fusion.283, pred[]{:T(512)S(6)} %eq.303, bf16[128,256]{0,1:T(8,128)(2,1)S(1)} %bitcast.527, bf16[128,256]{0,1:T(8,128)(2,1)S(1)} %bitcast.521, ...), kind=kOutput, calls=%fused_computation.48 | convolution fusion | flops 207552512 | bytes 14886913 | tf_op jit(solution)/shard_map/dot_general | solution.py:157
  409.7 3.2 fusion.44
  413.5 3.8 fusion.40
  418.1 6.7 %fusion.41 = bf16[3080,1024]{1,0:T(8,128)(2,1)} fusion(bf16[3080,1024]{1,0:T(8,128)(2,1)} %fusion.40, f32[1024,1024]{1,0:T(8,128)} %fusion.261, f32[1024,1024]{1,0:T(8,128)} %fusion.263, f32[1024,1024]{1,0:T(8,128)S(1)} %copy-done.254, f32[1024,1024]{1,0:T(8,128)S(1)} %copy-done.255, pred[]{:T(512)S(6)} %eq.303, ...), kind=kOutput, calls=%fused_computation.47 | convolution fusion | flops 292028416 | bytes 20186112 | tf_op jit(solution)/shard_map/dot_general | solution.py:157
  426.5 3.3 fusion.75
  430.6 3.3 collective-permute-start.32
  454.5 105.4 %all-reduce.3.cloned.1.call-done = bf16[3080,1024]{1,0:T(8,128)(2,1)} async-done(((bf16[3080,1024]{1,0:T(8,128)(2,1)}), bf16[3080,1024]{1,0:T(8,128)(2,1)}) %all-reduce.3.cloned.1.call-update) | async-done | bytes 6307856 | tf_op jit(solution)/shard_map/psum | solution.py:443
  559.9 4.3 convert_element_type.916
  571.2 4.2 slice_bitcast_fusion
  576.6 3.5 slice.703
  580.1 3.5 copy.182
  (1006 shorter events, 332.4 us)
Async XLA Ops:
  7.2 552.7 %all-reduce.3.cloned.1.call-start = ((), (), s32[]{:S(2)}) async-start(), calls=%async_computation | async-start | bytes 12615680 | tf_op jit(solution)/shard_map/psum | solution.py:443
  9.4 19.8 %collective-permute-start = (bf16[1024,256]{1,0:T(8,128)(2,1)S(1)}, bf16[1024,256]{1,0:T(8,128)(2,1)S(1)}, u32[]{:S(2)}, u32[]{:S(2)}) collective-permute-start(bf16[1024,256]{1,0:T(8,128)(2,1)S(1)} %constant_dynamic-update-slice_fusion), channel_id=1, source_target_pairs={{0,16},{16,32},{32,48},{48,0},{1,17},{17,33},{33,49},{49,1},{2,18}... | collective-permute-start | bytes 1572872 | tf_op jit(solution)/shard_map/ppermute | solution.py:28
  11.5 26.6 %collective-permute-start.1 = (bf16[1024,256]{1,0:T(8,128)(2,1)S(1)}, bf16[1024,256]{1,0:T(8,128)(2,1)}, u32[]{:S(2)}, u32[]{:S(2)}) collective-permute-start(bf16[1024,256]{1,0:T(8,128)(2,1)S(1)} %constant_dynamic-update-slice_fusion), channel_id=1, source_target_pairs={{0,32},{16,48},{32,0},{48,16},{1,33},{17,49},{33,1},{49,17},{2,34}... | collective-permute-start | bytes 1572872 | tf_op jit(solution)/shard_map/ppermute | solution.py:28
  15.0 23.0 %collective-permute-start.2 = (bf16[1024,256]{1,0:T(8,128)(2,1)S(1)}, bf16[1024,256]{1,0:T(8,128)(2,1)}, u32[]{:S(2)}, u32[]{:S(2)}) collective-permute-start(bf16[1024,256]{1,0:T(8,128)(2,1)S(1)} %constant_dynamic-update-slice_fusion), channel_id=1, source_target_pairs={{0,48},{16,0},{32,16},{48,32},{1,49},{17,1},{33,17},{49,33},{2,50}... | collective-permute-start | bytes 1572872 | tf_op jit(solution)/shard_map/ppermute | solution.py:28
  54.9 12.6 %collective-permute-start.6 = (bf16[128,256]{1,0:T(8,128)(2,1)S(1)}, bf16[128,256]{1,0:T(8,128)(2,1)S(1)}, u32[]{:S(2)}, u32[]{:S(2)}) collective-permute-start(bf16[128,256]{1,0:T(8,128)(2,1)S(1)} %add_convert_fusion.27), channel_id=1, source_target_pairs={{0,64},{16,80},{32,96},{48,112},{1,65},{17,81},{33,97},{49,113},{2... | collective-permute-start | bytes 196616 | tf_op jit(solution)/shard_map/ppermute | solution.py:86
  102.5 30.0 %collective-permute-start.10 = (bf16[128,256]{1,0:T(8,128)(2,1)S(1)}, bf16[128,256]{1,0:T(8,128)(2,1)S(1)}, u32[]{:S(2)}, u32[]{:S(2)}) collective-permute-start(bf16[128,256]{1,0:T(8,128)(2,1)S(1)} %get-tuple-element.207), channel_id=1, source_target_pairs={{0,16},{16,32},{32,48},{48,0},{1,17},{17,33},{33,49},{49,1},{2,18}... | collective-permute-start | bytes 196616 | tf_op jit(solution)/shard_map/ppermute | solution.py:68
  103.4 29.7 %collective-permute-start.11 = (bf16[128,256]{1,0:T(8,128)(2,1)S(1)}, bf16[128,256]{1,0:T(8,128)(2,1)S(1)}, u32[]{:S(2)}, u32[]{:S(2)}) collective-permute-start(bf16[128,256]{1,0:T(8,128)(2,1)S(1)} %get-tuple-element.206), channel_id=1, source_target_pairs={{0,32},{16,48},{32,0},{48,16},{1,33},{17,49},{33,1},{49,17},{2,34}... | collective-permute-start | bytes 196616 | tf_op jit(solution)/shard_map/ppermute | solution.py:68
  108.9 16.5 %collective-permute-start.34 = (bf16[128,256]{1,0:T(8,128)(2,1)S(1)}, bf16[128,256]{1,0:T(8,128)(2,1)S(1)}, u32[]{:S(2)}, u32[]{:S(2)}) collective-permute-start(bf16[128,256]{1,0:T(8,128)(2,1)S(1)} %get-tuple-element.183), channel_id=1, source_target_pairs={{0,16},{16,32},{32,48},{48,0},{1,17},{17,33},{33,49},{49,1},{2,18}... | collective-permute-start | bytes 196616 | tf_op jit(solution)/shard_map/ppermute | solution.py:68
  110.6 16.0 %collective-permute-start.35 = (bf16[128,256]{1,0:T(8,128)(2,1)S(1)}, bf16[128,256]{1,0:T(8,128)(2,1)S(1)}, u32[]{:S(2)}, u32[]{:S(2)}) collective-permute-start(bf16[128,256]{1,0:T(8,128)(2,1)S(1)} %get-tuple-element.182), channel_id=1, source_target_pairs={{0,32},{16,48},{32,0},{48,16},{1,33},{17,49},{33,1},{49,17},{2,34}... | collective-permute-start | bytes 196616 | tf_op jit(solution)/shard_map/ppermute | solution.py:68
  112.1 16.0 %collective-permute-start.36 = (bf16[128,256]{1,0:T(8,128)(2,1)S(1)}, bf16[128,256]{1,0:T(8,128)(2,1)S(1)}, u32[]{:S(2)}, u32[]{:S(2)}) collective-permute-start(bf16[128,256]{1,0:T(8,128)(2,1)S(1)} %get-tuple-element.181), channel_id=1, source_target_pairs={{0,48},{16,0},{32,16},{48,32},{1,49},{17,1},{33,17},{49,33},{2,50}... | collective-permute-start | bytes 196616 | tf_op jit(solution)/shard_map/ppermute | solution.py:68
  128.3 14.8 %collective-permute-start.37 = (f32[128,2]{0,1:T(2,128)S(1)}, f32[128,2]{0,1:T(2,128)S(1)}, u32[]{:S(2)}, u32[]{:S(2)}) collective-permute-start(f32[128,2]{0,1:T(2,128)S(1)} %pad_maximum_fusion.26), channel_id=1, source_target_pairs={{0,16},{16,32},{32,48},{48,0},{1,17},{17,33},{33,49},{49,1},{2,18}... | collective-permute-start | bytes 3080 | tf_op jit(solution)/shard_map/ppermute | solution.py:28
  129.4 15.4 %collective-permute-start.38 = (f32[128,2]{0,1:T(2,128)S(1)}, f32[128,2]{0,1:T(2,128)S(1)}, u32[]{:S(2)}, u32[]{:S(2)}) collective-permute-start(f32[128,2]{0,1:T(2,128)S(1)} %pad_maximum_fusion.26), channel_id=1, source_target_pairs={{0,32},{16,48},{32,0},{48,16},{1,33},{17,49},{33,1},{49,17},{2,34}... | collective-permute-start | bytes 3080 | tf_op jit(solution)/shard_map/ppermute | solution.py:28
  132.5 13.6 %collective-permute-start.39 = (f32[128,2]{0,1:T(2,128)S(1)}, f32[128,2]{0,1:T(2,128)S(1)}, u32[]{:S(2)}, u32[]{:S(2)}) collective-permute-start(f32[128,2]{0,1:T(2,128)S(1)} %pad_maximum_fusion.26), channel_id=1, source_target_pairs={{0,48},{16,0},{32,16},{48,32},{1,49},{17,1},{33,17},{49,33},{2,50}... | collective-permute-start | bytes 3080 | tf_op jit(solution)/shard_map/ppermute | solution.py:28
  134.7 12.8 %collective-permute-start.13 = (bf16[128,256]{1,0:T(8,128)(2,1)S(1)}, bf16[128,256]{1,0:T(8,128)(2,1)S(1)}, u32[]{:S(2)}, u32[]{:S(2)}) collective-permute-start(bf16[128,256]{1,0:T(8,128)(2,1)S(1)} %get-tuple-element.111), channel_id=1, source_target_pairs={{0,64},{16,80},{32,96},{48,112},{1,65},{17,81},{33,97},{49,113},{2... | collective-permute-start | bytes 196616 | tf_op jit(solution)/shard_map/ppermute | solution.py:86
  147.6 9.8 %collective-permute-start.41 = (bf16[128,256]{1,0:T(8,128)(2,1)S(1)}, bf16[128,256]{1,0:T(8,128)(2,1)S(1)}, u32[]{:S(2)}, u32[]{:S(2)}) collective-permute-start(bf16[128,256]{1,0:T(8,128)(2,1)S(1)} %add_convert_fusion.22), channel_id=1, source_target_pairs={{64,16},{80,32},{96,48},{112,0},{65,17},{81,33},{97,49},{113,1},{6... | collective-permute-start | bytes 196616 | tf_op jit(solution)/shard_map/ppermute | solution.py:86
  148.9 10.4 %collective-permute-start.42 = (bf16[128,256]{1,0:T(8,128)(2,1)S(1)}, bf16[128,256]{1,0:T(8,128)(2,1)S(1)}, u32[]{:S(2)}, u32[]{:S(2)}) collective-permute-start(bf16[128,256]{1,0:T(8,128)(2,1)S(1)} %add_convert_fusion.22), channel_id=1, source_target_pairs={{64,32},{80,48},{96,0},{112,16},{65,33},{81,49},{97,1},{113,17},{6... | collective-permute-start | bytes 196616 | tf_op jit(solution)/shard_map/ppermute | solution.py:86
  197.4 19.1 %collective-permute-start.17 = (bf16[128,256]{1,0:T(8,128)(2,1)S(1)}, bf16[128,256]{1,0:T(8,128)(2,1)S(1)}, u32[]{:S(2)}, u32[]{:S(2)}) collective-permute-start(bf16[128,256]{1,0:T(8,128)(2,1)S(1)} %get-tuple-element.200), channel_id=1, source_target_pairs={{0,16},{16,32},{32,48},{48,0},{1,17},{17,33},{33,49},{49,1},{2,18}... | collective-permute-start | bytes 196616 | tf_op jit(solution)/shard_map/ppermute | solution.py:68
  198.1 18.7 %collective-permute-start.18 = (bf16[128,256]{1,0:T(8,128)(2,1)S(1)}, bf16[128,256]{1,0:T(8,128)(2,1)S(1)}, u32[]{:S(2)}, u32[]{:S(2)}) collective-permute-start(bf16[128,256]{1,0:T(8,128)(2,1)S(1)} %get-tuple-element.199), channel_id=1, source_target_pairs={{0,32},{16,48},{32,0},{48,16},{1,33},{17,49},{33,1},{49,17},{2,34}... | collective-permute-start | bytes 196616 | tf_op jit(solution)/shard_map/ppermute | solution.py:68
  226.3 9.8 %collective-permute-start.51 = (bf16[128,256]{1,0:T(8,128)(2,1)S(1)}, bf16[128,256]{1,0:T(8,128)(2,1)S(1)}, u32[]{:S(2)}, u32[]{:S(2)}) collective-permute-start(bf16[128,256]{1,0:T(8,128)(2,1)S(1)} %get-tuple-element.88), channel_id=1, source_target_pairs={{64,16},{80,32},{96,48},{112,0},{65,17},{81,33},{97,49},{113,1},{6... | collective-permute-start | bytes 196616 | tf_op jit(solution)/shard_map/ppermute | solution.py:86
  227.6 10.6 %collective-permute-start.52 = (bf16[128,256]{1,0:T(8,128)(2,1)S(1)}, bf16[128,256]{1,0:T(8,128)(2,1)S(1)}, u32[]{:S(2)}, u32[]{:S(2)}) collective-permute-start(bf16[128,256]{1,0:T(8,128)(2,1)S(1)} %get-tuple-element.88), channel_id=1, source_target_pairs={{64,32},{80,48},{96,0},{112,16},{65,33},{81,49},{97,1},{113,17},{6... | collective-permute-start | bytes 196616 | tf_op jit(solution)/shard_map/ppermute | solution.py:86
  228.9 10.0 %collective-permute-start.53 = (bf16[128,256]{1,0:T(8,128)(2,1)S(1)}, bf16[128,256]{1,0:T(8,128)(2,1)S(1)}, u32[]{:S(2)}, u32[]{:S(2)}) collective-permute-start(bf16[128,256]{1,0:T(8,128)(2,1)S(1)} %get-tuple-element.88), channel_id=1, source_target_pairs={{64,48},{80,0},{96,16},{112,32},{65,49},{81,1},{97,17},{113,33},{6... | collective-permute-start | bytes 196616 | tf_op jit(solution)/shard_map/ppermute | solution.py:86
  278.5 19.3 %collective-permute-start.24 = (bf16[128,256]{1,0:T(8,128)(2,1)S(1)}, bf16[128,256]{1,0:T(8,128)(2,1)S(1)}, u32[]{:S(2)}, u32[]{:S(2)}) collective-permute-start(bf16[128,256]{1,0:T(8,128)(2,1)S(1)} %get-tuple-element.193), channel_id=1, source_target_pairs={{0,16},{16,32},{32,48},{48,0},{1,17},{17,33},{33,49},{49,1},{2,18}... | collective-permute-start | bytes 196616 | tf_op jit(solution)/shard_map/ppermute | solution.py:68
  279.4 18.7 %collective-permute-start.25 = (bf16[128,256]{1,0:T(8,128)(2,1)S(1)}, bf16[128,256]{1,0:T(8,128)(2,1)S(1)}, u32[]{:S(2)}, u32[]{:S(2)}) collective-permute-start(bf16[128,256]{1,0:T(8,128)(2,1)S(1)} %get-tuple-element.192), channel_id=1, source_target_pairs={{0,32},{16,48},{32,0},{48,16},{1,33},{17,49},{33,1},{49,17},{2,34}... | collective-permute-start | bytes 196616 | tf_op jit(solution)/shard_map/ppermute | solution.py:68
  307.6 9.8 %collective-permute-start.61 = (bf16[128,256]{1,0:T(8,128)(2,1)S(1)}, bf16[128,256]{1,0:T(8,128)(2,1)S(1)}, u32[]{:S(2)}, u32[]{:S(2)}) collective-permute-start(bf16[128,256]{1,0:T(8,128)(2,1)S(1)} %get-tuple-element.90), channel_id=1, source_target_pairs={{64,16},{80,32},{96,48},{112,0},{65,17},{81,33},{97,49},{113,1},{6... | collective-permute-start | bytes 196616 | tf_op jit(solution)/shard_map/ppermute | solution.py:86
  308.9 10.7 %collective-permute-start.62 = (bf16[128,256]{1,0:T(8,128)(2,1)S(1)}, bf16[128,256]{1,0:T(8,128)(2,1)S(1)}, u32[]{:S(2)}, u32[]{:S(2)}) collective-permute-start(bf16[128,256]{1,0:T(8,128)(2,1)S(1)} %get-tuple-element.90), channel_id=1, source_target_pairs={{64,32},{80,48},{96,0},{112,16},{65,33},{81,49},{97,1},{113,17},{6... | collective-permute-start | bytes 196616 | tf_op jit(solution)/shard_map/ppermute | solution.py:86
  310.2 10.1 %collective-permute-start.63 = (bf16[128,256]{1,0:T(8,128)(2,1)S(1)}, bf16[128,256]{1,0:T(8,128)(2,1)S(1)}, u32[]{:S(2)}, u32[]{:S(2)}) collective-permute-start(bf16[128,256]{1,0:T(8,128)(2,1)S(1)} %get-tuple-element.90), channel_id=1, source_target_pairs={{64,48},{80,0},{96,16},{112,32},{65,49},{81,1},{97,17},{113,33},{6... | collective-permute-start | bytes 196616 | tf_op jit(solution)/shard_map/ppermute | solution.py:86
  376.7 9.8 %collective-permute-start.71 = (bf16[128,256]{1,0:T(8,128)(2,1)S(1)}, bf16[128,256]{1,0:T(8,128)(2,1)S(1)}, u32[]{:S(2)}, u32[]{:S(2)}) collective-permute-start(bf16[128,256]{1,0:T(8,128)(2,1)S(1)} %get-tuple-element.92), channel_id=1, source_target_pairs={{64,16},{80,32},{96,48},{112,0},{65,17},{81,33},{97,49},{113,1},{6... | collective-permute-start | bytes 196616 | tf_op jit(solution)/shard_map/ppermute | solution.py:86
  378.0 10.7 %collective-permute-start.72 = (bf16[128,256]{1,0:T(8,128)(2,1)S(1)}, bf16[128,256]{1,0:T(8,128)(2,1)S(1)}, u32[]{:S(2)}, u32[]{:S(2)}) collective-permute-start(bf16[128,256]{1,0:T(8,128)(2,1)S(1)} %get-tuple-element.92), channel_id=1, source_target_pairs={{64,32},{80,48},{96,0},{112,16},{65,33},{81,49},{97,1},{113,17},{6... | collective-permute-start | bytes 196616 | tf_op jit(solution)/shard_map/ppermute | solution.py:86
  379.3 10.1 %collective-permute-start.73 = (bf16[128,256]{1,0:T(8,128)(2,1)S(1)}, bf16[128,256]{1,0:T(8,128)(2,1)S(1)}, u32[]{:S(2)}, u32[]{:S(2)}) collective-permute-start(bf16[128,256]{1,0:T(8,128)(2,1)S(1)} %get-tuple-element.92), channel_id=1, source_target_pairs={{64,48},{80,0},{96,16},{112,32},{65,49},{81,1},{97,17},{113,33},{6... | collective-permute-start | bytes 196616 | tf_op jit(solution)/shard_map/ppermute | solution.py:86
  564.3 20.0 %collective-permute-start.80 = (f32[4096]{0:T(1024)S(1)}, f32[4096]{0:T(1024)S(1)}, u32[]{:S(2)}, u32[]{:S(2)}) collective-permute-start(f32[4096]{0:T(1024)S(1)} %bitcast.681), channel_id=1, source_target_pairs={{0,16},{16,32},{32,48},{48,0},{1,17},{17,33},{33,49},{49,1},{2,18}... | collective-permute-start | bytes 49160 | tf_op jit(solution)/shard_map/ppermute | solution.py:28
  565.9 18.3 %collective-permute-start.81 = (f32[4096]{0:T(1024)S(1)}, f32[4096]{0:T(1024)S(1)}, u32[]{:S(2)}, u32[]{:S(2)}) collective-permute-start(f32[4096]{0:T(1024)S(1)} %bitcast.682), channel_id=1, source_target_pairs={{0,32},{16,48},{32,0},{48,16},{1,33},{17,49},{33,1},{49,17},{2,34}... | collective-permute-start | bytes 49160 | tf_op jit(solution)/shard_map/ppermute | solution.py:28
  568.8 15.5 %collective-permute-start.82 = (f32[4096]{0:T(1024)S(1)}, f32[4096]{0:T(1024)S(1)}, u32[]{:S(2)}, u32[]{:S(2)}) collective-permute-start(f32[4096]{0:T(1024)S(1)} %bitcast.683), channel_id=1, source_target_pairs={{0,48},{16,0},{32,16},{48,32},{1,49},{17,1},{33,17},{49,33},{2,50}... | collective-permute-start | bytes 49160 | tf_op jit(solution)/shard_map/ppermute | solution.py:28
  (308 other events, 2312.3 us)
Sparse Core Ops, SparseCore 0:
  425.6 134.3 all-reduce.2

commit v7 on v5

--- a/solution.py
+++ b/solution.py
@@ -438,14 +438,23 @@
     small_rows = totals[4][0]
     small_pad = (-small_rows.shape[0]) % model_width
     small_rows = jnp.pad(small_rows, (0, small_pad)).reshape(-1, model_width)
-    pieces = (totals[0][0], totals[1][0], totals[2][0], totals[3][0], small_rows)
-    slab = jnp.concatenate([piece.astype(jnp.bfloat16) for piece in pieces], axis=0)
-    slab = lax.psum(slab, "dp").astype(jnp.float32)
-    summed = []
-    offset = 0
-    for piece in pieces:
-        summed.append(slab[offset : offset + piece.shape[0]])
-        offset = offset + piece.shape[0]
+    early = jnp.concatenate(
+        [totals[1][0], totals[2][0], totals[3][0]], axis=0
+    ).astype(jnp.bfloat16)
+    early = lax.psum(early, "dp").astype(jnp.float32)
+    late = jnp.concatenate([totals[0][0], small_rows], axis=0).astype(jnp.bfloat16)
+    late = late + (early[0:1, 0:1] * 0).astype(jnp.bfloat16)
+    late = lax.psum(late, "dp").astype(jnp.float32)
+    dense_rows = totals[1].shape[1]
+    up_rows = totals[2].shape[1]
+    joined_rows = totals[0].shape[1]
+    summed = [
+        late[:joined_rows],
+        early[:dense_rows],
+        early[dense_rows : dense_rows + up_rows],
+        early[dense_rows + up_rows :],
+        late[joined_rows:],
+    ]
     grad_rows_all = jnp.concatenate(
         [jnp.where(leading, tick_grads[block + 1], tick_grads[block]) for block in range(NMB)],
         axis=0,

time: 439 us -> 549 us (1.25)
  waiting for transfers between devices: 165 us -> 260 us
  other arithmetic: 29 us -> 39.3 us
    psum x1 -> x2, waiting for transfers between devices: 108 us -> 214 us  [the longest x1 111 us: per_device(): late = lax.psum(late, 'dp').astype(jnp.float32)]
    ppermute x15, waiting for transfers between devices: 19.8 us -> 12.3 us  [tensor_pieces(): parts.append(lax.ppermute(x, 'tensor', pairs))]
    unnamed x347 -> x331, local copies, waits for them, and re-layouts: 18.2 us -> 21.1 us
  transfers between devices with their start and end apart: 50 -> 51, of which waited for: 28 -> 23; matrix products, arithmetic and copies ran while one was open for 10% -> 12% of each run, Pallas kernels for 0% -> 0%
where the time goes in v7:
time: 549 us; the launch traced here: 540 us
  waiting for transfers between devices  260 us (47%)
  matrix products  77 us (14%)
  starting transfers between devices  75.7 us (14%)
  local copies, waits for them, and re-layouts  70.5 us (13%)
  other arithmetic  39.3 us (7%)
  between operations  18 us (3%)
    psum x1, waiting for transfers between devices, per_device(): late = lax.psum(late, 'dp').astype(jnp.float32)  111 us
    psum x1, waiting for transfers between devices, per_device(): early = lax.psum(early, 'dp').astype(jnp.float32)  103 us
    ppermute x16, starting transfers between devices, cross_gather(): parts.append(lax.ppermute(x, ('pipe', 'tensor'), pairs))  34.7 us
    dot_general x12, matrix products, contract_rows(): lax.dot_general(left, right, (((0,), (0,)), ((), ())), preferred_element_...  31 us
    unnamed x331, local copies, waits for them, and re-layouts  21.1 us
    dot_general x12, matrix products, contract_cols(): lax.dot_general(left, right, (((1,), (1,)), ((), ())), preferred_element_...  21 us
    ppermute x18, starting transfers between devices, tensor_scatter_sum(): parts.append(lax.ppermute(piece_for((me + shift) % peers), 'tensor', pairs))  21 us
    ppermute x15, starting transfers between devices, tensor_pieces(): parts.append(lax.ppermute(x, 'tensor', pairs))  19.9 us
  transfers between devices with their start and end apart: 51, of which 23 were waited for; matrix products, arithmetic and copies ran while one was open for 12% of the time, Pallas kernels for 0%

profile of v7, /device:TPU:0, one launch (start us, length us, event | category | flops | bytes accessed | tf_op | source)
XLA Modules:
  0.0 540.1 jit_solution(13978016352806071405)
XLA Ops:
  9.3 4.2 collective-permute-start.2
  20.9 2.6 copy.125
  26.4 9.6 %collective-permute-done.2 = bf16[1024,256]{1,0:T(8,128)(2,1)S(1)} collective-permute-done((bf16[1024,256]{1,0:T(8,128)(2,1)S(1)}, bf16[1024,256]{1,0:T(8,128)(2,1)S(1)}, u32[]{:S(2)}, u32[]{:S(2)}) %collective-permute-start.2) | collective-permute-done | bytes 524320 | tf_op jit(solution)/shard_map/ppermute | solution.py:28
  36.7 2.7 collective-permute-done
  46.0 3.8 fusion.60
  54.7 3.3 collective-permute-done.5
  61.2 5.5 %collective-permute-start.9 = (bf16[256,256]{1,0:T(8,128)(2,1)S(1)}, bf16[256,256]{1,0:T(8,128)(2,1)S(1)}, u32[]{:S(2)}, u32[]{:S(2)}) collective-permute-start(bf16[256,256]{1,0:T(8,128)(2,1)S(1)} %add_convert_fusion.17), channel_id=1, source_target_pairs={{0,112},{16,64},{32,80},{48,96},{1,113},{17,65},{33,81},{49,97},{2... | collective-permute-start | bytes 393224 | tf_op jit(solution)/shard_map/ppermute | solution.py:86
  96.4 2.9 fusion.63
  99.4 2.6 fusion.152
  103.1 2.8 fusion.142
  106.0 4.2 convert_reduce_fusion.2
  110.2 3.1 fusion.147
  118.3 3.3 collective-permute-start.12
  123.5 3.0 collective-permute-done.20
  130.5 8.4 %collective-permute-start.16 = (bf16[256,256]{1,0:T(8,128)(2,1)S(1)}, bf16[256,256]{1,0:T(8,128)(2,1)S(1)}, u32[]{:S(2)}, u32[]{:S(2)}) collective-permute-start(bf16[256,256]{1,0:T(8,128)(2,1)S(1)} %get-tuple-element.75), channel_id=1, source_target_pairs={{0,112},{16,64},{32,80},{48,96},{1,113},{17,65},{33,81},{49,97},{2... | collective-permute-start | bytes 393224 | tf_op jit(solution)/shard_map/ppermute | solution.py:86
  150.0 5.2 collective-permute-done.29
  183.1 2.9 fusion.66
  186.1 2.7 fusion.150
  190.0 2.8 fusion.140
  194.0 3.4 convert_reduce_fusion.1
  197.4 3.1 fusion.145
  234.9 2.8 collective-permute-done.38
  239.6 5.3 convert_reduce_fusion
  251.5 4.4 add_convert_fusion
  275.7 5.0 add_convert_fusion.2
  288.0 102.6 %all-reduce.4.cloned.1.call-done = bf16[2304,1024]{1,0:T(8,128)(2,1)} async-done(((bf16[2304,1024]{1,0:T(8,128)(2,1)}), bf16[2304,1024]{1,0:T(8,128)(2,1)}) %all-reduce.4.cloned.1.call-update) | async-done | bytes 4718608 | tf_op jit(solution)/shard_map/psum | solution.py:444
  392.6 3.0 maximum_add_fusion
  397.6 3.5 convert_element_type.500
  402.1 4.2 slice_bitcast_fusion
  406.4 111.0 %all-reduce.6.cloned.1.call-done = bf16[776,1024]{1,0:T(8,128)(2,1)} async-done(((bf16[776,1024]{1,0:T(8,128)(2,1)}), bf16[776,1024]{1,0:T(8,128)(2,1)}) %all-reduce.6.cloned.1.call-update) | async-done | bytes 1589264 | tf_op jit(solution)/shard_map/psum | solution.py:447
  519.4 3.0 collective-permute-start.48
  527.3 3.5 copy.198
  (627 shorter events, 191.3 us)
Async XLA Ops:
  7.2 383.5 %all-reduce.4.cloned.1.call-start = ((), (), s32[]{:S(2)}) async-start(), calls=%async_computation | async-start | bytes 9437184 | tf_op jit(solution)/shard_map/psum | solution.py:444
  9.3 26.6 %collective-permute-start.2 = (bf16[1024,256]{1,0:T(8,128)(2,1)S(1)}, bf16[1024,256]{1,0:T(8,128)(2,1)S(1)}, u32[]{:S(2)}, u32[]{:S(2)}) collective-permute-start(bf16[1024,256]{1,0:T(8,128)(2,1)S(1)} %constant_dynamic-update-slice_fusion), channel_id=1, source_target_pairs={{0,48},{16,0},{32,16},{48,32},{1,49},{17,1},{33,17},{49,33},{2,50}... | collective-permute-start | bytes 1572872 | tf_op jit(solution)/shard_map/ppermute | solution.py:28
  13.5 22.4 %collective-permute-start.1 = (bf16[1024,256]{1,0:T(8,128)(2,1)S(1)}, bf16[1024,256]{1,0:T(8,128)(2,1)}, u32[]{:S(2)}, u32[]{:S(2)}) collective-permute-start(bf16[1024,256]{1,0:T(8,128)(2,1)S(1)} %constant_dynamic-update-slice_fusion), channel_id=1, source_target_pairs={{0,32},{16,48},{32,0},{48,16},{1,33},{17,49},{33,1},{49,17},{2,34}... | collective-permute-start | bytes 1572872 | tf_op jit(solution)/shard_map/ppermute | solution.py:28
  13.5 25.9 %collective-permute-start = (bf16[1024,256]{1,0:T(8,128)(2,1)S(1)}, bf16[1024,256]{1,0:T(8,128)(2,1)}, u32[]{:S(2)}, u32[]{:S(2)}) collective-permute-start(bf16[1024,256]{1,0:T(8,128)(2,1)S(1)} %constant_dynamic-update-slice_fusion), channel_id=1, source_target_pairs={{0,16},{16,32},{32,48},{48,0},{1,17},{17,33},{33,49},{49,1},{2,18}... | collective-permute-start | bytes 1572872 | tf_op jit(solution)/shard_map/ppermute | solution.py:28
  52.7 8.3 %collective-permute-start.3 = (bf16[256,256]{1,0:T(8,128)(2,1)S(1)}, bf16[256,256]{1,0:T(8,128)(2,1)S(1)}, u32[]{:S(2)}, u32[]{:S(2)}) collective-permute-start(bf16[256,256]{1,0:T(8,128)(2,1)S(1)} %get-tuple-element.132), channel_id=1, source_target_pairs={{0,16},{16,32},{32,48},{48,0},{1,17},{17,33},{33,49},{49,1},{2,18}... | collective-permute-start | bytes 393224 | tf_op jit(solution)/shard_map/ppermute | solution.py:68
  61.2 12.9 %collective-permute-start.9 = (bf16[256,256]{1,0:T(8,128)(2,1)S(1)}, bf16[256,256]{1,0:T(8,128)(2,1)S(1)}, u32[]{:S(2)}, u32[]{:S(2)}) collective-permute-start(bf16[256,256]{1,0:T(8,128)(2,1)S(1)} %add_convert_fusion.17), channel_id=1, source_target_pairs={{0,112},{16,64},{32,80},{48,96},{1,113},{17,65},{33,81},{49,97},{2... | collective-permute-start | bytes 393224 | tf_op jit(solution)/shard_map/ppermute | solution.py:86
  117.9 8.6 %collective-permute-start.20 = (bf16[256,256]{1,0:T(8,128)(2,1)S(1)}, bf16[256,256]{1,0:T(8,128)(2,1)S(1)}, u32[]{:S(2)}, u32[]{:S(2)}) collective-permute-start(bf16[256,256]{1,0:T(8,128)(2,1)S(1)} %get-tuple-element.115), channel_id=1, source_target_pairs={{0,16},{16,32},{32,48},{48,0},{1,17},{17,33},{33,49},{49,1},{2,18}... | collective-permute-start | bytes 393224 | tf_op jit(solution)/shard_map/ppermute | solution.py:68
  118.3 11.0 %collective-permute-start.12 = (bf16[256,256]{1,0:T(8,128)(2,1)S(1)}, bf16[256,256]{1,0:T(8,128)(2,1)S(1)}, u32[]{:S(2)}, u32[]{:S(2)}) collective-permute-start(bf16[256,256]{1,0:T(8,128)(2,1)S(1)} %get-tuple-element.123), channel_id=1, source_target_pairs={{0,48},{16,0},{32,16},{48,32},{1,49},{17,1},{33,17},{49,33},{2,50}... | collective-permute-start | bytes 393224 | tf_op jit(solution)/shard_map/ppermute | solution.py:68
  126.8 13.9 %collective-permute-start.25 = (f32[256,2]{0,1:T(2,128)S(1)}, f32[256,2]{0,1:T(2,128)S(1)}, u32[]{:S(2)}, u32[]{:S(2)}) collective-permute-start(f32[256,2]{0,1:T(2,128)S(1)} %pad_maximum_fusion.11), channel_id=1, source_target_pairs={{0,48},{16,0},{32,16},{48,32},{1,49},{17,1},{33,17},{49,33},{2,50}... | collective-permute-start | bytes 6152 | tf_op jit(solution)/shard_map/ppermute | solution.py:28
  126.9 15.0 %collective-permute-start.24 = (f32[256,2]{0,1:T(2,128)S(1)}, f32[256,2]{0,1:T(2,128)S(1)}, u32[]{:S(2)}, u32[]{:S(2)}) collective-permute-start(f32[256,2]{0,1:T(2,128)S(1)} %pad_maximum_fusion.11), channel_id=1, source_target_pairs={{0,32},{16,48},{32,0},{48,16},{1,33},{17,49},{33,1},{49,17},{2,34}... | collective-permute-start | bytes 6152 | tf_op jit(solution)/shard_map/ppermute | solution.py:28
  129.3 14.0 %collective-permute-start.23 = (f32[256,2]{0,1:T(2,128)S(1)}, f32[256,2]{0,1:T(2,128)S(1)}, u32[]{:S(2)}, u32[]{:S(2)}) collective-permute-start(f32[256,2]{0,1:T(2,128)S(1)} %pad_maximum_fusion.11), channel_id=1, source_target_pairs={{0,16},{16,32},{32,48},{48,0},{1,17},{17,33},{33,49},{49,1},{2,18}... | collective-permute-start | bytes 6152 | tf_op jit(solution)/shard_map/ppermute | solution.py:28
  130.5 15.3 %collective-permute-start.16 = (bf16[256,256]{1,0:T(8,128)(2,1)S(1)}, bf16[256,256]{1,0:T(8,128)(2,1)S(1)}, u32[]{:S(2)}, u32[]{:S(2)}) collective-permute-start(bf16[256,256]{1,0:T(8,128)(2,1)S(1)} %get-tuple-element.75), channel_id=1, source_target_pairs={{0,112},{16,64},{32,80},{48,96},{1,113},{17,65},{33,81},{49,97},{2... | collective-permute-start | bytes 393224 | tf_op jit(solution)/shard_map/ppermute | solution.py:86
  138.9 8.2 %collective-permute-start.15 = (bf16[256,256]{1,0:T(8,128)(2,1)S(1)}, bf16[256,256]{1,0:T(8,128)(2,1)S(1)}, u32[]{:S(2)}, u32[]{:S(2)}) collective-permute-start(bf16[256,256]{1,0:T(8,128)(2,1)S(1)} %get-tuple-element.75), channel_id=1, source_target_pairs={{0,96},{16,112},{32,64},{48,80},{1,97},{17,113},{33,65},{49,81},{2... | collective-permute-start | bytes 393224 | tf_op jit(solution)/shard_map/ppermute | solution.py:86
  144.5 10.7 %collective-permute-start.29 = (bf16[256,256]{1,0:T(8,128)(2,1)S(1)}, bf16[256,256]{1,0:T(8,128)(2,1)S(1)}, u32[]{:S(2)}, u32[]{:S(2)}) collective-permute-start(bf16[256,256]{1,0:T(8,128)(2,1)S(1)} %add_convert_fusion.14), channel_id=1, source_target_pairs={{64,48},{80,0},{96,16},{112,32},{65,49},{81,1},{97,17},{113,33},{6... | collective-permute-start | bytes 393224 | tf_op jit(solution)/shard_map/ppermute | solution.py:86
  145.8 11.4 %collective-permute-start.28 = (bf16[256,256]{1,0:T(8,128)(2,1)S(1)}, bf16[256,256]{1,0:T(8,128)(2,1)S(1)}, u32[]{:S(2)}, u32[]{:S(2)}) collective-permute-start(bf16[256,256]{1,0:T(8,128)(2,1)S(1)} %add_convert_fusion.14), channel_id=1, source_target_pairs={{64,32},{80,48},{96,0},{112,16},{65,33},{81,49},{97,1},{113,17},{6... | collective-permute-start | bytes 393224 | tf_op jit(solution)/shard_map/ppermute | solution.py:86
  147.1 11.6 %collective-permute-start.27 = (bf16[256,256]{1,0:T(8,128)(2,1)S(1)}, bf16[256,256]{1,0:T(8,128)(2,1)S(1)}, u32[]{:S(2)}, u32[]{:S(2)}) collective-permute-start(bf16[256,256]{1,0:T(8,128)(2,1)S(1)} %add_convert_fusion.14), channel_id=1, source_target_pairs={{64,16},{80,32},{96,48},{112,0},{65,17},{81,33},{97,49},{113,1},{6... | collective-permute-start | bytes 393224 | tf_op jit(solution)/shard_map/ppermute | solution.py:86
  148.4 11.1 %collective-permute-start.26 = (bf16[256,256]{1,0:T(8,128)(2,1)S(1)}, bf16[256,256]{1,0:T(8,128)(2,1)S(1)}, u32[]{:S(2)}, u32[]{:S(2)}) collective-permute-start(bf16[256,256]{1,0:T(8,128)(2,1)S(1)} %add_convert_fusion.14), channel_id=1, source_target_pairs={{64,0},{80,16},{96,32},{112,48},{65,1},{81,17},{97,33},{113,49},{6... | collective-permute-start | bytes 393224 | tf_op jit(solution)/shard_map/ppermute | solution.py:86
  214.8 8.6 %collective-permute-start.35 = (f32[256,2]{0,1:T(2,128)S(1)}, f32[256,2]{0,1:T(2,128)S(1)}, u32[]{:S(2)}, u32[]{:S(2)}) collective-permute-start(f32[256,2]{0,1:T(2,128)S(1)} %pad_maximum_fusion.12), channel_id=1, source_target_pairs={{0,48},{16,0},{32,16},{48,32},{1,49},{17,1},{33,17},{49,33},{2,50}... | collective-permute-start | bytes 6152 | tf_op jit(solution)/shard_map/ppermute | solution.py:28
  215.4 9.3 %collective-permute-start.34 = (f32[256,2]{0,1:T(2,128)S(1)}, f32[256,2]{0,1:T(2,128)S(1)}, u32[]{:S(2)}, u32[]{:S(2)}) collective-permute-start(f32[256,2]{0,1:T(2,128)S(1)} %pad_maximum_fusion.12), channel_id=1, source_target_pairs={{0,32},{16,48},{32,0},{48,16},{1,33},{17,49},{33,1},{49,17},{2,34}... | collective-permute-start | bytes 6152 | tf_op jit(solution)/shard_map/ppermute | solution.py:28
  223.3 9.8 %collective-permute-start.17 = (bf16[256,256]{1,0:T(8,128)(2,1)S(1)}, bf16[256,256]{1,0:T(8,128)(2,1)S(1)}, u32[]{:S(2)}, u32[]{:S(2)}) collective-permute-start(bf16[256,256]{1,0:T(8,128)(2,1)S(1)} %get-tuple-element.118), channel_id=1, source_target_pairs={{0,16},{16,32},{32,48},{48,0},{1,17},{17,33},{33,49},{49,1},{2,18}... | collective-permute-start | bytes 393224 | tf_op jit(solution)/shard_map/ppermute | solution.py:68
  225.6 9.3 %collective-permute-start.39 = (bf16[256,256]{1,0:T(8,128)(2,1)S(1)}, bf16[256,256]{1,0:T(8,128)(2,1)S(1)}, u32[]{:S(2)}, u32[]{:S(2)}) collective-permute-start(bf16[256,256]{1,0:T(8,128)(2,1)S(1)} %get-tuple-element.70), channel_id=1, source_target_pairs={{64,48},{80,0},{96,16},{112,32},{65,49},{81,1},{97,17},{113,33},{6... | collective-permute-start | bytes 393224 | tf_op jit(solution)/shard_map/ppermute | solution.py:86
  226.9 10.8 %collective-permute-start.38 = (bf16[256,256]{1,0:T(8,128)(2,1)S(1)}, bf16[256,256]{1,0:T(8,128)(2,1)S(1)}, u32[]{:S(2)}, u32[]{:S(2)}) collective-permute-start(bf16[256,256]{1,0:T(8,128)(2,1)S(1)} %get-tuple-element.70), channel_id=1, source_target_pairs={{64,32},{80,48},{96,0},{112,16},{65,33},{81,49},{97,1},{113,17},{6... | collective-permute-start | bytes 393224 | tf_op jit(solution)/shard_map/ppermute | solution.py:86
  228.2 11.2 %collective-permute-start.37 = (bf16[256,256]{1,0:T(8,128)(2,1)S(1)}, bf16[256,256]{1,0:T(8,128)(2,1)S(1)}, u32[]{:S(2)}, u32[]{:S(2)}) collective-permute-start(bf16[256,256]{1,0:T(8,128)(2,1)S(1)} %get-tuple-element.70), channel_id=1, source_target_pairs={{64,16},{80,32},{96,48},{112,0},{65,17},{81,33},{97,49},{113,1},{6... | collective-permute-start | bytes 393224 | tf_op jit(solution)/shard_map/ppermute | solution.py:86
  229.5 9.9 %collective-permute-start.36 = (bf16[256,256]{1,0:T(8,128)(2,1)S(1)}, bf16[256,256]{1,0:T(8,128)(2,1)S(1)}, u32[]{:S(2)}, u32[]{:S(2)}) collective-permute-start(bf16[256,256]{1,0:T(8,128)(2,1)S(1)} %get-tuple-element.70), channel_id=1, source_target_pairs={{64,0},{80,16},{96,32},{112,48},{65,1},{81,17},{97,33},{113,49},{6... | collective-permute-start | bytes 393224 | tf_op jit(solution)/shard_map/ppermute | solution.py:86
  261.0 256.4 %all-reduce.6.cloned.1.call-start = ((), (), s32[]{:S(2)}) async-start(), calls=%async_computation.1 | async-start | bytes 3178496 | tf_op jit(solution)/shard_map/psum | solution.py:447
  272.1 9.8 %collective-permute-start.42 = (bf16[256,256]{1,0:T(8,128)(2,1)S(1)}, bf16[256,256]{1,0:T(8,128)(2,1)S(1)}, u32[]{:S(2)}, u32[]{:S(2)}) collective-permute-start(bf16[256,256]{1,0:T(8,128)(2,1)S(1)} %get-tuple-element.99), channel_id=1, source_target_pairs={{0,48},{16,0},{32,16},{48,32},{1,49},{17,1},{33,17},{49,33},{2,50}... | collective-permute-start | bytes 393224 | tf_op jit(solution)/shard_map/ppermute | solution.py:68
  283.9 111.7 %collective-permute-start.45 = (f32[256,2]{0,1:T(2,128)S(1)}, f32[256,2]{0,1:T(2,128)S(1)}, u32[]{:S(2)}, u32[]{:S(2)}) collective-permute-start(f32[256,2]{0,1:T(2,128)S(1)} %pad_maximum_fusion.13), channel_id=1, source_target_pairs={{0,48},{16,0},{32,16},{48,32},{1,49},{17,1},{33,17},{49,33},{2,50}... | collective-permute-start | bytes 6152 | tf_op jit(solution)/shard_map/ppermute | solution.py:28
  285.8 109.8 %collective-permute-start.44 = (f32[256,2]{0,1:T(2,128)S(1)}, f32[256,2]{0,1:T(2,128)S(1)}, u32[]{:S(2)}, u32[]{:S(2)}) collective-permute-start(f32[256,2]{0,1:T(2,128)S(1)} %pad_maximum_fusion.13), channel_id=1, source_target_pairs={{0,32},{16,48},{32,0},{48,16},{1,33},{17,49},{33,1},{49,17},{2,34}... | collective-permute-start | bytes 6152 | tf_op jit(solution)/shard_map/ppermute | solution.py:28
  287.8 107.8 %collective-permute-start.43 = (f32[256,2]{0,1:T(2,128)S(1)}, f32[256,2]{0,1:T(2,128)S(1)}, u32[]{:S(2)}, u32[]{:S(2)}) collective-permute-start(f32[256,2]{0,1:T(2,128)S(1)} %pad_maximum_fusion.13), channel_id=1, source_target_pairs={{0,16},{16,32},{32,48},{48,0},{1,17},{17,33},{33,49},{49,1},{2,18}... | collective-permute-start | bytes 6152 | tf_op jit(solution)/shard_map/ppermute | solution.py:28
  519.4 12.1 %collective-permute-start.48 = (f32[4096]{0:T(1024)S(1)}, f32[4096]{0:T(1024)S(1)}, u32[]{:S(2)}, u32[]{:S(2)}) collective-permute-start(f32[4096]{0:T(1024)S(1)} %bitcast.529), channel_id=1, source_target_pairs={{0,48},{16,0},{32,16},{48,32},{1,49},{17,1},{33,17},{49,33},{2,50}... | collective-permute-start | bytes 49160 | tf_op jit(solution)/shard_map/ppermute | solution.py:28
  522.4 9.0 %collective-permute-start.47 = (f32[4096]{0:T(1024)S(1)}, f32[4096]{0:T(1024)S(1)}, u32[]{:S(2)}, u32[]{:S(2)}) collective-permute-start(f32[4096]{0:T(1024)S(1)} %bitcast.530), channel_id=1, source_target_pairs={{0,32},{16,48},{32,0},{48,16},{1,33},{17,49},{33,1},{49,17},{2,34}... | collective-permute-start | bytes 49160 | tf_op jit(solution)/shard_map/ppermute | solution.py:28
  523.1 8.4 %collective-permute-start.46 = (f32[4096]{0:T(1024)S(1)}, f32[4096]{0:T(1024)S(1)}, u32[]{:S(2)}, u32[]{:S(2)}) collective-permute-start(f32[4096]{0:T(1024)S(1)} %bitcast.531), channel_id=1, source_target_pairs={{0,16},{16,32},{32,48},{48,0},{1,17},{17,33},{33,49},{49,1},{2,18}... | collective-permute-start | bytes 49160 | tf_op jit(solution)/shard_map/ppermute | solution.py:28
  (163 other events, 939.8 us)
Sparse Core Ops, SparseCore 0:
  261.1 129.5 all-reduce.3
  395.7 121.7 all-reduce.5

commit v8 on v5

--- a/solution.py
+++ b/solution.py
@@ -398,21 +398,20 @@
             [jnp.sum(d_hattn * normed, axis=0), jnp.sum(d_hmlp * normed, axis=0)]
         )
         grad_shifts = jnp.concatenate([jnp.sum(d_hattn, axis=0), jnp.sum(d_hmlp, axis=0)])
-        d_norm = tensor_scatter_sum(
-            (d_hattn * ln_gains[0] + d_hmlp * ln_gains[1]).astype(jnp.bfloat16)
-        )
-        column_start = lax.axis_index("tensor") * quarter
-        own_normed = lax.dynamic_slice_in_dim(normed, column_start, quarter, 1)
-        own_grad = lax.dynamic_slice_in_dim(grad_wide, column_start, quarter, 1)
+        d_norm_part = d_hattn * ln_gains[0] + d_hmlp * ln_gains[1]
         row_stats = tensor_sum(
             jnp.concatenate(
                 [
-                    jnp.sum(d_norm, axis=1, keepdims=True),
-                    jnp.sum(d_norm * own_normed, axis=1, keepdims=True),
+                    jnp.sum(d_norm_part, axis=1, keepdims=True),
+                    jnp.sum(d_norm_part * normed, axis=1, keepdims=True),
                 ],
                 axis=1,
             )
         ) / model_width
+        d_norm = tensor_scatter_sum(d_norm_part.astype(jnp.bfloat16))
+        column_start = lax.axis_index("tensor") * quarter
+        own_normed = lax.dynamic_slice_in_dim(normed, column_start, quarter, 1)
+        own_grad = lax.dynamic_slice_in_dim(grad_wide, column_start, quarter, 1)
         grad_input = own_grad + inv_scale * (
             d_norm - row_stats[:, 0:1] - own_normed * row_stats[:, 1:2]
         )

time: 439 us -> 443 us (level)
  other arithmetic: 29 us -> 34 us
  starting transfers between devices: 73.7 us -> 78.2 us
    ppermute x18, waiting for transfers between devices: 16.8 us -> 30 us  [tensor_scatter_sum(): parts.append(lax.ppermute(piece_for((me + shift) % peers), 'tensor', pairs))]
    ppermute x15, waiting for transfers between devices: 19.8 us -> 12.4 us  [tensor_pieces(): parts.append(lax.ppermute(x, 'tensor', pairs))]
    psum x1, waiting for transfers between devices: 108 us -> 102 us  [per_device(): slab = lax.psum(slab, 'dp').astype(jnp.float32)]
  transfers between devices with their start and end apart: 50 -> 50, of which waited for: 28 -> 25; matrix products, arithmetic and copies ran while one was open for 10% -> 13% of each run, Pallas kernels for 0% -> 0%
where the time goes in v8:
time: 443 us; the launch traced here: 434 us
  waiting for transfers between devices  163 us (37%)
  starting transfers between devices  78.2 us (18%)
  matrix products  76.1 us (17%)
  local copies, waits for them, and re-layouts  65.6 us (15%)
  other arithmetic  34 us (8%)
  between operations  17.4 us (4%)
    psum x1, waiting for transfers between devices, per_device(): slab = lax.psum(slab, 'dp').astype(jnp.float32)  102 us
    ppermute x16, starting transfers between devices, cross_gather(): parts.append(lax.ppermute(x, ('pipe', 'tensor'), pairs))  34.3 us
    dot_general x12, matrix products, contract_rows(): lax.dot_general(left, right, (((0,), (0,)), ((), ())), preferred_element_...  30.6 us
    ppermute x18, waiting for transfers between devices, tensor_scatter_sum(): parts.append(lax.ppermute(piece_for((me + shift) % peers), 'tensor', pairs))  30 us
    ppermute x18, starting transfers between devices, tensor_scatter_sum(): parts.append(lax.ppermute(piece_for((me + shift) % peers), 'tensor', pairs))  23.9 us
    ppermute x15, starting transfers between devices, tensor_pieces(): parts.append(lax.ppermute(x, 'tensor', pairs))  20 us
    dot_general x12, matrix products, contract_cols(): lax.dot_general(left, right, (((1,), (1,)), ((), ())), preferred_element_...  18.8 us
    ppermute x16, waiting for transfers between devices, cross_gather(): parts.append(lax.ppermute(x, ('pipe', 'tensor'), pairs))  18.1 us
  transfers between devices with their start and end apart: 50, of which 25 were waited for; matrix products, arithmetic and copies ran while one was open for 13% of the time, Pallas kernels for 0%

profile of v8, /device:TPU:0, one launch (start us, length us, event | category | flops | bytes accessed | tf_op | source)
XLA Modules:
  0.0 434.0 jit_solution(3249436539675575019)
XLA Ops:
  9.3 4.2 collective-permute-start.2
  26.3 9.6 %collective-permute-done.2 = bf16[1024,256]{1,0:T(8,128)(2,1)S(1)} collective-permute-done((bf16[1024,256]{1,0:T(8,128)(2,1)S(1)}, bf16[1024,256]{1,0:T(8,128)(2,1)S(1)}, u32[]{:S(2)}, u32[]{:S(2)}) %collective-permute-start.2) | collective-permute-done | bytes 524320 | tf_op jit(solution)/shard_map/ppermute | solution.py:28
  36.7 2.7 collective-permute-done
  46.0 3.9 fusion.64
  54.7 3.3 collective-permute-done.5
  61.3 5.5 %collective-permute-start.9 = (bf16[256,256]{1,0:T(8,128)(2,1)S(1)}, bf16[256,256]{1,0:T(8,128)(2,1)S(1)}, u32[]{:S(2)}, u32[]{:S(2)}) collective-permute-start(bf16[256,256]{1,0:T(8,128)(2,1)S(1)} %add_convert_fusion.14), channel_id=1, source_target_pairs={{0,112},{16,64},{32,80},{48,96},{1,113},{17,65},{33,81},{49,97},{2... | collective-permute-start | bytes 393224 | tf_op jit(solution)/shard_map/ppermute | solution.py:86
  96.3 2.9 fusion.67
  99.3 3.8 convert_reduce_fusion.2
  111.1 3.1 fusion.151
  115.2 2.8 fusion.146
  118.6 3.3 collective-permute-start.12
  133.1 6.9 %collective-permute-start.16 = (bf16[256,256]{1,0:T(8,128)(2,1)S(1)}, bf16[256,256]{1,0:T(8,128)(2,1)S(1)}, u32[]{:S(2)}, u32[]{:S(2)}) collective-permute-start(bf16[256,256]{1,0:T(8,128)(2,1)S(1)} %get-tuple-element.78), channel_id=1, source_target_pairs={{0,112},{16,64},{32,80},{48,96},{1,113},{17,65},{33,81},{49,97},{2... | collective-permute-start | bytes 393224 | tf_op jit(solution)/shard_map/ppermute | solution.py:86
  140.0 2.7 collective-permute-start.15
  152.1 3.8 collective-permute-done.29
  155.9 3.2 collective-permute-done.28
  182.0 2.9 fusion.70
  185.2 3.2 convert_reduce_fusion.1
  198.0 3.1 fusion.149
  202.1 2.7 fusion.144
  211.6 4.0 collective-permute-done.31
  223.8 3.3 collective-permute-done.39
  227.1 3.2 collective-permute-done.38
  231.4 5.1 %convert_reduce_fusion = (f32[1024]{0:T(1024)}, bf16[256,1024]{1,0:T(8,128)(2,1)}) fusion(bf16[1,1024,1024]{2,1,0:T(8,128)(2,1)S(1)} %copy-done.12, bf16[256,256]{1,0:T(8,128)(2,1)S(1)} %get-tuple-element.103, bf16[256,256]{1,0:T(8,128)(2,1)S(1)} %get-tuple-element.104, bf16[256,256]{1,0:T(8,128)(2,1)S(1)} %get-tuple-element.105, ...), kind=kOutput, calls=%fused_computation.122 | convolution fusion | flops 558889984 | bytes 5246977 | tf_op jit(solution)/shard_map/dot_general | solution.py:163
  253.0 5.2 %fusion.26 = bf16[3080,1024]{1,0:T(8,128)(2,1)} fusion(f32[768,1024]{1,0:T(8,128)} %fusion.156, f32[768,1024]{1,0:T(8,128)} %fusion.154, pred[]{:T(512)S(6)} %eq.171, bf16[256,256]{0,1:T(8,128)(2,1)S(1)} %bitcast.422, bf16[256,256]{0,1:T(8,128)(2,1)S(1)} %bitcast.428, bf16[256,256]{0,1:T(8,128)(2,1)S(1)} %bitcast.425, ...), kind=kOutput, calls=%fused_computation.32 | convolution fusion | flops 409600000 | bytes 9318401 | tf_op jit(solution)/shard_map/dot_general | solution.py:157
  280.4 3.6 collective-permute-done.17
  293.2 3.6 collective-permute-done.41
  300.1 102.1 %all-reduce.3.cloned.1.call-done = bf16[3080,1024]{1,0:T(8,128)(2,1)} async-done(((bf16[3080,1024]{1,0:T(8,128)(2,1)}), bf16[3080,1024]{1,0:T(8,128)(2,1)}) %all-reduce.3.cloned.1.call-update) | async-done | bytes 6307856 | tf_op jit(solution)/shard_map/psum | solution.py:442
  402.3 4.3 convert_element_type.513
  406.6 3.0 collective-permute-start.48
  412.3 4.2 slice_bitcast_fusion
  417.7 3.6 slice.465
  421.3 3.5 copy.198
  (637 shorter events, 194.2 us)
Async XLA Ops:
  7.2 395.1 %all-reduce.3.cloned.1.call-start = ((), (), s32[]{:S(2)}) async-start(), calls=%async_computation | async-start | bytes 12615680 | tf_op jit(solution)/shard_map/psum | solution.py:442
  9.3 26.6 %collective-permute-start.2 = (bf16[1024,256]{1,0:T(8,128)(2,1)S(1)}, bf16[1024,256]{1,0:T(8,128)(2,1)S(1)}, u32[]{:S(2)}, u32[]{:S(2)}) collective-permute-start(bf16[1024,256]{1,0:T(8,128)(2,1)S(1)} %constant_dynamic-update-slice_fusion), channel_id=1, source_target_pairs={{0,48},{16,0},{32,16},{48,32},{1,49},{17,1},{33,17},{49,33},{2,50}... | collective-permute-start | bytes 1572872 | tf_op jit(solution)/shard_map/ppermute | solution.py:28
  13.5 22.4 %collective-permute-start.1 = (bf16[1024,256]{1,0:T(8,128)(2,1)S(1)}, bf16[1024,256]{1,0:T(8,128)(2,1)}, u32[]{:S(2)}, u32[]{:S(2)}) collective-permute-start(bf16[1024,256]{1,0:T(8,128)(2,1)S(1)} %constant_dynamic-update-slice_fusion), channel_id=1, source_target_pairs={{0,32},{16,48},{32,0},{48,16},{1,33},{17,49},{33,1},{49,17},{2,34}... | collective-permute-start | bytes 1572872 | tf_op jit(solution)/shard_map/ppermute | solution.py:28
  13.5 25.9 %collective-permute-start = (bf16[1024,256]{1,0:T(8,128)(2,1)S(1)}, bf16[1024,256]{1,0:T(8,128)(2,1)}, u32[]{:S(2)}, u32[]{:S(2)}) collective-permute-start(bf16[1024,256]{1,0:T(8,128)(2,1)S(1)} %constant_dynamic-update-slice_fusion), channel_id=1, source_target_pairs={{0,16},{16,32},{32,48},{48,0},{1,17},{17,33},{33,49},{49,1},{2,18}... | collective-permute-start | bytes 1572872 | tf_op jit(solution)/shard_map/ppermute | solution.py:28
  52.7 8.3 %collective-permute-start.3 = (bf16[256,256]{1,0:T(8,128)(2,1)S(1)}, bf16[256,256]{1,0:T(8,128)(2,1)S(1)}, u32[]{:S(2)}, u32[]{:S(2)}) collective-permute-start(bf16[256,256]{1,0:T(8,128)(2,1)S(1)} %get-tuple-element.132), channel_id=1, source_target_pairs={{0,16},{16,32},{32,48},{48,0},{1,17},{17,33},{33,49},{49,1},{2,18}... | collective-permute-start | bytes 393224 | tf_op jit(solution)/shard_map/ppermute | solution.py:68
  61.3 12.9 %collective-permute-start.9 = (bf16[256,256]{1,0:T(8,128)(2,1)S(1)}, bf16[256,256]{1,0:T(8,128)(2,1)S(1)}, u32[]{:S(2)}, u32[]{:S(2)}) collective-permute-start(bf16[256,256]{1,0:T(8,128)(2,1)S(1)} %add_convert_fusion.14), channel_id=1, source_target_pairs={{0,112},{16,64},{32,80},{48,96},{1,113},{17,65},{33,81},{49,97},{2... | collective-permute-start | bytes 393224 | tf_op jit(solution)/shard_map/ppermute | solution.py:86
  104.9 17.3 %collective-permute-start.25 = (f32[256,2]{0,1:T(2,128)S(1)}, f32[256,2]{0,1:T(2,128)S(1)}, u32[]{:S(2)}, u32[]{:S(2)}) collective-permute-start(f32[256,2]{0,1:T(2,128)S(1)} %pad_maximum_fusion.10), channel_id=1, source_target_pairs={{0,48},{16,0},{32,16},{48,32},{1,49},{17,1},{33,17},{49,33},{2,50}... | collective-permute-start | bytes 6152 | tf_op jit(solution)/shard_map/ppermute | solution.py:28
  105.7 18.2 %collective-permute-start.24 = (f32[256,2]{0,1:T(2,128)S(1)}, f32[256,2]{0,1:T(2,128)S(1)}, u32[]{:S(2)}, u32[]{:S(2)}) collective-permute-start(f32[256,2]{0,1:T(2,128)S(1)} %pad_maximum_fusion.10), channel_id=1, source_target_pairs={{0,32},{16,48},{32,0},{48,16},{1,33},{17,49},{33,1},{49,17},{2,34}... | collective-permute-start | bytes 6152 | tf_op jit(solution)/shard_map/ppermute | solution.py:28
  108.1 17.8 %collective-permute-start.23 = (f32[256,2]{0,1:T(2,128)S(1)}, f32[256,2]{0,1:T(2,128)S(1)}, u32[]{:S(2)}, u32[]{:S(2)}) collective-permute-start(f32[256,2]{0,1:T(2,128)S(1)} %pad_maximum_fusion.10), channel_id=1, source_target_pairs={{0,16},{16,32},{32,48},{48,0},{1,17},{17,33},{33,49},{49,1},{2,18}... | collective-permute-start | bytes 6152 | tf_op jit(solution)/shard_map/ppermute | solution.py:28
  118.6 10.0 %collective-permute-start.12 = (bf16[256,256]{1,0:T(8,128)(2,1)S(1)}, bf16[256,256]{1,0:T(8,128)(2,1)S(1)}, u32[]{:S(2)}, u32[]{:S(2)}) collective-permute-start(bf16[256,256]{1,0:T(8,128)(2,1)S(1)} %get-tuple-element.123), channel_id=1, source_target_pairs={{0,48},{16,0},{32,16},{48,32},{1,49},{17,1},{33,17},{49,33},{2,50}... | collective-permute-start | bytes 393224 | tf_op jit(solution)/shard_map/ppermute | solution.py:68
  122.7 9.6 %collective-permute-start.10 = (bf16[256,256]{1,0:T(8,128)(2,1)S(1)}, bf16[256,256]{1,0:T(8,128)(2,1)S(1)}, u32[]{:S(2)}, u32[]{:S(2)}) collective-permute-start(bf16[256,256]{1,0:T(8,128)(2,1)S(1)} %get-tuple-element.125), channel_id=1, source_target_pairs={{0,16},{16,32},{32,48},{48,0},{1,17},{17,33},{33,49},{49,1},{2,18}... | collective-permute-start | bytes 393224 | tf_op jit(solution)/shard_map/ppermute | solution.py:68
  123.9 18.9 %collective-permute-start.22 = (bf16[256,256]{1,0:T(8,128)(2,1)S(1)}, bf16[256,256]{1,0:T(8,128)(2,1)S(1)}, u32[]{:S(2)}, u32[]{:S(2)}) collective-permute-start(bf16[256,256]{1,0:T(8,128)(2,1)S(1)} %get-tuple-element.113), channel_id=1, source_target_pairs={{0,48},{16,0},{32,16},{48,32},{1,49},{17,1},{33,17},{49,33},{2,50}... | collective-permute-start | bytes 393224 | tf_op jit(solution)/shard_map/ppermute | solution.py:68
  125.9 18.2 %collective-permute-start.21 = (bf16[256,256]{1,0:T(8,128)(2,1)S(1)}, bf16[256,256]{1,0:T(8,128)(2,1)S(1)}, u32[]{:S(2)}, u32[]{:S(2)}) collective-permute-start(bf16[256,256]{1,0:T(8,128)(2,1)S(1)} %get-tuple-element.114), channel_id=1, source_target_pairs={{0,32},{16,48},{32,0},{48,16},{1,33},{17,49},{33,1},{49,17},{2,34}... | collective-permute-start | bytes 393224 | tf_op jit(solution)/shard_map/ppermute | solution.py:68
  128.6 16.8 %collective-permute-start.20 = (bf16[256,256]{1,0:T(8,128)(2,1)S(1)}, bf16[256,256]{1,0:T(8,128)(2,1)S(1)}, u32[]{:S(2)}, u32[]{:S(2)}) collective-permute-start(bf16[256,256]{1,0:T(8,128)(2,1)S(1)} %get-tuple-element.115), channel_id=1, source_target_pairs={{0,16},{16,32},{32,48},{48,0},{1,17},{17,33},{33,49},{49,1},{2,18}... | collective-permute-start | bytes 393224 | tf_op jit(solution)/shard_map/ppermute | solution.py:68
  133.1 14.8 %collective-permute-start.16 = (bf16[256,256]{1,0:T(8,128)(2,1)S(1)}, bf16[256,256]{1,0:T(8,128)(2,1)S(1)}, u32[]{:S(2)}, u32[]{:S(2)}) collective-permute-start(bf16[256,256]{1,0:T(8,128)(2,1)S(1)} %get-tuple-element.78), channel_id=1, source_target_pairs={{0,112},{16,64},{32,80},{48,96},{1,113},{17,65},{33,81},{49,97},{2... | collective-permute-start | bytes 393224 | tf_op jit(solution)/shard_map/ppermute | solution.py:86
  140.0 9.2 %collective-permute-start.15 = (bf16[256,256]{1,0:T(8,128)(2,1)S(1)}, bf16[256,256]{1,0:T(8,128)(2,1)S(1)}, u32[]{:S(2)}, u32[]{:S(2)}) collective-permute-start(bf16[256,256]{1,0:T(8,128)(2,1)S(1)} %get-tuple-element.78), channel_id=1, source_target_pairs={{0,96},{16,112},{32,64},{48,80},{1,97},{17,113},{33,65},{49,81},{2... | collective-permute-start | bytes 393224 | tf_op jit(solution)/shard_map/ppermute | solution.py:86
  144.1 7.9 %collective-permute-start.13 = (bf16[256,256]{1,0:T(8,128)(2,1)S(1)}, bf16[256,256]{1,0:T(8,128)(2,1)S(1)}, u32[]{:S(2)}, u32[]{:S(2)}) collective-permute-start(bf16[256,256]{1,0:T(8,128)(2,1)S(1)} %get-tuple-element.78), channel_id=1, source_target_pairs={{0,64},{16,80},{32,96},{48,112},{1,65},{17,81},{33,97},{49,113},{2... | collective-permute-start | bytes 393224 | tf_op jit(solution)/shard_map/ppermute | solution.py:86
  146.6 9.3 %collective-permute-start.29 = (bf16[256,256]{1,0:T(8,128)(2,1)S(1)}, bf16[256,256]{1,0:T(8,128)(2,1)S(1)}, u32[]{:S(2)}, u32[]{:S(2)}) collective-permute-start(bf16[256,256]{1,0:T(8,128)(2,1)S(1)} %add_convert_fusion.11), channel_id=1, source_target_pairs={{64,48},{80,0},{96,16},{112,32},{65,49},{81,1},{97,17},{113,33},{6... | collective-permute-start | bytes 393224 | tf_op jit(solution)/shard_map/ppermute | solution.py:86
  147.9 11.2 %collective-permute-start.28 = (bf16[256,256]{1,0:T(8,128)(2,1)S(1)}, bf16[256,256]{1,0:T(8,128)(2,1)S(1)}, u32[]{:S(2)}, u32[]{:S(2)}) collective-permute-start(bf16[256,256]{1,0:T(8,128)(2,1)S(1)} %add_convert_fusion.11), channel_id=1, source_target_pairs={{64,32},{80,48},{96,0},{112,16},{65,33},{81,49},{97,1},{113,17},{6... | collective-permute-start | bytes 393224 | tf_op jit(solution)/shard_map/ppermute | solution.py:86
  149.2 10.9 %collective-permute-start.27 = (bf16[256,256]{1,0:T(8,128)(2,1)S(1)}, bf16[256,256]{1,0:T(8,128)(2,1)S(1)}, u32[]{:S(2)}, u32[]{:S(2)}) collective-permute-start(bf16[256,256]{1,0:T(8,128)(2,1)S(1)} %add_convert_fusion.11), channel_id=1, source_target_pairs={{64,16},{80,32},{96,48},{112,0},{65,17},{81,33},{97,49},{113,1},{6... | collective-permute-start | bytes 393224 | tf_op jit(solution)/shard_map/ppermute | solution.py:86
  150.5 9.6 %collective-permute-start.26 = (bf16[256,256]{1,0:T(8,128)(2,1)S(1)}, bf16[256,256]{1,0:T(8,128)(2,1)S(1)}, u32[]{:S(2)}, u32[]{:S(2)}) collective-permute-start(bf16[256,256]{1,0:T(8,128)(2,1)S(1)} %add_convert_fusion.11), channel_id=1, source_target_pairs={{64,0},{80,16},{96,32},{112,48},{65,1},{81,17},{97,33},{113,49},{6... | collective-permute-start | bytes 393224 | tf_op jit(solution)/shard_map/ppermute | solution.py:86
  191.7 18.6 %collective-permute-start.35 = (f32[256,2]{0,1:T(2,128)S(1)}, f32[256,2]{0,1:T(2,128)S(1)}, u32[]{:S(2)}, u32[]{:S(2)}) collective-permute-start(f32[256,2]{0,1:T(2,128)S(1)} %pad_maximum_fusion.11), channel_id=1, source_target_pairs={{0,48},{16,0},{32,16},{48,32},{1,49},{17,1},{33,17},{49,33},{2,50}... | collective-permute-start | bytes 6152 | tf_op jit(solution)/shard_map/ppermute | solution.py:28
  193.3 17.4 %collective-permute-start.34 = (f32[256,2]{0,1:T(2,128)S(1)}, f32[256,2]{0,1:T(2,128)S(1)}, u32[]{:S(2)}, u32[]{:S(2)}) collective-permute-start(f32[256,2]{0,1:T(2,128)S(1)} %pad_maximum_fusion.11), channel_id=1, source_target_pairs={{0,32},{16,48},{32,0},{48,16},{1,33},{17,49},{33,1},{49,17},{2,34}... | collective-permute-start | bytes 6152 | tf_op jit(solution)/shard_map/ppermute | solution.py:28
  194.4 16.4 %collective-permute-start.33 = (f32[256,2]{0,1:T(2,128)S(1)}, f32[256,2]{0,1:T(2,128)S(1)}, u32[]{:S(2)}, u32[]{:S(2)}) collective-permute-start(f32[256,2]{0,1:T(2,128)S(1)} %pad_maximum_fusion.11), channel_id=1, source_target_pairs={{0,16},{16,32},{32,48},{48,0},{1,17},{17,33},{33,49},{49,1},{2,18}... | collective-permute-start | bytes 6152 | tf_op jit(solution)/shard_map/ppermute | solution.py:28
  217.8 9.3 %collective-permute-start.39 = (bf16[256,256]{1,0:T(8,128)(2,1)S(1)}, bf16[256,256]{1,0:T(8,128)(2,1)S(1)}, u32[]{:S(2)}, u32[]{:S(2)}) collective-permute-start(bf16[256,256]{1,0:T(8,128)(2,1)S(1)} %get-tuple-element.67), channel_id=1, source_target_pairs={{64,48},{80,0},{96,16},{112,32},{65,49},{81,1},{97,17},{113,33},{6... | collective-permute-start | bytes 393224 | tf_op jit(solution)/shard_map/ppermute | solution.py:86
  219.1 11.2 %collective-permute-start.38 = (bf16[256,256]{1,0:T(8,128)(2,1)S(1)}, bf16[256,256]{1,0:T(8,128)(2,1)S(1)}, u32[]{:S(2)}, u32[]{:S(2)}) collective-permute-start(bf16[256,256]{1,0:T(8,128)(2,1)S(1)} %get-tuple-element.67), channel_id=1, source_target_pairs={{64,32},{80,48},{96,0},{112,16},{65,33},{81,49},{97,1},{113,17},{6... | collective-permute-start | bytes 393224 | tf_op jit(solution)/shard_map/ppermute | solution.py:86
  220.4 10.9 %collective-permute-start.37 = (bf16[256,256]{1,0:T(8,128)(2,1)S(1)}, bf16[256,256]{1,0:T(8,128)(2,1)S(1)}, u32[]{:S(2)}, u32[]{:S(2)}) collective-permute-start(bf16[256,256]{1,0:T(8,128)(2,1)S(1)} %get-tuple-element.67), channel_id=1, source_target_pairs={{64,16},{80,32},{96,48},{112,0},{65,17},{81,33},{97,49},{113,1},{6... | collective-permute-start | bytes 393224 | tf_op jit(solution)/shard_map/ppermute | solution.py:86
  221.7 9.6 %collective-permute-start.36 = (bf16[256,256]{1,0:T(8,128)(2,1)S(1)}, bf16[256,256]{1,0:T(8,128)(2,1)S(1)}, u32[]{:S(2)}, u32[]{:S(2)}) collective-permute-start(bf16[256,256]{1,0:T(8,128)(2,1)S(1)} %get-tuple-element.67), channel_id=1, source_target_pairs={{64,0},{80,16},{96,32},{112,48},{65,1},{81,17},{97,33},{113,49},{6... | collective-permute-start | bytes 393224 | tf_op jit(solution)/shard_map/ppermute | solution.py:86
  274.5 9.5 %collective-permute-start.17 = (bf16[256,256]{1,0:T(8,128)(2,1)S(1)}, bf16[256,256]{1,0:T(8,128)(2,1)S(1)}, u32[]{:S(2)}, u32[]{:S(2)}) collective-permute-start(bf16[256,256]{1,0:T(8,128)(2,1)S(1)} %get-tuple-element.118), channel_id=1, source_target_pairs={{0,16},{16,32},{32,48},{48,0},{1,17},{17,33},{33,49},{49,1},{2,18}... | collective-permute-start | bytes 393224 | tf_op jit(solution)/shard_map/ppermute | solution.py:68
  406.6 18.8 %collective-permute-start.48 = (f32[4096]{0:T(1024)S(1)}, f32[4096]{0:T(1024)S(1)}, u32[]{:S(2)}, u32[]{:S(2)}) collective-permute-start(f32[4096]{0:T(1024)S(1)} %bitcast.528), channel_id=1, source_target_pairs={{0,48},{16,0},{32,16},{48,32},{1,49},{17,1},{33,17},{49,33},{2,50}... | collective-permute-start | bytes 49160 | tf_op jit(solution)/shard_map/ppermute | solution.py:28
  409.6 15.8 %collective-permute-start.47 = (f32[4096]{0:T(1024)S(1)}, f32[4096]{0:T(1024)S(1)}, u32[]{:S(2)}, u32[]{:S(2)}) collective-permute-start(f32[4096]{0:T(1024)S(1)} %bitcast.529), channel_id=1, source_target_pairs={{0,32},{16,48},{32,0},{48,16},{1,33},{17,49},{33,1},{49,17},{2,34}... | collective-permute-start | bytes 49160 | tf_op jit(solution)/shard_map/ppermute | solution.py:28
  410.3 15.2 %collective-permute-start.46 = (f32[4096]{0:T(1024)S(1)}, f32[4096]{0:T(1024)S(1)}, u32[]{:S(2)}, u32[]{:S(2)}) collective-permute-start(f32[4096]{0:T(1024)S(1)} %bitcast.530), channel_id=1, source_target_pairs={{0,16},{16,32},{32,48},{48,0},{1,17},{17,33},{33,49},{49,1},{2,18}... | collective-permute-start | bytes 49160 | tf_op jit(solution)/shard_map/ppermute | solution.py:28
  (170 other events, 1087.9 us)
Sparse Core Ops, SparseCore 0:
  267.9 134.3 all-reduce.2

commit v9 on v5

--- a/solution.py
+++ b/solution.py
@@ -440,11 +440,11 @@
     small_rows = jnp.pad(small_rows, (0, small_pad)).reshape(-1, model_width)
     pieces = (totals[0][0], totals[1][0], totals[2][0], totals[3][0], small_rows)
     slab = jnp.concatenate([piece.astype(jnp.bfloat16) for piece in pieces], axis=0)
-    slab = lax.psum(slab, "dp").astype(jnp.float32)
+    slab = lax.psum(slab, "dp")
     summed = []
     offset = 0
     for piece in pieces:
-        summed.append(slab[offset : offset + piece.shape[0]])
+        summed.append(slab[offset : offset + piece.shape[0]].astype(jnp.float32))
         offset = offset + piece.shape[0]
     grad_rows_all = jnp.concatenate(
         [jnp.where(leading, tick_grads[block + 1], tick_grads[block]) for block in range(NMB)],

time: 439 us -> 437 us (level)
  local copies, waits for them, and re-layouts: 67 us -> 58.1 us
  other arithmetic: 29 us -> 35.4 us
    broadcast_in_dim x0 -> x2, other arithmetic: none -> 6.55 us  [the longest x1 4.43 us: per_device(): grad_down = summed[3][None]]
    broadcast_in_dim x2 -> x0, local copies, waits for them, and re-layouts: 5.28 us -> none  [the longest x1 4.24 us: per_device(): grad_down = summed[3][None]]
    unnamed x347 -> x348, local copies, waits for them, and re-layouts: 18.2 us -> 18.2 us
  transfers between devices with their start and end apart: 50 -> 50, of which waited for: 28 -> 29; matrix products, arithmetic and copies ran while one was open for 10% -> 10% of each run, Pallas kernels for 0% -> 0%
where the time goes in v9:
time: 437 us; the launch traced here: 428 us
  waiting for transfers between devices  165 us (38%)
  matrix products  78.3 us (18%)
  starting transfers between devices  73.8 us (17%)
  local copies, waits for them, and re-layouts  58.1 us (13%)
  other arithmetic  35.4 us (8%)
  between operations  17.4 us (4%)
    psum x1, waiting for transfers between devices, per_device(): slab = lax.psum(slab, 'dp')  110 us
    ppermute x16, starting transfers between devices, cross_gather(): parts.append(lax.ppermute(x, ('pipe', 'tensor'), pairs))  34.7 us
    dot_general x12, matrix products, contract_rows(): lax.dot_general(left, right, (((0,), (0,)), ((), ())), preferred_element_...  30.6 us
    ppermute x18, starting transfers between devices, tensor_scatter_sum(): parts.append(lax.ppermute(piece_for((me + shift) % peers), 'tensor', pairs))  21.1 us
    dot_general x12, matrix products, contract_cols(): lax.dot_general(left, right, (((1,), (1,)), ((), ())), preferred_element_...  21 us
    ppermute x15, waiting for transfers between devices, tensor_pieces(): parts.append(lax.ppermute(x, 'tensor', pairs))  19.8 us
    ppermute x16, waiting for transfers between devices, cross_gather(): parts.append(lax.ppermute(x, ('pipe', 'tensor'), pairs))  18.5 us
    unnamed x348, local copies, waits for them, and re-layouts  18.2 us
  transfers between devices with their start and end apart: 50, of which 29 were waited for; matrix products, arithmetic and copies ran while one was open for 10% of the time, Pallas kernels for 0%

profile of v9, /device:TPU:0, one launch (start us, length us, event | category | flops | bytes accessed | tf_op | source)
XLA Modules:
  0.0 427.9 jit_solution(8818799455330097622)
XLA Ops:
  9.3 4.2 collective-permute-start.2
  20.9 2.6 copy.125
  26.3 9.6 %collective-permute-done.2 = bf16[1024,256]{1,0:T(8,128)(2,1)S(1)} collective-permute-done((bf16[1024,256]{1,0:T(8,128)(2,1)S(1)}, bf16[1024,256]{1,0:T(8,128)(2,1)S(1)}, u32[]{:S(2)}, u32[]{:S(2)}) %collective-permute-start.2) | collective-permute-done | bytes 524320 | tf_op jit(solution)/shard_map/ppermute | solution.py:28
  36.7 2.7 collective-permute-done
  46.0 3.9 fusion.66
  54.7 3.3 collective-permute-done.5
  61.3 5.5 %collective-permute-start.9 = (bf16[256,256]{1,0:T(8,128)(2,1)S(1)}, bf16[256,256]{1,0:T(8,128)(2,1)S(1)}, u32[]{:S(2)}, u32[]{:S(2)}) collective-permute-start(bf16[256,256]{1,0:T(8,128)(2,1)S(1)} %add_convert_fusion.17), channel_id=1, source_target_pairs={{0,112},{16,64},{32,80},{48,96},{1,113},{17,65},{33,81},{49,97},{2... | collective-permute-start | bytes 393224 | tf_op jit(solution)/shard_map/ppermute | solution.py:86
  96.4 2.9 fusion.69
  99.4 2.6 fusion.159
  103.0 2.8 fusion.149
  106.0 4.2 convert_reduce_fusion.2
  110.2 3.1 fusion.154
  118.3 3.3 collective-permute-start.12
  123.4 3.0 collective-permute-done.20
  130.5 8.4 %collective-permute-start.16 = (bf16[256,256]{1,0:T(8,128)(2,1)S(1)}, bf16[256,256]{1,0:T(8,128)(2,1)S(1)}, u32[]{:S(2)}, u32[]{:S(2)}) collective-permute-start(bf16[256,256]{1,0:T(8,128)(2,1)S(1)} %get-tuple-element.75), channel_id=1, source_target_pairs={{0,112},{16,64},{32,80},{48,96},{1,113},{17,65},{33,81},{49,97},{2... | collective-permute-start | bytes 393224 | tf_op jit(solution)/shard_map/ppermute | solution.py:86
  150.0 4.0 collective-permute-done.29
  154.0 3.0 collective-permute-done.28
  179.9 2.9 fusion.72
  185.2 2.6 fusion.157
  189.5 3.4 convert_reduce_fusion.1
  192.9 3.1 fusion.152
  200.5 2.7 fusion.147
  220.5 3.3 collective-permute-done.39
  223.8 3.2 collective-permute-done.38
  228.3 5.4 %convert_reduce_fusion = (f32[1024]{0:T(1024)}, bf16[256,1024]{1,0:T(8,128)(2,1)}) fusion(bf16[1,1024,1024]{2,1,0:T(8,128)(2,1)S(1)} %copy-done.12, bf16[256,256]{1,0:T(8,128)(2,1)S(1)} %get-tuple-element.105, bf16[256,256]{1,0:T(8,128)(2,1)S(1)} %get-tuple-element.106, bf16[256,256]{1,0:T(8,128)(2,1)S(1)} %get-tuple-element.107, ...), kind=kOutput, calls=%fused_computation.124 | convolution fusion | flops 558889984 | bytes 5246977 | tf_op jit(solution)/shard_map/dot_general | solution.py:163
  247.9 5.2 %fusion.28 = bf16[3080,1024]{1,0:T(8,128)(2,1)} fusion(f32[768,1024]{1,0:T(8,128)} %fusion.159, f32[768,1024]{1,0:T(8,128)} %fusion.157, pred[]{:T(512)S(6)} %eq.171, bf16[256,256]{0,1:T(8,128)(2,1)S(1)} %bitcast.431, bf16[256,256]{0,1:T(8,128)(2,1)S(1)} %bitcast.437, bf16[256,256]{0,1:T(8,128)(2,1)S(1)} %bitcast.434, ...), kind=kOutput, calls=%fused_computation.34 | convolution fusion | flops 409600000 | bytes 9318401 | tf_op jit(solution)/shard_map/dot_general | solution.py:157
  270.1 2.9 collective-permute-start.42
  288.5 110.0 %all-reduce.3.cloned.1.call-done = bf16[3080,1024]{1,0:T(8,128)(2,1)} async-done(((bf16[3080,1024]{1,0:T(8,128)(2,1)}), bf16[3080,1024]{1,0:T(8,128)(2,1)}) %all-reduce.3.cloned.1.call-update) | async-done | bytes 6307856 | tf_op jit(solution)/shard_map/psum | solution.py:443
  399.2 3.0 collective-permute-start.48
  406.0 3.6 slice_convert_fusion
  409.6 4.4 %fusion = (f32[1,1024,1024]{2,1,0:T(8,128)}, f32[1,1024,1024]{2,1,0:T(8,128)}) fusion(bf16[3080,1024]{1,0:T(8,128)(2,1)S(1)} %copy-done.23), kind=kLoop, calls=%fused_computation.4 | loop fusion | flops 2097152 | bytes 12582912 | tf_op jit(solution)/shard_map/broadcast_in_dim | solution.py:457
  415.8 3.5 copy.198
  (638 shorter events, 182.1 us)
Async XLA Ops:
  7.2 391.3 %all-reduce.3.cloned.1.call-start = ((), (), s32[]{:S(2)}) async-start(), calls=%async_computation | async-start | bytes 12615680 | tf_op jit(solution)/shard_map/psum | solution.py:443
  9.3 26.6 %collective-permute-start.2 = (bf16[1024,256]{1,0:T(8,128)(2,1)S(1)}, bf16[1024,256]{1,0:T(8,128)(2,1)S(1)}, u32[]{:S(2)}, u32[]{:S(2)}) collective-permute-start(bf16[1024,256]{1,0:T(8,128)(2,1)S(1)} %constant_dynamic-update-slice_fusion), channel_id=1, source_target_pairs={{0,48},{16,0},{32,16},{48,32},{1,49},{17,1},{33,17},{49,33},{2,50}... | collective-permute-start | bytes 1572872 | tf_op jit(solution)/shard_map/ppermute | solution.py:28
  13.5 22.4 %collective-permute-start.1 = (bf16[1024,256]{1,0:T(8,128)(2,1)S(1)}, bf16[1024,256]{1,0:T(8,128)(2,1)}, u32[]{:S(2)}, u32[]{:S(2)}) collective-permute-start(bf16[1024,256]{1,0:T(8,128)(2,1)S(1)} %constant_dynamic-update-slice_fusion), channel_id=1, source_target_pairs={{0,32},{16,48},{32,0},{48,16},{1,33},{17,49},{33,1},{49,17},{2,34}... | collective-permute-start | bytes 1572872 | tf_op jit(solution)/shard_map/ppermute | solution.py:28
  13.5 25.9 %collective-permute-start = (bf16[1024,256]{1,0:T(8,128)(2,1)S(1)}, bf16[1024,256]{1,0:T(8,128)(2,1)}, u32[]{:S(2)}, u32[]{:S(2)}) collective-permute-start(bf16[1024,256]{1,0:T(8,128)(2,1)S(1)} %constant_dynamic-update-slice_fusion), channel_id=1, source_target_pairs={{0,16},{16,32},{32,48},{48,0},{1,17},{17,33},{33,49},{49,1},{2,18}... | collective-permute-start | bytes 1572872 | tf_op jit(solution)/shard_map/ppermute | solution.py:28
  52.5 7.7 %collective-permute-start.4 = (bf16[256,256]{1,0:T(8,128)(2,1)S(1)}, bf16[256,256]{1,0:T(8,128)(2,1)S(1)}, u32[]{:S(2)}, u32[]{:S(2)}) collective-permute-start(bf16[256,256]{1,0:T(8,128)(2,1)S(1)} %get-tuple-element.133), channel_id=1, source_target_pairs={{0,32},{16,48},{32,0},{48,16},{1,33},{17,49},{33,1},{49,17},{2,34}... | collective-permute-start | bytes 393224 | tf_op jit(solution)/shard_map/ppermute | solution.py:68
  52.8 8.3 %collective-permute-start.3 = (bf16[256,256]{1,0:T(8,128)(2,1)S(1)}, bf16[256,256]{1,0:T(8,128)(2,1)S(1)}, u32[]{:S(2)}, u32[]{:S(2)}) collective-permute-start(bf16[256,256]{1,0:T(8,128)(2,1)S(1)} %get-tuple-element.134), channel_id=1, source_target_pairs={{0,16},{16,32},{32,48},{48,0},{1,17},{17,33},{33,49},{49,1},{2,18}... | collective-permute-start | bytes 393224 | tf_op jit(solution)/shard_map/ppermute | solution.py:68
  61.3 12.9 %collective-permute-start.9 = (bf16[256,256]{1,0:T(8,128)(2,1)S(1)}, bf16[256,256]{1,0:T(8,128)(2,1)S(1)}, u32[]{:S(2)}, u32[]{:S(2)}) collective-permute-start(bf16[256,256]{1,0:T(8,128)(2,1)S(1)} %add_convert_fusion.17), channel_id=1, source_target_pairs={{0,112},{16,64},{32,80},{48,96},{1,113},{17,65},{33,81},{49,97},{2... | collective-permute-start | bytes 393224 | tf_op jit(solution)/shard_map/ppermute | solution.py:86
  66.8 7.4 %collective-permute-start.8 = (bf16[256,256]{1,0:T(8,128)(2,1)S(1)}, bf16[256,256]{1,0:T(8,128)(2,1)}, u32[]{:S(2)}, u32[]{:S(2)}) collective-permute-start(bf16[256,256]{1,0:T(8,128)(2,1)S(1)} %add_convert_fusion.17), channel_id=1, source_target_pairs={{0,96},{16,112},{32,64},{48,80},{1,97},{17,113},{33,65},{49,81},{2... | collective-permute-start | bytes 393224 | tf_op jit(solution)/shard_map/ppermute | solution.py:86
  115.5 8.0 %collective-permute-start.21 = (bf16[256,256]{1,0:T(8,128)(2,1)S(1)}, bf16[256,256]{1,0:T(8,128)(2,1)S(1)}, u32[]{:S(2)}, u32[]{:S(2)}) collective-permute-start(bf16[256,256]{1,0:T(8,128)(2,1)S(1)} %get-tuple-element.116), channel_id=1, source_target_pairs={{0,32},{16,48},{32,0},{48,16},{1,33},{17,49},{33,1},{49,17},{2,34}... | collective-permute-start | bytes 393224 | tf_op jit(solution)/shard_map/ppermute | solution.py:68
  117.8 8.6 %collective-permute-start.20 = (bf16[256,256]{1,0:T(8,128)(2,1)S(1)}, bf16[256,256]{1,0:T(8,128)(2,1)S(1)}, u32[]{:S(2)}, u32[]{:S(2)}) collective-permute-start(bf16[256,256]{1,0:T(8,128)(2,1)S(1)} %get-tuple-element.117), channel_id=1, source_target_pairs={{0,16},{16,32},{32,48},{48,0},{1,17},{17,33},{33,49},{49,1},{2,18}... | collective-permute-start | bytes 393224 | tf_op jit(solution)/shard_map/ppermute | solution.py:68
  118.3 11.0 %collective-permute-start.12 = (bf16[256,256]{1,0:T(8,128)(2,1)S(1)}, bf16[256,256]{1,0:T(8,128)(2,1)S(1)}, u32[]{:S(2)}, u32[]{:S(2)}) collective-permute-start(bf16[256,256]{1,0:T(8,128)(2,1)S(1)} %get-tuple-element.125), channel_id=1, source_target_pairs={{0,48},{16,0},{32,16},{48,32},{1,49},{17,1},{33,17},{49,33},{2,50}... | collective-permute-start | bytes 393224 | tf_op jit(solution)/shard_map/ppermute | solution.py:68
  121.6 7.9 %collective-permute-start.11 = (bf16[256,256]{1,0:T(8,128)(2,1)S(1)}, bf16[256,256]{1,0:T(8,128)(2,1)S(1)}, u32[]{:S(2)}, u32[]{:S(2)}) collective-permute-start(bf16[256,256]{1,0:T(8,128)(2,1)S(1)} %get-tuple-element.126), channel_id=1, source_target_pairs={{0,32},{16,48},{32,0},{48,16},{1,33},{17,49},{33,1},{49,17},{2,34}... | collective-permute-start | bytes 393224 | tf_op jit(solution)/shard_map/ppermute | solution.py:68
  122.2 7.4 %collective-permute-start.10 = (bf16[256,256]{1,0:T(8,128)(2,1)S(1)}, bf16[256,256]{1,0:T(8,128)(2,1)S(1)}, u32[]{:S(2)}, u32[]{:S(2)}) collective-permute-start(bf16[256,256]{1,0:T(8,128)(2,1)S(1)} %get-tuple-element.127), channel_id=1, source_target_pairs={{0,16},{16,32},{32,48},{48,0},{1,17},{17,33},{33,49},{49,1},{2,18}... | collective-permute-start | bytes 393224 | tf_op jit(solution)/shard_map/ppermute | solution.py:68
  126.8 13.9 %collective-permute-start.25 = (f32[256,2]{0,1:T(2,128)S(1)}, f32[256,2]{0,1:T(2,128)S(1)}, u32[]{:S(2)}, u32[]{:S(2)}) collective-permute-start(f32[256,2]{0,1:T(2,128)S(1)} %pad_maximum_fusion.10), channel_id=1, source_target_pairs={{0,48},{16,0},{32,16},{48,32},{1,49},{17,1},{33,17},{49,33},{2,50}... | collective-permute-start | bytes 6152 | tf_op jit(solution)/shard_map/ppermute | solution.py:28
  126.9 15.0 %collective-permute-start.24 = (f32[256,2]{0,1:T(2,128)S(1)}, f32[256,2]{0,1:T(2,128)S(1)}, u32[]{:S(2)}, u32[]{:S(2)}) collective-permute-start(f32[256,2]{0,1:T(2,128)S(1)} %pad_maximum_fusion.10), channel_id=1, source_target_pairs={{0,32},{16,48},{32,0},{48,16},{1,33},{17,49},{33,1},{49,17},{2,34}... | collective-permute-start | bytes 6152 | tf_op jit(solution)/shard_map/ppermute | solution.py:28
  129.3 14.0 %collective-permute-start.23 = (f32[256,2]{0,1:T(2,128)S(1)}, f32[256,2]{0,1:T(2,128)S(1)}, u32[]{:S(2)}, u32[]{:S(2)}) collective-permute-start(f32[256,2]{0,1:T(2,128)S(1)} %pad_maximum_fusion.10), channel_id=1, source_target_pairs={{0,16},{16,32},{32,48},{48,0},{1,17},{17,33},{33,49},{49,1},{2,18}... | collective-permute-start | bytes 6152 | tf_op jit(solution)/shard_map/ppermute | solution.py:28
  130.5 15.3 %collective-permute-start.16 = (bf16[256,256]{1,0:T(8,128)(2,1)S(1)}, bf16[256,256]{1,0:T(8,128)(2,1)S(1)}, u32[]{:S(2)}, u32[]{:S(2)}) collective-permute-start(bf16[256,256]{1,0:T(8,128)(2,1)S(1)} %get-tuple-element.75), channel_id=1, source_target_pairs={{0,112},{16,64},{32,80},{48,96},{1,113},{17,65},{33,81},{49,97},{2... | collective-permute-start | bytes 393224 | tf_op jit(solution)/shard_map/ppermute | solution.py:86
  138.9 8.2 %collective-permute-start.15 = (bf16[256,256]{1,0:T(8,128)(2,1)S(1)}, bf16[256,256]{1,0:T(8,128)(2,1)S(1)}, u32[]{:S(2)}, u32[]{:S(2)}) collective-permute-start(bf16[256,256]{1,0:T(8,128)(2,1)S(1)} %get-tuple-element.75), channel_id=1, source_target_pairs={{0,96},{16,112},{32,64},{48,80},{1,97},{17,113},{33,65},{49,81},{2... | collective-permute-start | bytes 393224 | tf_op jit(solution)/shard_map/ppermute | solution.py:86
  140.7 7.8 %collective-permute-start.14 = (bf16[256,256]{1,0:T(8,128)(2,1)S(1)}, bf16[256,256]{1,0:T(8,128)(2,1)S(1)}, u32[]{:S(2)}, u32[]{:S(2)}) collective-permute-start(bf16[256,256]{1,0:T(8,128)(2,1)S(1)} %get-tuple-element.75), channel_id=1, source_target_pairs={{0,80},{16,96},{32,112},{48,64},{1,81},{17,97},{33,113},{49,65},{2... | collective-permute-start | bytes 393224 | tf_op jit(solution)/shard_map/ppermute | solution.py:86
  142.0 7.9 %collective-permute-start.13 = (bf16[256,256]{1,0:T(8,128)(2,1)S(1)}, bf16[256,256]{1,0:T(8,128)(2,1)S(1)}, u32[]{:S(2)}, u32[]{:S(2)}) collective-permute-start(bf16[256,256]{1,0:T(8,128)(2,1)S(1)} %get-tuple-element.75), channel_id=1, source_target_pairs={{0,64},{16,80},{32,96},{48,112},{1,65},{17,81},{33,97},{49,113},{2... | collective-permute-start | bytes 393224 | tf_op jit(solution)/shard_map/ppermute | solution.py:86
  144.5 9.5 %collective-permute-start.29 = (bf16[256,256]{1,0:T(8,128)(2,1)S(1)}, bf16[256,256]{1,0:T(8,128)(2,1)S(1)}, u32[]{:S(2)}, u32[]{:S(2)}) collective-permute-start(bf16[256,256]{1,0:T(8,128)(2,1)S(1)} %add_convert_fusion.14), channel_id=1, source_target_pairs={{64,48},{80,0},{96,16},{112,32},{65,49},{81,1},{97,17},{113,33},{6... | collective-permute-start | bytes 393224 | tf_op jit(solution)/shard_map/ppermute | solution.py:86
  145.8 11.2 %collective-permute-start.28 = (bf16[256,256]{1,0:T(8,128)(2,1)S(1)}, bf16[256,256]{1,0:T(8,128)(2,1)S(1)}, u32[]{:S(2)}, u32[]{:S(2)}) collective-permute-start(bf16[256,256]{1,0:T(8,128)(2,1)S(1)} %add_convert_fusion.14), channel_id=1, source_target_pairs={{64,32},{80,48},{96,0},{112,16},{65,33},{81,49},{97,1},{113,17},{6... | collective-permute-start | bytes 393224 | tf_op jit(solution)/shard_map/ppermute | solution.py:86
  147.1 10.9 %collective-permute-start.27 = (bf16[256,256]{1,0:T(8,128)(2,1)S(1)}, bf16[256,256]{1,0:T(8,128)(2,1)S(1)}, u32[]{:S(2)}, u32[]{:S(2)}) collective-permute-start(bf16[256,256]{1,0:T(8,128)(2,1)S(1)} %add_convert_fusion.14), channel_id=1, source_target_pairs={{64,16},{80,32},{96,48},{112,0},{65,17},{81,33},{97,49},{113,1},{6... | collective-permute-start | bytes 393224 | tf_op jit(solution)/shard_map/ppermute | solution.py:86
  148.4 9.7 %collective-permute-start.26 = (bf16[256,256]{1,0:T(8,128)(2,1)S(1)}, bf16[256,256]{1,0:T(8,128)(2,1)S(1)}, u32[]{:S(2)}, u32[]{:S(2)}) collective-permute-start(bf16[256,256]{1,0:T(8,128)(2,1)S(1)} %add_convert_fusion.14), channel_id=1, source_target_pairs={{64,0},{80,16},{96,32},{112,48},{65,1},{81,17},{97,33},{113,49},{6... | collective-permute-start | bytes 393224 | tf_op jit(solution)/shard_map/ppermute | solution.py:86
  197.3 7.4 %collective-permute-start.32 = (bf16[256,256]{1,0:T(8,128)(2,1)S(1)}, bf16[256,256]{1,0:T(8,128)(2,1)S(1)}, u32[]{:S(2)}, u32[]{:S(2)}) collective-permute-start(bf16[256,256]{1,0:T(8,128)(2,1)S(1)} %get-tuple-element.108), channel_id=1, source_target_pairs={{0,48},{16,0},{32,16},{48,32},{1,49},{17,1},{33,17},{49,33},{2,50}... | collective-permute-start | bytes 393224 | tf_op jit(solution)/shard_map/ppermute | solution.py:68
  214.5 9.3 %collective-permute-start.39 = (bf16[256,256]{1,0:T(8,128)(2,1)S(1)}, bf16[256,256]{1,0:T(8,128)(2,1)S(1)}, u32[]{:S(2)}, u32[]{:S(2)}) collective-permute-start(bf16[256,256]{1,0:T(8,128)(2,1)S(1)} %get-tuple-element.70), channel_id=1, source_target_pairs={{64,48},{80,0},{96,16},{112,32},{65,49},{81,1},{97,17},{113,33},{6... | collective-permute-start | bytes 393224 | tf_op jit(solution)/shard_map/ppermute | solution.py:86
  215.8 11.1 %collective-permute-start.38 = (bf16[256,256]{1,0:T(8,128)(2,1)S(1)}, bf16[256,256]{1,0:T(8,128)(2,1)S(1)}, u32[]{:S(2)}, u32[]{:S(2)}) collective-permute-start(bf16[256,256]{1,0:T(8,128)(2,1)S(1)} %get-tuple-element.70), channel_id=1, source_target_pairs={{64,32},{80,48},{96,0},{112,16},{65,33},{81,49},{97,1},{113,17},{6... | collective-permute-start | bytes 393224 | tf_op jit(solution)/shard_map/ppermute | solution.py:86
  217.1 10.9 %collective-permute-start.37 = (bf16[256,256]{1,0:T(8,128)(2,1)S(1)}, bf16[256,256]{1,0:T(8,128)(2,1)S(1)}, u32[]{:S(2)}, u32[]{:S(2)}) collective-permute-start(bf16[256,256]{1,0:T(8,128)(2,1)S(1)} %get-tuple-element.70), channel_id=1, source_target_pairs={{64,16},{80,32},{96,48},{112,0},{65,17},{81,33},{97,49},{113,1},{6... | collective-permute-start | bytes 393224 | tf_op jit(solution)/shard_map/ppermute | solution.py:86
  218.4 9.8 %collective-permute-start.36 = (bf16[256,256]{1,0:T(8,128)(2,1)S(1)}, bf16[256,256]{1,0:T(8,128)(2,1)S(1)}, u32[]{:S(2)}, u32[]{:S(2)}) collective-permute-start(bf16[256,256]{1,0:T(8,128)(2,1)S(1)} %get-tuple-element.70), channel_id=1, source_target_pairs={{64,0},{80,16},{96,32},{112,48},{65,1},{81,17},{97,33},{113,49},{6... | collective-permute-start | bytes 393224 | tf_op jit(solution)/shard_map/ppermute | solution.py:86
  399.2 20.1 %collective-permute-start.48 = (f32[4096]{0:T(1024)S(1)}, f32[4096]{0:T(1024)S(1)}, u32[]{:S(2)}, u32[]{:S(2)}) collective-permute-start(f32[4096]{0:T(1024)S(1)} %bitcast.537), channel_id=1, source_target_pairs={{0,48},{16,0},{32,16},{48,32},{1,49},{17,1},{33,17},{49,33},{2,50}... | collective-permute-start | bytes 49160 | tf_op jit(solution)/shard_map/ppermute | solution.py:28
  402.2 17.1 %collective-permute-start.47 = (f32[4096]{0:T(1024)S(1)}, f32[4096]{0:T(1024)S(1)}, u32[]{:S(2)}, u32[]{:S(2)}) collective-permute-start(f32[4096]{0:T(1024)S(1)} %bitcast.538), channel_id=1, source_target_pairs={{0,32},{16,48},{32,0},{48,16},{1,33},{17,49},{33,1},{49,17},{2,34}... | collective-permute-start | bytes 49160 | tf_op jit(solution)/shard_map/ppermute | solution.py:28
  402.9 16.4 %collective-permute-start.46 = (f32[4096]{0:T(1024)S(1)}, f32[4096]{0:T(1024)S(1)}, u32[]{:S(2)}, u32[]{:S(2)}) collective-permute-start(f32[4096]{0:T(1024)S(1)} %bitcast.539), channel_id=1, source_target_pairs={{0,16},{16,32},{32,48},{48,0},{1,17},{17,33},{33,49},{49,1},{2,18}... | collective-permute-start | bytes 49160 | tf_op jit(solution)/shard_map/ppermute | solution.py:28
  (171 other events, 1032.3 us)
Sparse Core Ops, SparseCore 0:
  262.7 135.6 all-reduce.2
